TPU v7x, 32 devices: a whole 2x2x4 slice. The times are simulated.
32 devices in a mesh: depth: 4 (over y, x), res: 8 (over z, core).
Axes of the slice: x: 2, y: 2, z: 4, core: 2. Of those that a mesh axis runs over, the one named last changes fastest.
Arguments:
- alignment_left: bfloat16 [1024, 8192], P('depth', 'res'), may hold values from -6 to 6
- alignment_right: bfloat16 [1024, 8192], P('depth', 'res'), may hold values from -6 to 6
- window_starts: int32 [4], replicated, may hold values from 0 to 248
- outer_product_weight: bfloat16 [1024, 128], replicated, may hold values from -6 to 6
- outer_product_bias: float32 [128], replicated, may hold values from -3 to 3
- query_key_value_gate_weight: bfloat16 [128, 512], replicated, may hold values from -0.5 to 0.5
- output_weight: bfloat16 [128, 128], replicated, may hold values from -2 to 2
- triangle_pair_bias: bfloat16 [4, 256, 256], P(None, 'res'), may hold values from -3 to 260
- residue_chain: int32 [256], replicated, may hold values from 0 to 7, never falling along the last dimension, each value on 1 to 64 neighbouring positions
- interchain_offset: float32 [4], replicated, may hold values from -3 to -0.5
Outputs:
- pair_strip: bfloat16 [32, 256, 128], P('depth', 'res')
- update: bfloat16 [32, 256, 128], P('depth', 'res')
All inputs are finite; a program needn't handle non-finite values.
Results may differ from a plain program's by a relative error of at most 0.014.
Values may be sent and summed in bfloat16 or wider, within the bound.
No kernel may reach another device: no remote copies, remote signals or barrier semaphores. Data moves between devices by JAX's collectives and lax.ppermute only.
A program may use at most 128 MiB of HBM per device.

v0:
```python
import jax
import jax.numpy as jnp
from jax import lax
from jax.sharding import PartitionSpec as P

PROJ_CHANNELS = 32
CZ = 128
H = 4
DH = 32
R_DEV = 8


epsilon = 1e-05


def layer_norm(values):
    average = jnp.mean(values, axis=-1, keepdims=True)
    centred = values - average
    variance = jnp.mean(centred * centred, axis=-1, keepdims=True)
    return centred * lax.rsqrt(variance + epsilon)


def split_project(flat_outer, weight):
    upper = lax.optimization_barrier(flat_outer.astype(jnp.bfloat16))
    lower = (flat_outer - upper.astype(jnp.float32)).astype(jnp.bfloat16)
    return jnp.dot(upper, weight, preferred_element_type=jnp.float32) + jnp.dot(
        lower, weight, preferred_element_type=jnp.float32
    )


def body(
    alignment_left,
    alignment_right,
    window_starts,
    outer_product_weight,
    outer_product_bias,
    query_key_value_gate_weight,
    output_weight,
    triangle_pair_bias,
    residue_chain,
    interchain_offset,
):
    depth_count = lax.axis_size("depth")
    res_index = lax.axis_index("res")
    sequence_shards = alignment_left.shape[0]
    token_shards = alignment_left.shape[1] // PROJ_CHANNELS
    groups = window_starts.shape[0]
    gathered_rows = groups * R_DEV
    total_seqs = sequence_shards * depth_count
    shard_left = alignment_left.reshape(sequence_shards, token_shards, PROJ_CHANNELS)
    shard_right = alignment_right.reshape(sequence_shards, token_shards, PROJ_CHANNELS)
    row_ids = (window_starts[:, None] + jnp.arange(R_DEV, dtype=jnp.int32)[None, :]).reshape(
        gathered_rows
    )
    first_token = res_index * token_shards
    selector = (
        row_ids[:, None] == first_token + jnp.arange(token_shards, dtype=jnp.int32)[None, :]
    ).astype(jnp.bfloat16)
    shard_rows = jnp.einsum(
        "it,stc->sic", selector, shard_left, preferred_element_type=jnp.float32
    ).astype(jnp.bfloat16)
    alignment_band = lax.psum(
        shard_rows.reshape(sequence_shards, gathered_rows * PROJ_CHANNELS), "res"
    ).astype(jnp.float32)
    alignment_band = alignment_band.astype(jnp.bfloat16).reshape(
        sequence_shards, gathered_rows, PROJ_CHANNELS
    )
    outer_prod = jnp.einsum(
        "hbv,hqz->bqvz", alignment_band, shard_right, preferred_element_type=jnp.float32
    )
    flat_block = outer_prod.reshape(
        R_DEV * lax.axis_size("depth"), token_shards * PROJ_CHANNELS * PROJ_CHANNELS
    ).reshape(R_DEV * lax.axis_size("depth") * token_shards, PROJ_CHANNELS * PROJ_CHANNELS)
    block_out = split_project(flat_block, outer_product_weight)
    projected = lax.psum_scatter(
        block_out.reshape(R_DEV * lax.axis_size("depth"), token_shards * CZ).astype(jnp.bfloat16),
        "depth",
        scatter_dimension=0,
        tiled=True,
    ).astype(jnp.float32)
    pair_strip = (
        projected.reshape(R_DEV * token_shards, CZ) / total_seqs + outer_product_bias[None, :]
    ).astype(jnp.bfloat16)
    pair_strip = pair_strip.reshape(R_DEV, token_shards, CZ)
    normed = layer_norm(pair_strip.astype(jnp.float32)).astype(jnp.bfloat16)
    flat_normed = normed.reshape(R_DEV * token_shards, CZ)
    query_weight = jnp.concatenate(
        [query_key_value_gate_weight[:, :CZ], query_key_value_gate_weight[:, 3 * CZ :]], axis=1
    )
    query_gate = jnp.dot(flat_normed, query_weight, preferred_element_type=jnp.float32).astype(
        jnp.bfloat16
    )
    queries = query_gate[:, :CZ]
    gate_pre = query_gate[:, CZ:]
    queries = queries.reshape(R_DEV, token_shards, H, DH)
    own_chain = lax.dynamic_slice_in_dim(residue_chain, first_token, token_shards, 0)
    score_scale = DH ** (-0.5)
    normed_piece = lax.all_gather(normed, "res", axis=1, tiled=True)
    key_count = normed_piece.shape[1]
    kv_block = jnp.dot(
        normed_piece.reshape(R_DEV * key_count, CZ),
        query_key_value_gate_weight[:, CZ : 3 * CZ],
        preferred_element_type=jnp.float32,
    ).astype(jnp.bfloat16)
    pair_kv = kv_block.reshape(R_DEV, key_count, 2 * CZ)
    run_max = jnp.full((R_DEV, H, token_shards), -jnp.inf, jnp.float32)
    run_sum = jnp.zeros((R_DEV, H, token_shards), jnp.float32)
    run_acc = jnp.zeros((R_DEV, token_shards, CZ), jnp.float32)
    absorb_key_count = pair_kv.shape[1]
    key_heads = pair_kv[:, :, :CZ].reshape(R_DEV, absorb_key_count, H, DH)
    value_heads = pair_kv[:, :, CZ:].reshape(R_DEV, absorb_key_count, H, DH)
    scores = (
        jnp.einsum("rqhd,rkhd->rhqk", queries, key_heads, preferred_element_type=jnp.float32)
        * score_scale
    )
    bias_block = triangle_pair_bias.astype(jnp.float32)
    differ = (own_chain[:, None] != residue_chain[None, :]).astype(jnp.float32)
    scores = scores + (bias_block + interchain_offset[:, None, None] * differ[None, :, :])[None]
    new_max = jnp.max(scores, axis=-1)
    shrink = jnp.exp(run_max - new_max)
    weights = jnp.exp(scores - new_max[..., None])
    new_sum = run_sum * shrink + jnp.sum(weights, axis=-1)
    increment = jnp.einsum(
        "rhqk,rkhd->rqhd",
        weights.astype(jnp.bfloat16),
        value_heads,
        preferred_element_type=jnp.float32,
    ).reshape(R_DEV, token_shards, CZ)
    factor = jnp.repeat(jnp.transpose(shrink, (0, 2, 1)), DH, axis=2)
    run_max, run_sum, run_acc = (new_max, new_sum, run_acc * factor + increment)
    factor_total = jnp.repeat(jnp.transpose(run_sum, (0, 2, 1)), DH, axis=2)
    attended = run_acc / factor_total
    gated_out = (
        jax.nn.sigmoid(gate_pre.astype(jnp.float32)).reshape(R_DEV, token_shards, CZ) * attended
    ).astype(jnp.bfloat16)
    update = jnp.dot(
        gated_out.reshape(R_DEV * token_shards, CZ),
        output_weight,
        preferred_element_type=jnp.float32,
    )
    update = update.astype(jnp.bfloat16).reshape(R_DEV, token_shards, CZ)
    return (pair_strip, update)


def solution(mesh):
    in_specs = (
        P("depth", "res"),
        P("depth", "res"),
        P(),
        P(),
        P(),
        P(),
        P(),
        P(None, "res", None),
        P(),
        P(),
    )
    out_specs = (P("depth", "res", None), P("depth", "res", None))
    return jax.shard_map(body, mesh=mesh, in_specs=in_specs, out_specs=out_specs, check_vma=False)
```

profile of v0, /device:TPU:0, one launch (start us, length us, event | category | flops | bytes accessed | tf_op | source)
XLA Modules:
  0.0 166.3 jit_solution(6662840116127178980)
XLA Ops:
  7.3 1.3 copy.23
  8.6 0.7 iota_add_fusion
  9.4 1.2 fusion.3
  11.0 59.0 %all-reduce.4.cloned.1.call-done = bf16[256,32,32]{0,1,2:T(8,128)(2,1)} async-done(((bf16[256,32,32]{0,1,2:T(8,128)(2,1)}), bf16[256,32,32]{0,1,2:T(8,128)(2,1)}) %all-reduce.4.cloned.1.call-update) | async-done | bytes 524304 | tf_op jit(solution)/shard_map/psum | solution.py:62
  70.1 8.1 %convolution_bitcast_fusion = f32[32,32,32,32]{3,2,1,0:T(8,128)} fusion(bf16[256,32,32,1]{0,2,1,3:T(8,128)(2,1)S(1)} %bitcast.41, bf16[256,32,32,1]{0,1,2,3:T(8,128)(2,1)} %bitcast.45), kind=kOutput, calls=%fused_computation | convolution fusion | flops 536870912 | bytes 5242880 | tf_op jit(solution)/shard_map/hbv,hqz->bqvz/dot_general | solution.py:68
  78.2 13.7 %reshape_reshape.3 = f32[1024,1024]{1,0:T(8,128)} reshape(f32[32,32,32,32]{3,2,1,0:T(8,128)} %convolution_bitcast_fusion) | data formatting | bytes 8388608 | tf_op jit(solution)/shard_map/reshape;reshape | solution.py:73
  91.8 2.7 %convert_element_type.77 = bf16[1024,1024]{1,0:T(8,128)(2,1)S(1)} convert(f32[1024,1024]{1,0:T(8,128)} %reshape_reshape.3) | non-fusion elementwise | flops 1048576 | bytes 6291456 | tf_op jit(solution)/shard_map/convert_element_type | solution.py:24
  94.5 0.7 fusion.38
  95.3 0.7 fusion.6
  96.0 0.8 convert_element_type.81
  96.9 0.6 dynamic-slice
  98.3 40.8 %all-reduce.6.cloned.1.call-done = bf16[32,4096]{1,0:T(8,128)(2,1)} async-done(((bf16[32,4096]{1,0:T(8,128)(2,1)}), bf16[32,4096]{1,0:T(8,128)(2,1)}) %all-reduce.6.cloned.1.call-update) | async-done | bytes 262160
  139.1 0.9 convert_multiply_fusion
  140.6 14.7 %all_gather.3 = bf16[8,256,128]{2,1,0:T(8,128)(2,1)S(1)} all-gather(bf16[8,32,128]{2,1,0:T(8,128)(2,1)S(1)} %fusion.17), channel_id=1, replica_groups=mesh['depth'=4,'res'=8] {'res'}, dimensions={1}, use_global_device_ids=true | all-gather | bytes 589824 | tf_op jit(solution)/shard_map/all_gather | solution.py:98
  155.3 0.4 convolution_convert_fusion
  155.7 0.3 fusion.35
  156.0 0.2 copy.28
  156.3 0.3 convolution_convert_fusion.2
  156.7 0.4 fusion.37
  157.1 0.4 fusion.7
  157.7 0.4 fusion.5
  158.1 0.2 copy.31
  158.4 0.3 div.37
  158.6 0.8 convolution_convert_fusion.3
  (45 shorter events, 1.8 us)
Async XLA Ops:
  7.2 87.3 %copy-start = (bf16[1024,128]{1,0:T(8,128)(2,1)S(1)}, bf16[1024,128]{1,0:T(8,128)(2,1)}, u32[]{:S(2)}) copy-start(bf16[1024,128]{1,0:T(8,128)(2,1)} %param.13) | copy-start | bytes 786436
  7.2 3.5 %copy-start.3 = (bf16[256,1024]{1,0:T(8,128)(2,1)S(1)}, bf16[256,1024]{1,0:T(8,128)(2,1)}, u32[]{:S(2)}) copy-start(bf16[256,1024]{1,0:T(8,128)(2,1)} %param.11) | copy-start | bytes 1572868
  7.2 3.7 %copy-start.7 = (s32[256]{0:T(256)S(1)}, s32[256]{0:T(256)}, u32[]{:S(2)}) copy-start(s32[256]{0:T(256)} %param.18) | copy-start | bytes 3076
  7.2 3.8 %copy-start.4 = (bf16[128,512]{1,0:T(8,128)(2,1)S(1)}, bf16[128,512]{1,0:T(8,128)(2,1)}, u32[]{:S(2)}) copy-start(bf16[128,512]{1,0:T(8,128)(2,1)} %param.15) | copy-start | bytes 393220
  7.2 62.8 %all-reduce.4.cloned.1.call-start = ((), (), s32[]{:S(2)}) async-start(), calls=%async_computation | async-start | bytes 1048576 | tf_op jit(solution)/shard_map/psum | solution.py:62
  10.6 128.5 %all-reduce.6.cloned.1.call-start = ((), (), s32[]{:S(2)}) async-start(), calls=%async_computation.1 | async-start | bytes 524288
  91.8 3.4 %copy-start.1 = (f32[1024,1024]{1,0:T(8,128)S(1)}, f32[1024,1024]{1,0:T(8,128)}, u32[]{:S(2)}) copy-start(f32[1024,1024]{1,0:T(8,128)} %reshape_reshape.3) | copy-start | bytes 12582916
  95.3 1.7 copy-start.10
  95.3 2.9 %copy-start.5 = (bf16[4,32,256]{2,1,0:T(8,128)(2,1)S(1)}, bf16[4,32,256]{2,1,0:T(8,128)(2,1)}, u32[]{:S(2)}) copy-start(bf16[4,32,256]{2,1,0:T(8,128)(2,1)} %param.17) | copy-start | bytes 196612
  95.3 2.9 %copy-start.8 = (f32[4]{0:T(128)S(1)}, f32[4]{0:T(128)}, u32[]{:S(2)}) copy-start(f32[4]{0:T(128)} %param.19) | copy-start | bytes 52
  95.3 44.7 %copy-start.6 = (f32[128]{0:T(128)S(1)}, f32[128]{0:T(128)}, u32[]{:S(2)}) copy-start(f32[128]{0:T(128)} %param.14) | copy-start | bytes 1540
  140.1 15.9 %copy-start.2 = (bf16[8,32,128]{2,1,0:T(8,128)(2,1)}, bf16[8,32,128]{2,1,0:T(8,128)(2,1)S(1)}, u32[]{:S(2)}) copy-start(bf16[8,32,128]{2,1,0:T(8,128)(2,1)S(1)} %get-tuple-element.3) | copy-start | bytes 196612
  157.7 0.9 copy-start.9
Sparse Core Ops, SparseCore 0:
  10.8 59.2 all-reduce.3
  97.0 42.0 all-reduce.5
where the time goes:
time: 167 us; the launch traced here: 166 us
  waiting for transfers between devices  99.9 us (60%)
  local copies, waits for them, and re-layouts  18.4 us (11%)
  between operations  15 us (9%)
  blocking collectives  14.7 us (9%)
  matrix products  13 us (8%)
  other arithmetic  5.27 us (3%)
    psum x1, waiting for transfers between devices, body(): lax.psum(shard_rows.reshape(sequence_shards, gathered_rows * PROJ_CHANNEL...  59 us
    unnamed x3, waiting for transfers between devices  40.9 us
    all_gather x1, blocking collectives, body(): normed_piece = lax.all_gather(normed, 'res', axis=1, tiled=True)  14.7 us
    another operation x1, local copies, waits for them, and re-layouts, body(): flat_block = outer_prod.reshape(R_DEV * lax.axis_size('depth'), token_sha...  13.7 us
    dot_general x1, matrix products, body(): jnp.einsum('hbv,hqz->bqvz', alignment_band, shard_right, preferred_elemen...  8.12 us
  transfers between devices with their start and end apart: 2, of which 2 were waited for; matrix products, arithmetic and copies ran while one was open for 1% of the time, Pallas kernels for 0%

commit v1 on v0

v1 whole, which is shorter than its diff:
```python
import functools

import jax
import jax.numpy as jnp
from jax import lax
from jax.experimental import pallas as pl
from jax.experimental.pallas import tpu as pltpu
from jax.sharding import PartitionSpec as P

PROJ_CHANNELS = 32
CZ = 128
H = 4
DH = 32
R_DEV = 8
LANES = 128
PACK = LANES // PROJ_CHANNELS
WINDOW = R_DEV * PROJ_CHANNELS
SPAN = WINDOW + LANES

epsilon = 1e-05
VMEM = pl.BlockSpec(memory_space=pltpu.VMEM)
SMEM = pl.BlockSpec(memory_space=pltpu.SMEM)
BF = jnp.bfloat16
F32 = jnp.float32


def call(kernel, outs, specs, scratch=(), flops=0, name=None):
    return pl.pallas_call(
        kernel,
        out_shape=outs,
        in_specs=specs,
        out_specs=jax.tree.map(lambda _: VMEM, outs),
        scratch_shapes=list(scratch),
        name=name,
        cost_estimate=pl.CostEstimate(
            flops=flops, bytes_accessed=1 << 20, transcendentals=0
        ),
    )


def prep_kernel(idx, off, w_ref, tri_ref, chain_ref, wbd_ref, bias_ref):
    wbd_ref[...] = jnp.zeros_like(wbd_ref)
    for c in range(PROJ_CHANNELS):
        block = w_ref[c * PROJ_CHANNELS : (c + 1) * PROJ_CHANNELS, :]
        for j in range(PACK):
            row = c * LANES + j * PROJ_CHANNELS
            wbd_ref[row : row + PROJ_CHANNELS, j * CZ : (j + 1) * CZ] = block
    tokens, keys = tri_ref.shape[1:]
    first = idx[1] * tokens
    chain = jnp.broadcast_to(chain_ref[...], (tokens, keys))
    rows = lax.broadcasted_iota(jnp.int32, (tokens, keys), 0)
    cols = lax.broadcasted_iota(jnp.int32, (tokens, keys), 1)
    own = jnp.sum(jnp.where(cols == rows + first, chain, 0), axis=1, keepdims=True)
    differ = (chain != own).astype(F32)
    for h in range(H):
        bias_ref[h * tokens : (h + 1) * tokens, :] = (
            tri_ref[h].astype(F32) + off[h] * differ
        )


def select_kernel(idx, starts, own_ref, recv_ref, out_ref, chip_ref):
    chips, size, half = out_ref.shape
    width = own_ref.shape[1]
    res = idx[1]
    core = res % 2
    z = res // 2
    own_at = pl.multiple_of(core * width, LANES)
    recv_at = pl.multiple_of((1 - core) * width, LANES)
    seq_at = pl.multiple_of(core * half, half)
    chip_ref[:, pl.ds(own_at, width)] = own_ref[pl.ds(seq_at, half), :]
    chip_ref[:, pl.ds(recv_at, width)] = recv_ref[...]
    m = lax.broadcasted_iota(jnp.int32, (size, SPAN), 0)
    lane = lax.broadcasted_iota(jnp.int32, (size, SPAN), 1)
    delta = lane - (m % R_DEV) * PROJ_CHANNELS - m // R_DEV
    for k in range(chips):
        g = jnp.bitwise_xor(z, k)
        split = WINDOW // size
        first = g % split * (size // R_DEV)
        start = starts[g // split] * PROJ_CHANNELS - z * (2 * width)
        base = jnp.clip(start, 0, 2 * width - SPAN) // LANES * LANES
        base = pl.multiple_of(base, LANES)
        pick = (delta == start + first - base).astype(F32).astype(BF)
        out_ref[k] = lax.dot_general(
            pick,
            chip_ref[:, pl.ds(base, SPAN)],
            (((1,), (1,)), ((), ())),
            preferred_element_type=F32,
        ).astype(BF)


def outer_kernel(chips, idx, *refs):
    mine = refs[:chips]
    theirs, b_ref, wbd_ref, out_ref, at_ref, lhs_ref, acc_ref = refs[chips:]
    size, half = mine[0].shape
    groups = out_ref.shape[0]
    z = idx[1] // 2
    core = idx[1] % 2
    mine_at = pl.multiple_of(core * half, LANES)
    theirs_at = pl.multiple_of((1 - core) * half, LANES)
    for k in range(chips):
        row = pl.multiple_of(jnp.bitwise_xor(z, k) * size, size)
        at_ref[pl.ds(row, size), pl.ds(mine_at, half)] = mine[k][...]
        at_ref[pl.ds(row, size), pl.ds(theirs_at, half)] = theirs[k]
    width = b_ref.shape[1]
    rows = groups * R_DEV
    for n in range(width // (2 * LANES)):
        part = jnp.dot(
            at_ref[...],
            b_ref[:, n * 2 * LANES : (n + 1) * 2 * LANES],
            preferred_element_type=F32,
        ).reshape(groups, PROJ_CHANNELS, R_DEV, 2 * LANES)
        for c in range(PROJ_CHANNELS):
            for q in range(2):
                slab = part[:, c, :, q * LANES : (q + 1) * LANES].reshape(rows, LANES)
                lhs_ref[
                    (2 * n + q) * rows : (2 * n + q + 1) * rows,
                    c * LANES : (c + 1) * LANES,
                ] = slab.astype(BF)
    acc = jnp.dot(lhs_ref[...], wbd_ref[...], preferred_element_type=F32)
    chunks = width // LANES
    acc_ref[...] = acc.reshape(chunks, groups, R_DEV, PACK * CZ)
    for k in range(groups):
        g = jnp.bitwise_xor(idx[0], k)
        block = acc_ref[:, g]
        block = jnp.stack(
            [block[:, :, j * CZ : (j + 1) * CZ] for j in range(PACK)], axis=1
        )
        out_ref[k] = block.reshape(chunks * PACK * R_DEV, CZ).astype(BF)


def norm_kernel(scale, *refs):
    parts = refs[:-4]
    bias_ref, pair_ref, normed_ref, sum_ref = refs[-4:]
    total = parts[0][...].astype(F32)
    for p in parts[1:]:
        total = total + p[...].astype(F32)
    sum_ref[...] = total * scale + bias_ref[...]
    tokens = pair_ref.shape[1]
    for u in range(R_DEV):
        pair = sum_ref[pl.ds(u, tokens, stride=R_DEV), :].astype(BF)
        pair_ref[u] = pair
        values = pair.astype(F32)
        centred = values - jnp.mean(values, axis=-1, keepdims=True)
        variance = jnp.mean(centred * centred, axis=-1, keepdims=True)
        normed_ref[u] = (centred * lax.rsqrt(variance + epsilon)).astype(BF)


def query_kernel(normed_ref, w_ref, q_ref, gate_ref):
    rows = R_DEV * normed_ref.shape[1]
    x = normed_ref[...].reshape(rows, CZ)
    q_ref[...] = jnp.dot(x, w_ref[:, :CZ], preferred_element_type=F32).astype(BF)
    g = jnp.dot(x, w_ref[:, 3 * CZ :], preferred_element_type=F32).astype(BF)
    gate_ref[...] = jax.nn.sigmoid(g.astype(F32))


def attend_kernel(chips, idx, *refs):
    mine = refs[:chips]
    theirs, q_ref, gate_ref, w_ref, wo_ref, bias_ref, out_ref, all_ref, gated_ref = refs[chips:]
    tokens = mine[0].shape[1]
    z = idx[1] // 2
    core = idx[1] % 2
    for k in range(chips):
        chip = jnp.bitwise_xor(z, k) * 2
        mine_at = pl.multiple_of((chip + core) * tokens, tokens)
        theirs_at = pl.multiple_of((chip + 1 - core) * tokens, tokens)
        all_ref[:, pl.ds(mine_at, tokens), :] = mine[k][...]
        all_ref[:, pl.ds(theirs_at, tokens), :] = theirs[k]
    scale = DH ** (-0.5)
    lane_head = lax.broadcasted_iota(jnp.int32, (tokens, CZ), 1) // DH
    for u in range(R_DEV):
        kv = jnp.dot(
            all_ref[u], w_ref[:, CZ : 3 * CZ], preferred_element_type=F32
        ).astype(BF)
        q = q_ref[u * tokens : (u + 1) * tokens, :]
        spread = jnp.concatenate(
            [jnp.where(lane_head == h, q, jnp.zeros_like(q)) for h in range(H)], axis=0
        )
        scores = lax.dot_general(
            spread, kv[:, :CZ], (((1,), (1,)), ((), ())), preferred_element_type=F32
        )
        scores = scores * scale + bias_ref[...]
        weights = jnp.exp(scores - jnp.max(scores, axis=-1, keepdims=True))
        denom = jnp.sum(weights, axis=-1, keepdims=True)
        value = jnp.dot(weights.astype(BF), kv[:, CZ:], preferred_element_type=F32)
        value = value / denom
        attended = jnp.zeros((tokens, CZ), F32)
        for h in range(H):
            attended = jnp.where(
                lane_head == h, value[h * tokens : (h + 1) * tokens, :], attended
            )
        gated_ref[u * tokens : (u + 1) * tokens, :] = (
            gate_ref[u * tokens : (u + 1) * tokens, :] * attended
        ).astype(BF)
    out = jnp.dot(gated_ref[...], wo_ref[...], preferred_element_type=F32)
    out_ref[...] = out.astype(BF).reshape(R_DEV, tokens, CZ)


def swap(x, axis, mask):
    n = lax.axis_size(axis)
    return lax.ppermute(x, axis, [(i, i ^ mask) for i in range(n)])


def body(
    alignment_left,
    alignment_right,
    window_starts,
    outer_product_weight,
    outer_product_bias,
    query_key_value_gate_weight,
    output_weight,
    triangle_pair_bias,
    residue_chain,
    interchain_offset,
):
    depth_count = lax.axis_size("depth")
    res_count = lax.axis_size("res")
    groups = window_starts.shape[0]
    chips = res_count // 2
    size = groups * WINDOW // chips
    assert groups == depth_count and WINDOW % size == 0
    seqs, width = alignment_left.shape
    half = seqs // 2
    tokens = width // PROJ_CHANNELS
    keys = residue_chain.shape[0]
    rows = groups * R_DEV
    res = lax.axis_index("res")
    idx = jnp.stack([lax.axis_index("depth"), res]).astype(jnp.int32)

    core = res % 2
    sent = lax.dynamic_slice_in_dim(alignment_left, (1 - core) * half, half, 0)
    recv = swap(sent, "res", 1)

    wbd, bias = call(
        prep_kernel,
        (
            jax.ShapeDtypeStruct((PROJ_CHANNELS * LANES, PACK * CZ), BF),
            jax.ShapeDtypeStruct((H * tokens, keys), F32),
        ),
        [SMEM, SMEM, VMEM, VMEM, VMEM],
        flops=1 << 28,
        name="prep",
    )(idx, interchain_offset, outer_product_weight, triangle_pair_bias, residue_chain[None, :])

    picked = call(
        select_kernel,
        jax.ShapeDtypeStruct((chips, size, half), BF),
        [SMEM, SMEM, VMEM, VMEM],
        [pltpu.VMEM((half, 2 * width), BF)],
        flops=1 << 28,
        name="select",
    )(idx, window_starts, alignment_left, recv)
    piece = picked[0]
    for k in range(1, chips):
        piece = piece + swap(picked[k], "res", 2 * k)
    mine = [piece] + [swap(piece, "res", 2 * k) for k in range(1, chips)]
    theirs = swap(jnp.stack(mine), "res", 1)

    partial = call(
        functools.partial(outer_kernel, chips),
        jax.ShapeDtypeStruct((groups, R_DEV * tokens, CZ), BF),
        [SMEM] + [VMEM] * (chips + 3),
        [
            pltpu.VMEM((groups * WINDOW, seqs), BF),
            pltpu.VMEM((rows * width // LANES, PROJ_CHANNELS * LANES), BF),
            pltpu.VMEM((width // LANES, groups, R_DEV, PACK * CZ), F32),
        ],
        flops=1 << 31,
        name="outer",
    )(idx, *mine, theirs, alignment_right, wbd)
    parts = [partial[0]] + [swap(partial[k], "depth", k) for k in range(1, groups)]

    pair_strip, normed = call(
        functools.partial(norm_kernel, 1.0 / (seqs * depth_count)),
        (
            jax.ShapeDtypeStruct((R_DEV, tokens, CZ), BF),
            jax.ShapeDtypeStruct((R_DEV, tokens, CZ), BF),
        ),
        [VMEM] * (groups + 1),
        [pltpu.VMEM((R_DEV * tokens, CZ), F32)],
        flops=1 << 24,
        name="norm",
    )(*parts, outer_product_bias[None, :])

    near = [normed] + [swap(normed, "res", 2 * k) for k in range(1, chips)]
    far = swap(jnp.stack(near), "res", 1)
    queries, gate = call(
        query_kernel,
        (
            jax.ShapeDtypeStruct((R_DEV * tokens, CZ), BF),
            jax.ShapeDtypeStruct((R_DEV * tokens, CZ), F32),
        ),
        [VMEM] * 2,
        flops=1 << 27,
        name="query",
    )(normed, query_key_value_gate_weight)
    update = call(
        functools.partial(attend_kernel, chips),
        jax.ShapeDtypeStruct((R_DEV, tokens, CZ), BF),
        [SMEM] + [VMEM] * (chips + 6),
        [
            pltpu.VMEM((R_DEV, keys, CZ), BF),
            pltpu.VMEM((R_DEV * tokens, CZ), BF),
        ],
        flops=1 << 29,
        name="attend",
    )(idx, *near, far, queries, gate, query_key_value_gate_weight, output_weight, bias)
    return (pair_strip, update)


def solution(mesh):
    in_specs = (
        P("depth", "res"),
        P("depth", "res"),
        P(),
        P(),
        P(),
        P(),
        P(),
        P(None, "res", None),
        P(),
        P(),
    )
    out_specs = (P("depth", "res", None), P("depth", "res", None))
    return jax.shard_map(body, mesh=mesh, in_specs=in_specs, out_specs=out_specs, check_vma=False)
```

time: 167 us -> 66.5 us (0.40)
  waiting for transfers between devices: 99.9 us -> 19 us
  Pallas kernels: 0 us -> 18.9 us
  starting transfers between devices: 0.08 us -> 18.6 us
  blocking collectives: 14.7 us -> 0 us
  between operations: 15 us -> 0.76 us
  matrix products: 13 us -> 0 us
  local copies, waits for them, and re-layouts: 18.4 us -> 6.17 us
  other arithmetic: 5.27 us -> 2.47 us
    psum x1 -> x0, waiting for transfers between devices: 59 us -> none  [body(): lax.psum(shard_rows.reshape(sequence_shards, gathered_rows * PROJ_CHANNEL...]
    unnamed x3 -> x0, waiting for transfers between devices: 40.9 us -> none
    ppermute x0 -> x15, waiting for transfers between devices: none -> 19 us  [swap(): return lax.ppermute(x, axis, [(i, i ^ mask) for i in range(n)])]
    pallas_call x0 -> x6, Pallas kernels: none -> 18.9 us  [the longest x1 5.19 us: body(): call(functools.partial(outer_kernel, chips), jax.ShapeDtypeStruct((groups...]
    ppermute x0 -> x15, starting transfers between devices: none -> 18.6 us  [swap(): return lax.ppermute(x, axis, [(i, i ^ mask) for i in range(n)])]
    all_gather x1 -> x0, blocking collectives: 14.7 us -> none  [body(): normed_piece = lax.all_gather(normed, 'res', axis=1, tiled=True)]
    another operation x1 -> x0, local copies, waits for them, and re-layouts: 13.7 us -> none  [body(): flat_block = outer_prod.reshape(R_DEV * lax.axis_size('depth'), token_sha...]
    dot_general x9 -> x0, matrix products: 13 us -> none  [the longest x1 8.12 us: body(): jnp.einsum('hbv,hqz->bqvz', alignment_band, shard_right, preferred_elemen...]
  transfers between devices with their start and end apart: 2 -> 15, of which waited for: 2 -> 10; matrix products, arithmetic and copies ran while one was open for 1% -> 1% of each run, Pallas kernels for 0% -> 8%
where the time goes in v1:
time: 66.5 us; the launch traced here: 65.9 us
  waiting for transfers between devices  19 us (29%)
  Pallas kernels  18.9 us (28%)
  starting transfers between devices  18.6 us (28%)
  local copies, waits for them, and re-layouts  6.17 us (9%)
  other arithmetic  2.47 us (4%)
  between operations  0.76 us (1%)
    ppermute x15, waiting for transfers between devices, swap(): return lax.ppermute(x, axis, [(i, i ^ mask) for i in range(n)])  19 us
    ppermute x15, starting transfers between devices, swap(): return lax.ppermute(x, axis, [(i, i ^ mask) for i in range(n)])  18.6 us
    pallas_call x1, Pallas kernels, body(): call(functools.partial(outer_kernel, chips), jax.ShapeDtypeStruct((groups...  5.19 us
    pallas_call x1, Pallas kernels, body(): call(functools.partial(attend_kernel, chips), jax.ShapeDtypeStruct((R_DEV...  4.41 us
    pallas_call x1, Pallas kernels, body(): call(prep_kernel, (jax.ShapeDtypeStruct((PROJ_CHANNELS * LANES, PACK * CZ...  3.45 us
    unnamed x26, local copies, waits for them, and re-layouts  2.7 us
    pallas_call x1, Pallas kernels, body(): call(select_kernel, jax.ShapeDtypeStruct((chips, size, half), BF), [SMEM,...  2.26 us
    pallas_call x1, Pallas kernels, body(): call(functools.partial(norm_kernel, 1.0 / (seqs * depth_count)), (jax.Sha...  1.82 us
  transfers between devices with their start and end apart: 15, of which 10 were waited for; matrix products, arithmetic and copies ran while one was open for 1% of the time, Pallas kernels for 8%

profile of v1, /device:TPU:0, one launch (start us, length us, event | category | flops | bytes accessed | tf_op | source)
XLA Modules:
  0.0 65.9 jit_solution(5901326448722716897)
XLA Ops:
  0.6 1.0 %constant_dynamic-slice_fusion = bf16[128,1024]{1,0:T(8,128)(2,1)S(1)} fusion(bf16[256,1024]{1,0:T(8,128)(2,1)} %own_ref.1, s32[]{:T(128)S(6)} %select_n.11), kind=kLoop, calls=%fused_computation.14 | loop fusion | bytes 524292 | tf_op jit(solution)/shard_map/dynamic_slice | solution.py:230
  4.0 2.3 %select.3 = bf16[4,256,128]{2,1,0:T(8,128)(2,1)} custom-call(s32[2]{0:T(128)} %pad_add_fusion.idx, s32[4]{0:T(128)} %starts.1, bf16[256,1024]{1,0:T(8,128)(2,1)} %own_ref.1, bf16[128,1024]{1,0:T(8,128)(2,1)} %copy-done), custom_call_target="tpu_custom_call" | custom-call | flops 268435456 | bytes 1048576 | tf_op jit(solution)/shard_map/select/pallas_call | solution.py:244
  7.2 3.0 %collective-permute-start.1 = (bf16[256,128]{1,0:T(8,128)(2,1)S(1)}, bf16[256,128]{1,0:T(8,128)(2,1)S(1)}, u32[]{:S(2)}, u32[]{:S(2)}) collective-permute-start(bf16[256,128]{1,0:T(8,128)(2,1)S(1)} %get-tuple-element.18), channel_id=1, source_target_pairs={{0,2},{1,3},{2,0},{3,1},{4,6},{5,7},{6,4},{7,5},{8,10},{9,11},{10,... | collective-permute-start | bytes 196616 | tf_op jit(solution)/shard_map/ppermute | solution.py:200
  10.2 2.5 %collective-permute-start.3 = (bf16[256,128]{1,0:T(8,128)(2,1)S(1)}, bf16[256,128]{1,0:T(8,128)(2,1)S(1)}, u32[]{:S(2)}, u32[]{:S(2)}) collective-permute-start(bf16[256,128]{1,0:T(8,128)(2,1)S(1)} %get-tuple-element.19), channel_id=1, source_target_pairs={{0,6},{1,7},{2,4},{3,5},{4,2},{5,3},{6,0},{7,1},{8,14},{9,15},{10,... | collective-permute-start | bytes 196616 | tf_op jit(solution)/shard_map/ppermute | solution.py:200
  12.8 4.1 %collective-permute-done.3 = bf16[256,128]{1,0:T(8,128)(2,1)S(1)} collective-permute-done((bf16[256,128]{1,0:T(8,128)(2,1)S(1)}, bf16[256,128]{1,0:T(8,128)(2,1)S(1)}, u32[]{:S(2)}, u32[]{:S(2)}) %collective-permute-start.3) | collective-permute-done | bytes 65568 | tf_op jit(solution)/shard_map/ppermute | solution.py:200
  16.9 2.4 %collective-permute-done.2 = bf16[256,128]{1,0:T(8,128)(2,1)S(1)} collective-permute-done((bf16[256,128]{1,0:T(8,128)(2,1)S(1)}, bf16[256,128]{1,0:T(8,128)(2,1)S(1)}, u32[]{:S(2)}, u32[]{:S(2)}) %collective-permute-start.2) | collective-permute-done | bytes 65568 | tf_op jit(solution)/shard_map/ppermute | solution.py:200
  20.1 2.7 %collective-permute-start.6 = (bf16[256,128]{1,0:T(8,128)(2,1)S(1)}, bf16[256,128]{1,0:T(8,128)(2,1)S(1)}, u32[]{:S(2)}, u32[]{:S(2)}) collective-permute-start(bf16[256,128]{1,0:T(8,128)(2,1)S(1)} %fusion.2.refs_0_), channel_id=1, source_target_pairs={{0,6},{1,7},{2,4},{3,5},{4,2},{5,3},{6,0},{7,1},{8,14},{9,15},{10,... | collective-permute-start | bytes 196616 | tf_op jit(solution)/shard_map/ppermute | solution.py:200
  22.8 1.8 %collective-permute-start.4 = (bf16[256,128]{1,0:T(8,128)(2,1)S(1)}, bf16[256,128]{1,0:T(8,128)(2,1)S(1)}, u32[]{:S(2)}, u32[]{:S(2)}) collective-permute-start(bf16[256,128]{1,0:T(8,128)(2,1)S(1)} %fusion.2.refs_0_), channel_id=1, source_target_pairs={{0,2},{1,3},{2,0},{3,1},{4,6},{5,7},{6,4},{7,5},{8,10},{9,11},{10,... | collective-permute-start | bytes 196616 | tf_op jit(solution)/shard_map/ppermute | solution.py:200
  24.6 2.4 %collective-permute-done.6.refs_3_ = bf16[256,128]{1,0:T(8,128)(2,1)S(1)} collective-permute-done((bf16[256,128]{1,0:T(8,128)(2,1)S(1)}, bf16[256,128]{1,0:T(8,128)(2,1)S(1)}, u32[]{:S(2)}, u32[]{:S(2)}) %collective-permute-start.6) | collective-permute-done | bytes 65568 | tf_op jit(solution)/shard_map/ppermute | solution.py:200
  27.0 1.9 %collective-permute-done.5.refs_2_ = bf16[256,128]{1,0:T(8,128)(2,1)S(1)} collective-permute-done((bf16[256,128]{1,0:T(8,128)(2,1)S(1)}, bf16[256,128]{1,0:T(8,128)(2,1)S(1)}, u32[]{:S(2)}, u32[]{:S(2)}) %collective-permute-start.5) | collective-permute-done | bytes 65568 | tf_op jit(solution)/shard_map/ppermute | solution.py:200
  29.0 3.4 %prep.1 = (bf16[4096,512]{1,0:T(8,128)(2,1)}, f32[128,256]{1,0:T(8,128)}) custom-call(s32[2]{0:T(128)} %pad_add_fusion.idx, f32[4]{0:T(128)} %off.1, bf16[1024,128]{1,0:T(8,128)(2,1)} %w_ref.2, bf16[4,32,256]{2,1,0:T(8,128)(2,1)} %tri_ref.1, s32[1,256]{1,0:T(1,128)} %bitcast.43), custom_call_target="tpu_custom_call" | custom-call | flops 268435456 | bytes 1048576 | tf_op jit(solution)/shard_map/prep/pallas_call | solution.py:233
  33.2 5.2 %outer.1 = bf16[4,256,128]{2,1,0:T(8,128)(2,1)} custom-call(s32[2]{0:T(128)} %pad_add_fusion.idx, bf16[256,128]{1,0:T(8,128)(2,1)} %copy-done.1, bf16[256,128]{1,0:T(8,128)(2,1)} %copy-done.10, bf16[256,128]{1,0:T(8,128)(2,1)} %copy-done.9, bf16[256,128]{1,0:T(8,128)(2,1)} %copy-done.7, bf16[4,256,128]{2,1,0:T(8,128)(2,1)} %copy-done.12, ...), custom_call_target="tpu_custom_call" | custom-call | flops 2147483648 | bytes 1048576 | tf_op jit(solution)/shard_map/outer/pallas_call | solution.py:258
  38.4 1.6 %slice_bitcast_fusion = (bf16[256,128]{1,0:T(8,128)(2,1)S(1)}, bf16[256,128]{1,0:T(8,128)(2,1)S(1)}, bf16[256,128]{1,0:T(8,128)(2,1)S(1)}, bf16[256,128]{1,0:T(8,128)(2,1)}) fusion(bf16[4,256,128]{2,1,0:T(8,128)(2,1)} %outer.1), kind=kLoop, calls=%fused_computation.2 | loop fusion | bytes 524288 | tf_op jit(solution)/shard_map/squeeze | solution.py:270
  39.9 2.5 %collective-permute-start.10 = (bf16[256,128]{1,0:T(8,128)(2,1)S(1)}, bf16[256,128]{1,0:T(8,128)(2,1)S(1)}, u32[]{:S(2)}, u32[]{:S(2)}) collective-permute-start(bf16[256,128]{1,0:T(8,128)(2,1)S(1)} %get-tuple-element.14), channel_id=1, source_target_pairs={{0,24},{8,16},{16,8},{24,0},{1,25},{9,17},{17,9},{25,1},{2,26},{10... | collective-permute-start | bytes 196616 | tf_op jit(solution)/shard_map/ppermute | solution.py:200
  43.4 1.9 %collective-permute-done.10.refs_3_ = bf16[256,128]{1,0:T(8,128)(2,1)S(1)} collective-permute-done((bf16[256,128]{1,0:T(8,128)(2,1)S(1)}, bf16[256,128]{1,0:T(8,128)(2,1)S(1)}, u32[]{:S(2)}, u32[]{:S(2)}) %collective-permute-start.10) | collective-permute-done | bytes 65568 | tf_op jit(solution)/shard_map/ppermute | solution.py:200
  45.4 1.4 %collective-permute-done.9.refs_2_ = bf16[256,128]{1,0:T(8,128)(2,1)S(1)} collective-permute-done((bf16[256,128]{1,0:T(8,128)(2,1)S(1)}, bf16[256,128]{1,0:T(8,128)(2,1)S(1)}, u32[]{:S(2)}, u32[]{:S(2)}) %collective-permute-start.9) | collective-permute-done | bytes 65568 | tf_op jit(solution)/shard_map/ppermute | solution.py:200
  47.8 1.8 %norm.1 = (bf16[8,32,128]{2,1,0:T(8,128)(2,1)}, bf16[8,32,128]{2,1,0:T(8,128)(2,1)}) custom-call(bf16[256,128]{1,0:T(8,128)(2,1)} %get-tuple-element.17.refs_0_, bf16[256,128]{1,0:T(8,128)(2,1)} %copy-done.4, bf16[256,128]{1,0:T(8,128)(2,1)} %copy-done.3, bf16[256,128]{1,0:T(8,128)(2,1)} %copy-done.2, f32[1,128]{1,0:T(1,128)} %bitcast.42), custom_call_target="tpu_custom_call" | custom-call | flops 16777216 | bytes 1048576 | tf_op jit(solution)/shard_map/norm/pallas_call | solution.py:272
  49.6 1.7 %collective-permute-start.13 = (bf16[8,32,128]{2,1,0:T(8,128)(2,1)}, bf16[8,32,128]{2,1,0:T(8,128)(2,1)S(1)}, u32[]{:S(2)}, u32[]{:S(2)}) collective-permute-start(bf16[8,32,128]{2,1,0:T(8,128)(2,1)} %get-tuple-element.10.normed_ref.refs_0_), channel_id=1, source_target_pairs={{0,6},{1,7},{2,4},{3,5},{4,2},{5,3},{6,0},{7,1},{8,14},{9,15},{10,... | collective-permute-start | bytes 196616 | tf_op jit(solution)/shard_map/ppermute | solution.py:200
  51.4 2.7 %collective-permute-start.11 = (bf16[8,32,128]{2,1,0:T(8,128)(2,1)}, bf16[8,32,128]{2,1,0:T(8,128)(2,1)S(1)}, u32[]{:S(2)}, u32[]{:S(2)}) collective-permute-start(bf16[8,32,128]{2,1,0:T(8,128)(2,1)} %get-tuple-element.10.normed_ref.refs_0_), channel_id=1, source_target_pairs={{0,2},{1,3},{2,0},{3,1},{4,6},{5,7},{6,4},{7,5},{8,10},{9,11},{10,... | collective-permute-start | bytes 196616 | tf_op jit(solution)/shard_map/ppermute | solution.py:200
  54.0 2.4 %collective-permute-done.13.refs_3_ = bf16[8,32,128]{2,1,0:T(8,128)(2,1)S(1)} collective-permute-done((bf16[8,32,128]{2,1,0:T(8,128)(2,1)}, bf16[8,32,128]{2,1,0:T(8,128)(2,1)S(1)}, u32[]{:S(2)}, u32[]{:S(2)}) %collective-permute-start.13) | collective-permute-done | bytes 65568 | tf_op jit(solution)/shard_map/ppermute | solution.py:200
  56.5 1.6 %collective-permute-done.12.refs_2_ = bf16[8,32,128]{2,1,0:T(8,128)(2,1)S(1)} collective-permute-done((bf16[8,32,128]{2,1,0:T(8,128)(2,1)}, bf16[8,32,128]{2,1,0:T(8,128)(2,1)S(1)}, u32[]{:S(2)}, u32[]{:S(2)}) %collective-permute-start.12) | collective-permute-done | bytes 65568 | tf_op jit(solution)/shard_map/ppermute | solution.py:200
  58.0 0.9 %pad_maximum_fusion.1 = bf16[4,8,32,128]{3,2,1,0:T(8,128)(2,1)S(1)} fusion(bf16[1,8,32,128]{3,2,1,0:T(8,128)(2,1)S(1)} %bitcast.36, bf16[1,8,32,128]{3,2,1,0:T(8,128)(2,1)S(1)} %bitcast.37, bf16[1,8,32,128]{3,2,1,0:T(8,128)(2,1)S(1)} %bitcast.39, bf16[1,8,32,128]{3,2,1,0:T(8,128)(2,1)} %bitcast.35), kind=kLoop, calls=%fused_computation.1 | loop fusion | flops 393216 | bytes 524288 | tf_op jit(solution)/shard_map/stack | solution.py:285
  59.0 1.8 %query.1 = (bf16[256,128]{1,0:T(8,128)(2,1)}, f32[256,128]{1,0:T(8,128)}) custom-call(bf16[8,32,128]{2,1,0:T(8,128)(2,1)} %get-tuple-element.10.normed_ref.refs_0_, bf16[128,512]{1,0:T(8,128)(2,1)} %refs_7_.1), custom_call_target="tpu_custom_call" | custom-call | flops 134217728 | bytes 1048576 | tf_op jit(solution)/shard_map/query/pallas_call | solution.py:286
  61.5 4.4 %attend.1 = bf16[8,32,128]{2,1,0:T(8,128)(2,1)} custom-call(s32[2]{0:T(128)} %pad_add_fusion.idx, bf16[8,32,128]{2,1,0:T(8,128)(2,1)} %get-tuple-element.10.normed_ref.refs_0_, bf16[8,32,128]{2,1,0:T(8,128)(2,1)} %copy-done.8, bf16[8,32,128]{2,1,0:T(8,128)(2,1)} %copy-done.6, bf16[8,32,128]{2,1,0:T(8,128)(2,1)} %copy-done.5, ...), custom_call_target="tpu_custom_call" | custom-call | flops 536870912 | bytes 1048576 | tf_op jit(solution)/shard_map/attend/pallas_call | solution.py:296
  (45 shorter events, 8.0 us)
Async XLA Ops:
  1.6 1.7 %collective-permute-start = (bf16[128,1024]{1,0:T(8,128)(2,1)S(1)}, bf16[128,1024]{1,0:T(8,128)(2,1)S(1)}, u32[]{:S(2)}, u32[]{:S(2)}) collective-permute-start(bf16[128,1024]{1,0:T(8,128)(2,1)S(1)} %constant_dynamic-slice_fusion), channel_id=1, source_target_pairs={{0,1},{1,0},{2,3},{3,2},{4,5},{5,4},{6,7},{7,6},{8,9},{9,8},{10,11... | collective-permute-start | bytes 786440 | tf_op jit(solution)/shard_map/ppermute | solution.py:200
  7.2 5.6 %collective-permute-start.1 = (bf16[256,128]{1,0:T(8,128)(2,1)S(1)}, bf16[256,128]{1,0:T(8,128)(2,1)S(1)}, u32[]{:S(2)}, u32[]{:S(2)}) collective-permute-start(bf16[256,128]{1,0:T(8,128)(2,1)S(1)} %get-tuple-element.18), channel_id=1, source_target_pairs={{0,2},{1,3},{2,0},{3,1},{4,6},{5,7},{6,4},{7,5},{8,10},{9,11},{10,... | collective-permute-start | bytes 196616 | tf_op jit(solution)/shard_map/ppermute | solution.py:200
  10.2 6.7 %collective-permute-start.3 = (bf16[256,128]{1,0:T(8,128)(2,1)S(1)}, bf16[256,128]{1,0:T(8,128)(2,1)S(1)}, u32[]{:S(2)}, u32[]{:S(2)}) collective-permute-start(bf16[256,128]{1,0:T(8,128)(2,1)S(1)} %get-tuple-element.19), channel_id=1, source_target_pairs={{0,6},{1,7},{2,4},{3,5},{4,2},{5,3},{6,0},{7,1},{8,14},{9,15},{10,... | collective-permute-start | bytes 196616 | tf_op jit(solution)/shard_map/ppermute | solution.py:200
  12.7 6.6 %collective-permute-start.2 = (bf16[256,128]{1,0:T(8,128)(2,1)S(1)}, bf16[256,128]{1,0:T(8,128)(2,1)S(1)}, u32[]{:S(2)}, u32[]{:S(2)}) collective-permute-start(bf16[256,128]{1,0:T(8,128)(2,1)S(1)} %get-tuple-element.20), channel_id=1, source_target_pairs={{0,4},{1,5},{2,6},{3,7},{4,0},{5,1},{6,2},{7,3},{8,12},{9,13},{10,... | collective-permute-start | bytes 196616 | tf_op jit(solution)/shard_map/ppermute | solution.py:200
  20.1 12.4 %copy-start.1 = (bf16[256,128]{1,0:T(8,128)(2,1)}, bf16[256,128]{1,0:T(8,128)(2,1)S(1)}, u32[]{:S(2)}) copy-start(bf16[256,128]{1,0:T(8,128)(2,1)S(1)} %fusion.2.refs_0_) | copy-start | bytes 196612
  20.1 6.8 %collective-permute-start.6 = (bf16[256,128]{1,0:T(8,128)(2,1)S(1)}, bf16[256,128]{1,0:T(8,128)(2,1)S(1)}, u32[]{:S(2)}, u32[]{:S(2)}) collective-permute-start(bf16[256,128]{1,0:T(8,128)(2,1)S(1)} %fusion.2.refs_0_), channel_id=1, source_target_pairs={{0,6},{1,7},{2,4},{3,5},{4,2},{5,3},{6,0},{7,1},{8,14},{9,15},{10,... | collective-permute-start | bytes 196616 | tf_op jit(solution)/shard_map/ppermute | solution.py:200
  22.8 6.1 %collective-permute-start.5 = (bf16[256,128]{1,0:T(8,128)(2,1)S(1)}, bf16[256,128]{1,0:T(8,128)(2,1)S(1)}, u32[]{:S(2)}, u32[]{:S(2)}) collective-permute-start(bf16[256,128]{1,0:T(8,128)(2,1)S(1)} %fusion.2.refs_0_), channel_id=1, source_target_pairs={{0,4},{1,5},{2,6},{3,7},{4,0},{5,1},{6,2},{7,3},{8,12},{9,13},{10,... | collective-permute-start | bytes 196616 | tf_op jit(solution)/shard_map/ppermute | solution.py:200
  22.8 6.1 %collective-permute-start.4 = (bf16[256,128]{1,0:T(8,128)(2,1)S(1)}, bf16[256,128]{1,0:T(8,128)(2,1)S(1)}, u32[]{:S(2)}, u32[]{:S(2)}) collective-permute-start(bf16[256,128]{1,0:T(8,128)(2,1)S(1)} %fusion.2.refs_0_), channel_id=1, source_target_pairs={{0,2},{1,3},{2,0},{3,1},{4,6},{5,7},{6,4},{7,5},{8,10},{9,11},{10,... | collective-permute-start | bytes 196616 | tf_op jit(solution)/shard_map/ppermute | solution.py:200
  27.0 5.5 %copy-start.7 = (bf16[256,128]{1,0:T(8,128)(2,1)}, bf16[256,128]{1,0:T(8,128)(2,1)S(1)}, u32[]{:S(2)}) copy-start(bf16[256,128]{1,0:T(8,128)(2,1)S(1)} %collective-permute-done.6.refs_3_) | copy-start | bytes 196612
  28.9 3.6 %copy-start.9 = (bf16[256,128]{1,0:T(8,128)(2,1)}, bf16[256,128]{1,0:T(8,128)(2,1)S(1)}, u32[]{:S(2)}) copy-start(bf16[256,128]{1,0:T(8,128)(2,1)S(1)} %collective-permute-done.5.refs_2_) | copy-start | bytes 196612
  28.9 3.6 %copy-start.10 = (bf16[256,128]{1,0:T(8,128)(2,1)}, bf16[256,128]{1,0:T(8,128)(2,1)S(1)}, u32[]{:S(2)}) copy-start(bf16[256,128]{1,0:T(8,128)(2,1)S(1)} %collective-permute-done.4.refs_1_) | copy-start | bytes 196612
  28.9 3.5 %collective-permute-start.7 = (bf16[4,256,128]{2,1,0:T(8,128)(2,1)S(1)}, bf16[4,256,128]{2,1,0:T(8,128)(2,1)S(1)}, u32[]{:S(2)}, u32[]{:S(2)}) collective-permute-start(bf16[4,256,128]{2,1,0:T(8,128)(2,1)S(1)} %pad_maximum_fusion), channel_id=1, source_target_pairs={{0,1},{1,0},{2,3},{3,2},{4,5},{5,4},{6,7},{7,6},{8,9},{9,8},{10,11... | collective-permute-start | bytes 786440 | tf_op jit(solution)/shard_map/ppermute | solution.py:200
  32.5 0.7 %copy-start.12 = (bf16[4,256,128]{2,1,0:T(8,128)(2,1)}, bf16[4,256,128]{2,1,0:T(8,128)(2,1)S(1)}, u32[]{:S(2)}) copy-start(bf16[4,256,128]{2,1,0:T(8,128)(2,1)S(1)} %collective-permute-done.7.refs_4_) | copy-start | bytes 786436
  39.9 5.4 %collective-permute-start.10 = (bf16[256,128]{1,0:T(8,128)(2,1)S(1)}, bf16[256,128]{1,0:T(8,128)(2,1)S(1)}, u32[]{:S(2)}, u32[]{:S(2)}) collective-permute-start(bf16[256,128]{1,0:T(8,128)(2,1)S(1)} %get-tuple-element.14), channel_id=1, source_target_pairs={{0,24},{8,16},{16,8},{24,0},{1,25},{9,17},{17,9},{25,1},{2,26},{10... | collective-permute-start | bytes 196616 | tf_op jit(solution)/shard_map/ppermute | solution.py:200
  42.4 4.3 %collective-permute-start.9 = (bf16[256,128]{1,0:T(8,128)(2,1)S(1)}, bf16[256,128]{1,0:T(8,128)(2,1)S(1)}, u32[]{:S(2)}, u32[]{:S(2)}) collective-permute-start(bf16[256,128]{1,0:T(8,128)(2,1)S(1)} %get-tuple-element.15), channel_id=1, source_target_pairs={{0,16},{8,24},{16,0},{24,8},{1,17},{9,25},{17,1},{25,9},{2,18},{10... | collective-permute-start | bytes 196616 | tf_op jit(solution)/shard_map/ppermute | solution.py:200
  42.9 4.3 %collective-permute-start.8 = (bf16[256,128]{1,0:T(8,128)(2,1)S(1)}, bf16[256,128]{1,0:T(8,128)(2,1)S(1)}, u32[]{:S(2)}, u32[]{:S(2)}) collective-permute-start(bf16[256,128]{1,0:T(8,128)(2,1)S(1)} %get-tuple-element.16), channel_id=1, source_target_pairs={{0,8},{8,0},{16,24},{24,16},{1,9},{9,1},{17,25},{25,17},{2,10},{10... | collective-permute-start | bytes 196616 | tf_op jit(solution)/shard_map/ppermute | solution.py:200
  45.4 1.8 %copy-start.2 = (bf16[256,128]{1,0:T(8,128)(2,1)}, bf16[256,128]{1,0:T(8,128)(2,1)S(1)}, u32[]{:S(2)}) copy-start(bf16[256,128]{1,0:T(8,128)(2,1)S(1)} %collective-permute-done.10.refs_3_) | copy-start | bytes 196612
  49.6 6.8 %collective-permute-start.13 = (bf16[8,32,128]{2,1,0:T(8,128)(2,1)}, bf16[8,32,128]{2,1,0:T(8,128)(2,1)S(1)}, u32[]{:S(2)}, u32[]{:S(2)}) collective-permute-start(bf16[8,32,128]{2,1,0:T(8,128)(2,1)} %get-tuple-element.10.normed_ref.refs_0_), channel_id=1, source_target_pairs={{0,6},{1,7},{2,4},{3,5},{4,2},{5,3},{6,0},{7,1},{8,14},{9,15},{10,... | collective-permute-start | bytes 196616 | tf_op jit(solution)/shard_map/ppermute | solution.py:200
  51.3 6.7 %collective-permute-start.12 = (bf16[8,32,128]{2,1,0:T(8,128)(2,1)}, bf16[8,32,128]{2,1,0:T(8,128)(2,1)S(1)}, u32[]{:S(2)}, u32[]{:S(2)}) collective-permute-start(bf16[8,32,128]{2,1,0:T(8,128)(2,1)} %get-tuple-element.10.normed_ref.refs_0_), channel_id=1, source_target_pairs={{0,4},{1,5},{2,6},{3,7},{4,0},{5,1},{6,2},{7,3},{8,12},{9,13},{10,... | collective-permute-start | bytes 196616 | tf_op jit(solution)/shard_map/ppermute | solution.py:200
  51.4 6.7 %collective-permute-start.11 = (bf16[8,32,128]{2,1,0:T(8,128)(2,1)}, bf16[8,32,128]{2,1,0:T(8,128)(2,1)S(1)}, u32[]{:S(2)}, u32[]{:S(2)}) collective-permute-start(bf16[8,32,128]{2,1,0:T(8,128)(2,1)} %get-tuple-element.10.normed_ref.refs_0_), channel_id=1, source_target_pairs={{0,2},{1,3},{2,0},{3,1},{4,6},{5,7},{6,4},{7,5},{8,10},{9,11},{10,... | collective-permute-start | bytes 196616 | tf_op jit(solution)/shard_map/ppermute | solution.py:200
  56.5 4.4 %copy-start.5 = (bf16[8,32,128]{2,1,0:T(8,128)(2,1)}, bf16[8,32,128]{2,1,0:T(8,128)(2,1)S(1)}, u32[]{:S(2)}) copy-start(bf16[8,32,128]{2,1,0:T(8,128)(2,1)S(1)} %collective-permute-done.13.refs_3_) | copy-start | bytes 196612
  58.0 2.8 %copy-start.6 = (bf16[8,32,128]{2,1,0:T(8,128)(2,1)}, bf16[8,32,128]{2,1,0:T(8,128)(2,1)S(1)}, u32[]{:S(2)}) copy-start(bf16[8,32,128]{2,1,0:T(8,128)(2,1)S(1)} %collective-permute-done.12.refs_2_) | copy-start | bytes 196612
  58.0 2.8 %copy-start.8 = (bf16[8,32,128]{2,1,0:T(8,128)(2,1)}, bf16[8,32,128]{2,1,0:T(8,128)(2,1)S(1)}, u32[]{:S(2)}) copy-start(bf16[8,32,128]{2,1,0:T(8,128)(2,1)S(1)} %collective-permute-done.11.refs_1_) | copy-start | bytes 196612
  58.9 1.9 %collective-permute-start.14 = (bf16[4,8,32,128]{3,2,1,0:T(8,128)(2,1)S(1)}, bf16[4,8,32,128]{3,2,1,0:T(8,128)(2,1)S(1)}, u32[]{:S(2)}, u32[]{:S(2)}) collective-permute-start(bf16[4,8,32,128]{3,2,1,0:T(8,128)(2,1)S(1)} %pad_maximum_fusion.1), channel_id=1, source_target_pairs={{0,1},{1,0},{2,3},{3,2},{4,5},{5,4},{6,7},{7,6},{8,9},{9,8},{10,11... | collective-permute-start | bytes 786440 | tf_op jit(solution)/shard_map/ppermute | solution.py:200
  (4 other events, 2.7 us)

commit v2 on v1

--- a/solution.py
+++ b/solution.py
@@ -6,6 +6,7 @@
 from jax.experimental import pallas as pl
 from jax.experimental.pallas import tpu as pltpu
 from jax.sharding import PartitionSpec as P
+
 
 PROJ_CHANNELS = 32
 CZ = 128
@@ -17,6 +18,7 @@
 WINDOW = R_DEV * PROJ_CHANNELS
 SPAN = WINDOW + LANES
 
+
 epsilon = 1e-05
 VMEM = pl.BlockSpec(memory_space=pltpu.VMEM)
 SMEM = pl.BlockSpec(memory_space=pltpu.SMEM)
@@ -24,21 +26,22 @@
 F32 = jnp.float32
 
 
-def call(kernel, outs, specs, scratch=(), flops=0, name=None):
+def call(kernel, outs, specs, scratch=(), flops=0, limit=8):
     return pl.pallas_call(
         kernel,
         out_shape=outs,
         in_specs=specs,
-        out_specs=jax.tree.map(lambda _: VMEM, outs),
+        out_specs=[VMEM] * len(outs),
         scratch_shapes=list(scratch),
-        name=name,
+        compiler_params=pltpu.CompilerParams(vmem_limit_bytes=limit << 20),
         cost_estimate=pl.CostEstimate(
             flops=flops, bytes_accessed=1 << 20, transcendentals=0
         ),
     )
 
 
-def prep_kernel(idx, off, w_ref, tri_ref, chain_ref, wbd_ref, bias_ref):
+def prep_kernel(idx, off, w_ref, tri_ref, chain_ref, right_ref, wbd_ref, bias_ref, copy_ref):
+    copy_ref[...] = right_ref[...]
     wbd_ref[...] = jnp.zeros_like(wbd_ref)
     for c in range(PROJ_CHANNELS):
         block = w_ref[c * PROJ_CHANNELS : (c + 1) * PROJ_CHANNELS, :]
@@ -58,8 +61,10 @@
         )
 
 
-def select_kernel(idx, starts, own_ref, recv_ref, out_ref, chip_ref):
-    chips, size, half = out_ref.shape
+def select_kernel(idx, starts, own_ref, recv_ref, *refs):
+    outs, chip_ref = refs[:-1], refs[-1]
+    chips = len(outs)
+    size, half = outs[0].shape
     width = own_ref.shape[1]
     res = idx[1]
     core = res % 2
@@ -80,7 +85,7 @@
         base = jnp.clip(start, 0, 2 * width - SPAN) // LANES * LANES
         base = pl.multiple_of(base, LANES)
         pick = (delta == start + first - base).astype(F32).astype(BF)
-        out_ref[k] = lax.dot_general(
+        outs[k][...] = lax.dot_general(
             pick,
             chip_ref[:, pl.ds(base, SPAN)],
             (((1,), (1,)), ((), ())),
@@ -89,10 +94,11 @@
 
 
 def outer_kernel(chips, idx, *refs):
-    mine = refs[:chips]
-    theirs, b_ref, wbd_ref, out_ref, at_ref, lhs_ref, acc_ref = refs[chips:]
+    mine, theirs = refs[:chips], refs[chips : 2 * chips]
+    b_ref, wbd_ref, *outs = refs[2 * chips : -3]
+    at_ref, lhs_ref, acc_ref = refs[-3:]
     size, half = mine[0].shape
-    groups = out_ref.shape[0]
+    groups = len(outs)
     z = idx[1] // 2
     core = idx[1] % 2
     mine_at = pl.multiple_of(core * half, LANES)
@@ -100,7 +106,7 @@
     for k in range(chips):
         row = pl.multiple_of(jnp.bitwise_xor(z, k) * size, size)
         at_ref[pl.ds(row, size), pl.ds(mine_at, half)] = mine[k][...]
-        at_ref[pl.ds(row, size), pl.ds(theirs_at, half)] = theirs[k]
+        at_ref[pl.ds(row, size), pl.ds(theirs_at, half)] = theirs[k][...]
     width = b_ref.shape[1]
     rows = groups * R_DEV
     for n in range(width // (2 * LANES)):
@@ -125,7 +131,7 @@
         block = jnp.stack(
             [block[:, :, j * CZ : (j + 1) * CZ] for j in range(PACK)], axis=1
         )
-        out_ref[k] = block.reshape(chunks * PACK * R_DEV, CZ).astype(BF)
+        outs[k][...] = block.reshape(chunks * PACK * R_DEV, CZ).astype(BF)
 
 
 def norm_kernel(scale, *refs):
@@ -154,8 +160,8 @@
 
 
 def attend_kernel(chips, idx, *refs):
-    mine = refs[:chips]
-    theirs, q_ref, gate_ref, w_ref, wo_ref, bias_ref, out_ref, all_ref, gated_ref = refs[chips:]
+    mine, theirs = refs[:chips], refs[chips : 2 * chips]
+    q_ref, gate_ref, w_ref, wo_ref, bias_ref, out_ref, all_ref, gated_ref = refs[2 * chips :]
     tokens = mine[0].shape[1]
     z = idx[1] // 2
     core = idx[1] % 2
@@ -164,7 +170,7 @@
         mine_at = pl.multiple_of((chip + core) * tokens, tokens)
         theirs_at = pl.multiple_of((chip + 1 - core) * tokens, tokens)
         all_ref[:, pl.ds(mine_at, tokens), :] = mine[k][...]
-        all_ref[:, pl.ds(theirs_at, tokens), :] = theirs[k]
+        all_ref[:, pl.ds(theirs_at, tokens), :] = theirs[k][...]
     scale = DH ** (-0.5)
     lane_head = lax.broadcasted_iota(jnp.int32, (tokens, CZ), 1) // DH
     for u in range(R_DEV):
@@ -230,80 +236,77 @@
     sent = lax.dynamic_slice_in_dim(alignment_left, (1 - core) * half, half, 0)
     recv = swap(sent, "res", 1)
 
-    wbd, bias = call(
+    wbd, bias, right = call(
         prep_kernel,
-        (
-            jax.ShapeDtypeStruct((PROJ_CHANNELS * LANES, PACK * CZ), BF),
-            jax.ShapeDtypeStruct((H * tokens, keys), F32),
-        ),
-        [SMEM, SMEM, VMEM, VMEM, VMEM],
+        [
+            pltpu.VMEM((PROJ_CHANNELS * LANES, PACK * CZ), BF),
+            pltpu.VMEM((H * tokens, keys), F32),
+            pltpu.VMEM(alignment_right.shape, BF),
+        ],
+        [SMEM, SMEM, VMEM, VMEM, VMEM, VMEM],
         flops=1 << 28,
-        name="prep",
-    )(idx, interchain_offset, outer_product_weight, triangle_pair_bias, residue_chain[None, :])
+    )(idx, interchain_offset, outer_product_weight, triangle_pair_bias, residue_chain[None, :], alignment_right)
 
     picked = call(
         select_kernel,
-        jax.ShapeDtypeStruct((chips, size, half), BF),
+        [pltpu.VMEM((size, half), BF)] * chips,
         [SMEM, SMEM, VMEM, VMEM],
         [pltpu.VMEM((half, 2 * width), BF)],
         flops=1 << 28,
-        name="select",
     )(idx, window_starts, alignment_left, recv)
     piece = picked[0]
     for k in range(1, chips):
         piece = piece + swap(picked[k], "res", 2 * k)
     mine = [piece] + [swap(piece, "res", 2 * k) for k in range(1, chips)]
-    theirs = swap(jnp.stack(mine), "res", 1)
+    theirs = [swap(m, "res", 1) for m in mine]
 
     partial = call(
         functools.partial(outer_kernel, chips),
-        jax.ShapeDtypeStruct((groups, R_DEV * tokens, CZ), BF),
-        [SMEM] + [VMEM] * (chips + 3),
+        [pltpu.VMEM((R_DEV * tokens, CZ), BF)] * groups,
+        [SMEM] + [VMEM] * (2 * chips + 2),
         [
             pltpu.VMEM((groups * WINDOW, seqs), BF),
             pltpu.VMEM((rows * width // LANES, PROJ_CHANNELS * LANES), BF),
             pltpu.VMEM((width // LANES, groups, R_DEV, PACK * CZ), F32),
         ],
         flops=1 << 31,
-        name="outer",
-    )(idx, *mine, theirs, alignment_right, wbd)
+        limit=32,
+    )(idx, *mine, *theirs, right, wbd)
     parts = [partial[0]] + [swap(partial[k], "depth", k) for k in range(1, groups)]
 
     pair_strip, normed = call(
         functools.partial(norm_kernel, 1.0 / (seqs * depth_count)),
-        (
+        [
             jax.ShapeDtypeStruct((R_DEV, tokens, CZ), BF),
-            jax.ShapeDtypeStruct((R_DEV, tokens, CZ), BF),
-        ),
+            pltpu.VMEM((R_DEV, tokens, CZ), BF),
+        ],
         [VMEM] * (groups + 1),
         [pltpu.VMEM((R_DEV * tokens, CZ), F32)],
         flops=1 << 24,
-        name="norm",
     )(*parts, outer_product_bias[None, :])
 
     near = [normed] + [swap(normed, "res", 2 * k) for k in range(1, chips)]
-    far = swap(jnp.stack(near), "res", 1)
+    far = [swap(n, "res", 1) for n in near]
     queries, gate = call(
         query_kernel,
-        (
-            jax.ShapeDtypeStruct((R_DEV * tokens, CZ), BF),
-            jax.ShapeDtypeStruct((R_DEV * tokens, CZ), F32),
-        ),
+        [
+            pltpu.VMEM((R_DEV * tokens, CZ), BF),
+            pltpu.VMEM((R_DEV * tokens, CZ), F32),
+        ],
         [VMEM] * 2,
         flops=1 << 27,
-        name="query",
     )(normed, query_key_value_gate_weight)
-    update = call(
+    (update,) = call(
         functools.partial(attend_kernel, chips),
-        jax.ShapeDtypeStruct((R_DEV, tokens, CZ), BF),
-        [SMEM] + [VMEM] * (chips + 6),
+        [jax.ShapeDtypeStruct((R_DEV, tokens, CZ), BF)],
+        [SMEM] + [VMEM] * (2 * chips + 5),
         [
             pltpu.VMEM((R_DEV, keys, CZ), BF),
             pltpu.VMEM((R_DEV * tokens, CZ), BF),
         ],
         flops=1 << 29,
-        name="attend",
-    )(idx, *near, far, queries, gate, query_key_value_gate_weight, output_weight, bias)
+        limit=16,
+    )(idx, *near, *far, queries, gate, query_key_value_gate_weight, output_weight, bias)
     return (pair_strip, update)
 
 

time: 66.5 us -> 55.9 us (0.84)
  Pallas kernels: 18.9 us -> 9.01 us
  other arithmetic: 2.47 us -> 0.09 us
  starting transfers between devices: 18.6 us -> 19.6 us
  local copies, waits for them, and re-layouts: 6.17 us -> 6.85 us
    pallas_call x6, Pallas kernels: 18.9 us -> 9.01 us  [the longest x1 3.69 us: body(): call(functools.partial(attend_kernel, chips), [jax.ShapeDtypeStruct((R_DE...]
    unnamed x26 -> x20, local copies, waits for them, and re-layouts: 2.7 us -> 5.88 us
    squeeze x2 -> x0, local copies, waits for them, and re-layouts: 2.5 us -> none  [the longest x1 1.58 us: body(): partial[k]]
    ppermute x15 -> x21, starting transfers between devices: 18.6 us -> 19.6 us  [swap(): return lax.ppermute(x, axis, [(i, i ^ mask) for i in range(n)])]
    another operation x2 -> x0, other arithmetic: 0.96 us -> none  [the longest x1 0.92 us: body(): far = swap(jnp.stack(near), 'res', 1)]
    add x1, other arithmetic: 0.86 us -> 0.02 us  [body(): piece = piece + swap(picked[k], 'res', 2 * k)]
    ppermute x15 -> x21, waiting for transfers between devices: 19 us -> 19.2 us  [swap(): return lax.ppermute(x, axis, [(i, i ^ mask) for i in range(n)])]
  transfers between devices with their start and end apart: 15 -> 21, of which waited for: 10 -> 12; matrix products, arithmetic and copies ran while one was open for 1% -> 0% of each run, Pallas kernels for 8% -> 2%
where the time goes in v2:
time: 55.9 us; the launch traced here: 55.5 us
  starting transfers between devices  19.6 us (35%)
  waiting for transfers between devices  19.2 us (34%)
  Pallas kernels  9.01 us (16%)
  local copies, waits for them, and re-layouts  6.85 us (12%)
  between operations  0.78 us (1%)
    ppermute x21, starting transfers between devices, swap(): return lax.ppermute(x, axis, [(i, i ^ mask) for i in range(n)])  19.6 us
    ppermute x21, waiting for transfers between devices, swap(): return lax.ppermute(x, axis, [(i, i ^ mask) for i in range(n)])  19.2 us
    unnamed x20, local copies, waits for them, and re-layouts  5.88 us
    pallas_call x1, Pallas kernels, body(): call(functools.partial(attend_kernel, chips), [jax.ShapeDtypeStruct((R_DE...  3.69 us
    pallas_call x1, Pallas kernels, body(): call(functools.partial(outer_kernel, chips), [pltpu.VMEM((R_DEV * tokens,...  2.48 us
  transfers between devices with their start and end apart: 21, of which 12 were waited for; matrix products, arithmetic and copies ran while one was open for 0% of the time, Pallas kernels for 2%

profile of v2, /device:TPU:0, one launch (start us, length us, event | category | flops | bytes accessed | tf_op | source)
XLA Modules:
  0.0 55.5 jit_solution(16099726697571052354)
XLA Ops:
  0.6 1.0 %constant_dynamic-slice_fusion = bf16[128,1024]{1,0:T(8,128)(2,1)S(1)} fusion(bf16[256,1024]{1,0:T(8,128)(2,1)} %own_ref.1, s32[]{:T(128)S(6)} %select_n.11), kind=kLoop, calls=%fused_computation.2 | loop fusion | bytes 524292 | tf_op jit(solution)/shard_map/dynamic_slice | solution.py:236
  2.3 1.1 %collective-permute-done.recv_ref = bf16[128,1024]{1,0:T(8,128)(2,1)S(1)} collective-permute-done((bf16[128,1024]{1,0:T(8,128)(2,1)S(1)}, bf16[128,1024]{1,0:T(8,128)(2,1)S(1)}, u32[]{:S(2)}, u32[]{:S(2)}) %collective-permute-start) | collective-permute-done | bytes 262176 | tf_op jit(solution)/shard_map/ppermute | solution.py:206
  3.3 1.0 %copy-done = bf16[256,1024]{1,0:T(8,128)(2,1)S(1)} copy-done((bf16[256,1024]{1,0:T(8,128)(2,1)S(1)}, bf16[256,1024]{1,0:T(8,128)(2,1)}, u32[]{:S(2)}) %copy-start) | copy-done | bytes 524312
  5.0 1.0 %shard_map.113 = (bf16[256,128]{1,0:T(8,128)(2,1)S(1)}, bf16[256,128]{1,0:T(8,128)(2,1)S(1)}, bf16[256,128]{1,0:T(8,128)(2,1)S(1)}, bf16[256,128]{1,0:T(8,128)(2,1)S(1)}) custom-call(s32[2]{0:T(128)S(1)} %pad_add_fusion.idx, s32[4]{0:T(128)S(1)} %copy-done.8, bf16[256,1024]{1,0:T(8,128)(2,1)S(1)} %copy-done, bf16[128,1024]{1,0:T(8,128)(2,1)S(1)} %collective-permute-done.recv_ref), custom_call_target="tpu_custom_call" | custom-call | flops 268435456 | bytes 1048576 | tf_op jit(solution)/shard_map/pallas_call | solution.py:250
  6.0 3.0 %collective-permute-start.1 = (bf16[256,128]{1,0:T(8,128)(2,1)S(1)}, bf16[256,128]{1,0:T(8,128)(2,1)S(1)}, u32[]{:S(2)}, u32[]{:S(2)}) collective-permute-start(bf16[256,128]{1,0:T(8,128)(2,1)S(1)} %get-tuple-element.18), channel_id=1, source_target_pairs={{0,2},{1,3},{2,0},{3,1},{4,6},{5,7},{6,4},{7,5},{8,10},{9,11},{10,... | collective-permute-start | bytes 196616 | tf_op jit(solution)/shard_map/ppermute | solution.py:206
  9.0 2.6 %collective-permute-start.2 = (bf16[256,128]{1,0:T(8,128)(2,1)S(1)}, bf16[256,128]{1,0:T(8,128)(2,1)S(1)}, u32[]{:S(2)}, u32[]{:S(2)}) collective-permute-start(bf16[256,128]{1,0:T(8,128)(2,1)S(1)} %get-tuple-element.19), channel_id=1, source_target_pairs={{0,4},{1,5},{2,6},{3,7},{4,0},{5,1},{6,2},{7,3},{8,12},{9,13},{10,... | collective-permute-start | bytes 196616 | tf_op jit(solution)/shard_map/ppermute | solution.py:206
  11.6 4.9 %collective-permute-done.2 = bf16[256,128]{1,0:T(8,128)(2,1)S(1)} collective-permute-done((bf16[256,128]{1,0:T(8,128)(2,1)S(1)}, bf16[256,128]{1,0:T(8,128)(2,1)S(1)}, u32[]{:S(2)}, u32[]{:S(2)}) %collective-permute-start.2) | collective-permute-done | bytes 65568 | tf_op jit(solution)/shard_map/ppermute | solution.py:206
  16.5 1.2 %collective-permute-done.3 = bf16[256,128]{1,0:T(8,128)(2,1)S(1)} collective-permute-done((bf16[256,128]{1,0:T(8,128)(2,1)S(1)}, bf16[256,128]{1,0:T(8,128)(2,1)S(1)}, u32[]{:S(2)}, u32[]{:S(2)}) %collective-permute-start.3) | collective-permute-done | bytes 65568 | tf_op jit(solution)/shard_map/ppermute | solution.py:206
  17.8 2.0 %collective-permute-start.6 = (bf16[256,128]{1,0:T(8,128)(2,1)S(1)}, bf16[256,128]{1,0:T(8,128)(2,1)S(1)}, u32[]{:S(2)}, u32[]{:S(2)}) collective-permute-start(bf16[256,128]{1,0:T(8,128)(2,1)S(1)} %add_add_fusion.refs_0_), channel_id=1, source_target_pairs={{0,6},{1,7},{2,4},{3,5},{4,2},{5,3},{6,0},{7,1},{8,14},{9,15},{10,... | collective-permute-start | bytes 196616 | tf_op jit(solution)/shard_map/ppermute | solution.py:206
  20.2 2.1 %collective-permute-start.4 = (bf16[256,128]{1,0:T(8,128)(2,1)S(1)}, bf16[256,128]{1,0:T(8,128)(2,1)S(1)}, u32[]{:S(2)}, u32[]{:S(2)}) collective-permute-start(bf16[256,128]{1,0:T(8,128)(2,1)S(1)} %add_add_fusion.refs_0_), channel_id=1, source_target_pairs={{0,2},{1,3},{2,0},{3,1},{4,6},{5,7},{6,4},{7,5},{8,10},{9,11},{10,... | collective-permute-start | bytes 196616 | tf_op jit(solution)/shard_map/ppermute | solution.py:206
  22.3 1.8 %collective-permute-done.6.refs_3_ = bf16[256,128]{1,0:T(8,128)(2,1)S(1)} collective-permute-done((bf16[256,128]{1,0:T(8,128)(2,1)S(1)}, bf16[256,128]{1,0:T(8,128)(2,1)S(1)}, u32[]{:S(2)}, u32[]{:S(2)}) %collective-permute-start.6) | collective-permute-done | bytes 65568 | tf_op jit(solution)/shard_map/ppermute | solution.py:206
  24.1 1.5 %collective-permute-done.5.refs_2_ = bf16[256,128]{1,0:T(8,128)(2,1)S(1)} collective-permute-done((bf16[256,128]{1,0:T(8,128)(2,1)S(1)}, bf16[256,128]{1,0:T(8,128)(2,1)S(1)}, u32[]{:S(2)}, u32[]{:S(2)}) %collective-permute-start.5) | collective-permute-done | bytes 65568 | tf_op jit(solution)/shard_map/ppermute | solution.py:206
  26.1 1.0 %copy-done.2 = bf16[256,1024]{1,0:T(8,128)(2,1)S(1)} copy-done((bf16[256,1024]{1,0:T(8,128)(2,1)S(1)}, bf16[256,1024]{1,0:T(8,128)(2,1)}, u32[]{:S(2)}) %copy-start.2) | copy-done | bytes 524312
  30.3 1.0 %shard_map.114 = (bf16[4096,512]{1,0:T(8,128)(2,1)S(1)}, f32[128,256]{1,0:T(8,128)S(1)}, bf16[256,1024]{1,0:T(8,128)(2,1)S(1)}) custom-call(s32[2]{0:T(128)S(1)} %pad_add_fusion.idx, f32[4]{0:T(128)S(1)} %copy-done.9, bf16[1024,128]{1,0:T(8,128)(2,1)S(1)} %copy-done.3, bf16[4,32,256]{2,1,0:T(8,128)(2,1)S(1)} %copy-done.5, s32[1,256]{1,0:T(1,128)S(1)} %bitcast.5, ...), custom_call_target="tpu_custom_call" | custom-call | flops 268435456 | bytes 1048576 | tf_op jit(solution)/shard_map/pallas_call | solution.py:239
  31.4 2.5 %shard_map.115 = (bf16[256,128]{1,0:T(8,128)(2,1)S(1)}, bf16[256,128]{1,0:T(8,128)(2,1)S(1)}, bf16[256,128]{1,0:T(8,128)(2,1)S(1)}, bf16[256,128]{1,0:T(8,128)(2,1)S(1)}) custom-call(s32[2]{0:T(128)S(1)} %pad_add_fusion.idx, bf16[256,128]{1,0:T(8,128)(2,1)S(1)} %add_add_fusion.refs_0_, bf16[256,128]{1,0:T(8,128)(2,1)S(1)} %collective-permute-done.4.refs_1_, ...), custom_call_target="tpu_custom_call" | custom-call | flops 2147483648 | bytes 1048576 | tf_op jit(solution)/shard_map/pallas_call | solution.py:263
  33.8 1.6 %collective-permute-start.11 = (bf16[256,128]{1,0:T(8,128)(2,1)S(1)}, bf16[256,128]{1,0:T(8,128)(2,1)S(1)}, u32[]{:S(2)}, u32[]{:S(2)}) collective-permute-start(bf16[256,128]{1,0:T(8,128)(2,1)S(1)} %get-tuple-element.24), channel_id=1, source_target_pairs={{0,8},{8,0},{16,24},{24,16},{1,9},{9,1},{17,25},{25,17},{2,10},{10... | collective-permute-start | bytes 196616 | tf_op jit(solution)/shard_map/ppermute | solution.py:206
  35.4 1.5 %collective-permute-start.12 = (bf16[256,128]{1,0:T(8,128)(2,1)S(1)}, bf16[256,128]{1,0:T(8,128)(2,1)S(1)}, u32[]{:S(2)}, u32[]{:S(2)}) collective-permute-start(bf16[256,128]{1,0:T(8,128)(2,1)S(1)} %get-tuple-element.25), channel_id=1, source_target_pairs={{0,16},{8,24},{16,0},{24,8},{1,17},{9,25},{17,1},{25,9},{2,18},{10... | collective-permute-start | bytes 196616 | tf_op jit(solution)/shard_map/ppermute | solution.py:206
  38.2 1.5 %collective-permute-done.12.refs_2_ = bf16[256,128]{1,0:T(8,128)(2,1)S(1)} collective-permute-done((bf16[256,128]{1,0:T(8,128)(2,1)S(1)}, bf16[256,128]{1,0:T(8,128)(2,1)S(1)}, u32[]{:S(2)}, u32[]{:S(2)}) %collective-permute-start.12) | collective-permute-done | bytes 65568 | tf_op jit(solution)/shard_map/ppermute | solution.py:206
  39.7 2.4 %collective-permute-done.13.refs_3_ = bf16[256,128]{1,0:T(8,128)(2,1)S(1)} collective-permute-done((bf16[256,128]{1,0:T(8,128)(2,1)S(1)}, bf16[256,128]{1,0:T(8,128)(2,1)S(1)}, u32[]{:S(2)}, u32[]{:S(2)}) %collective-permute-start.13) | collective-permute-done | bytes 65568 | tf_op jit(solution)/shard_map/ppermute | solution.py:206
  42.8 1.9 %collective-permute-start.16 = (bf16[8,32,128]{2,1,0:T(8,128)(2,1)S(1)}, bf16[8,32,128]{2,1,0:T(8,128)(2,1)S(1)}, u32[]{:S(2)}, u32[]{:S(2)}) collective-permute-start(bf16[8,32,128]{2,1,0:T(8,128)(2,1)S(1)} %get-tuple-element.28.normed_ref.refs_0_), channel_id=1, source_target_pairs={{0,6},{1,7},{2,4},{3,5},{4,2},{5,3},{6,0},{7,1},{8,14},{9,15},{10,... | collective-permute-start | bytes 196616 | tf_op jit(solution)/shard_map/ppermute | solution.py:206
  44.7 2.4 %collective-permute-start.14 = (bf16[8,32,128]{2,1,0:T(8,128)(2,1)S(1)}, bf16[8,32,128]{2,1,0:T(8,128)(2,1)S(1)}, u32[]{:S(2)}, u32[]{:S(2)}) collective-permute-start(bf16[8,32,128]{2,1,0:T(8,128)(2,1)S(1)} %get-tuple-element.28.normed_ref.refs_0_), channel_id=1, source_target_pairs={{0,2},{1,3},{2,0},{3,1},{4,6},{5,7},{6,4},{7,5},{8,10},{9,11},{10,... | collective-permute-start | bytes 196616 | tf_op jit(solution)/shard_map/ppermute | solution.py:206
  47.2 1.8 %collective-permute-done.16.refs_3_ = bf16[8,32,128]{2,1,0:T(8,128)(2,1)S(1)} collective-permute-done((bf16[8,32,128]{2,1,0:T(8,128)(2,1)S(1)}, bf16[8,32,128]{2,1,0:T(8,128)(2,1)S(1)}, u32[]{:S(2)}, u32[]{:S(2)}) %collective-permute-start.16) | collective-permute-done | bytes 65568 | tf_op jit(solution)/shard_map/ppermute | solution.py:206
  49.0 1.4 %collective-permute-done.15.refs_2_ = bf16[8,32,128]{2,1,0:T(8,128)(2,1)S(1)} collective-permute-done((bf16[8,32,128]{2,1,0:T(8,128)(2,1)S(1)}, bf16[8,32,128]{2,1,0:T(8,128)(2,1)S(1)}, u32[]{:S(2)}, u32[]{:S(2)}) %collective-permute-start.15) | collective-permute-done | bytes 65568 | tf_op jit(solution)/shard_map/ppermute | solution.py:206
  51.8 3.7 %shard_map.118 = bf16[8,32,128]{2,1,0:T(8,128)(2,1)} custom-call(s32[2]{0:T(128)S(1)} %pad_add_fusion.idx, bf16[8,32,128]{2,1,0:T(8,128)(2,1)S(1)} %get-tuple-element.28.normed_ref.refs_0_, bf16[8,32,128]{2,1,0:T(8,128)(2,1)S(1)} %collective-permute-done.14.refs_1_, bf16[8,32,128]{2,1,0:T(8,128)(2,1)S(1)} %collective-permute-done.15.refs_2_, ...), custom_call_target="tpu_custom_call" | custom-call | flops 536870912 | bytes 1048576 | tf_op jit(solution)/shard_map/pallas_call | solution.py:299
  (47 shorter events, 8.6 us)
Async XLA Ops:
  1.6 1.7 %collective-permute-start = (bf16[128,1024]{1,0:T(8,128)(2,1)S(1)}, bf16[128,1024]{1,0:T(8,128)(2,1)S(1)}, u32[]{:S(2)}, u32[]{:S(2)}) collective-permute-start(bf16[128,1024]{1,0:T(8,128)(2,1)S(1)} %constant_dynamic-slice_fusion), channel_id=1, source_target_pairs={{0,1},{1,0},{2,3},{3,2},{4,5},{5,4},{6,7},{7,6},{8,9},{9,8},{10,11... | collective-permute-start | bytes 786440 | tf_op jit(solution)/shard_map/ppermute | solution.py:206
  6.0 5.6 %collective-permute-start.1 = (bf16[256,128]{1,0:T(8,128)(2,1)S(1)}, bf16[256,128]{1,0:T(8,128)(2,1)S(1)}, u32[]{:S(2)}, u32[]{:S(2)}) collective-permute-start(bf16[256,128]{1,0:T(8,128)(2,1)S(1)} %get-tuple-element.18), channel_id=1, source_target_pairs={{0,2},{1,3},{2,0},{3,1},{4,6},{5,7},{6,4},{7,5},{8,10},{9,11},{10,... | collective-permute-start | bytes 196616 | tf_op jit(solution)/shard_map/ppermute | solution.py:206
  9.0 7.5 %collective-permute-start.2 = (bf16[256,128]{1,0:T(8,128)(2,1)S(1)}, bf16[256,128]{1,0:T(8,128)(2,1)S(1)}, u32[]{:S(2)}, u32[]{:S(2)}) collective-permute-start(bf16[256,128]{1,0:T(8,128)(2,1)S(1)} %get-tuple-element.19), channel_id=1, source_target_pairs={{0,4},{1,5},{2,6},{3,7},{4,0},{5,1},{6,2},{7,3},{8,12},{9,13},{10,... | collective-permute-start | bytes 196616 | tf_op jit(solution)/shard_map/ppermute | solution.py:206
  11.6 6.2 %collective-permute-start.3 = (bf16[256,128]{1,0:T(8,128)(2,1)S(1)}, bf16[256,128]{1,0:T(8,128)(2,1)S(1)}, u32[]{:S(2)}, u32[]{:S(2)}) collective-permute-start(bf16[256,128]{1,0:T(8,128)(2,1)S(1)} %get-tuple-element.20), channel_id=1, source_target_pairs={{0,6},{1,7},{2,4},{3,5},{4,2},{5,3},{6,0},{7,1},{8,14},{9,15},{10,... | collective-permute-start | bytes 196616 | tf_op jit(solution)/shard_map/ppermute | solution.py:206
  17.8 6.3 %collective-permute-start.6 = (bf16[256,128]{1,0:T(8,128)(2,1)S(1)}, bf16[256,128]{1,0:T(8,128)(2,1)S(1)}, u32[]{:S(2)}, u32[]{:S(2)}) collective-permute-start(bf16[256,128]{1,0:T(8,128)(2,1)S(1)} %add_add_fusion.refs_0_), channel_id=1, source_target_pairs={{0,6},{1,7},{2,4},{3,5},{4,2},{5,3},{6,0},{7,1},{8,14},{9,15},{10,... | collective-permute-start | bytes 196616 | tf_op jit(solution)/shard_map/ppermute | solution.py:206
  19.9 5.7 %collective-permute-start.5 = (bf16[256,128]{1,0:T(8,128)(2,1)S(1)}, bf16[256,128]{1,0:T(8,128)(2,1)S(1)}, u32[]{:S(2)}, u32[]{:S(2)}) collective-permute-start(bf16[256,128]{1,0:T(8,128)(2,1)S(1)} %add_add_fusion.refs_0_), channel_id=1, source_target_pairs={{0,4},{1,5},{2,6},{3,7},{4,0},{5,1},{6,2},{7,3},{8,12},{9,13},{10,... | collective-permute-start | bytes 196616 | tf_op jit(solution)/shard_map/ppermute | solution.py:206
  20.2 5.4 %collective-permute-start.4 = (bf16[256,128]{1,0:T(8,128)(2,1)S(1)}, bf16[256,128]{1,0:T(8,128)(2,1)S(1)}, u32[]{:S(2)}, u32[]{:S(2)}) collective-permute-start(bf16[256,128]{1,0:T(8,128)(2,1)S(1)} %add_add_fusion.refs_0_), channel_id=1, source_target_pairs={{0,2},{1,3},{2,0},{3,1},{4,6},{5,7},{6,4},{7,5},{8,10},{9,11},{10,... | collective-permute-start | bytes 196616 | tf_op jit(solution)/shard_map/ppermute | solution.py:206
  22.3 9.1 %collective-permute-start.7 = (bf16[256,128]{1,0:T(8,128)(2,1)S(1)}, bf16[256,128]{1,0:T(8,128)(2,1)S(1)}, u32[]{:S(2)}, u32[]{:S(2)}) collective-permute-start(bf16[256,128]{1,0:T(8,128)(2,1)S(1)} %add_add_fusion.refs_0_), channel_id=1, source_target_pairs={{0,1},{1,0},{2,3},{3,2},{4,5},{5,4},{6,7},{7,6},{8,9},{9,8},{10,11... | collective-permute-start | bytes 196616 | tf_op jit(solution)/shard_map/ppermute | solution.py:206
  24.1 7.3 %collective-permute-start.10 = (bf16[256,128]{1,0:T(8,128)(2,1)S(1)}, bf16[256,128]{1,0:T(8,128)(2,1)S(1)}, u32[]{:S(2)}, u32[]{:S(2)}) collective-permute-start(bf16[256,128]{1,0:T(8,128)(2,1)S(1)} %collective-permute-done.6.refs_3_), channel_id=1, source_target_pairs={{0,1},{1,0},{2,3},{3,2},{4,5},{5,4},{6,7},{7,6},{8,9},{9,8},{10,11... | collective-permute-start | bytes 196616 | tf_op jit(solution)/shard_map/ppermute | solution.py:206
  25.6 5.7 %collective-permute-start.9 = (bf16[256,128]{1,0:T(8,128)(2,1)S(1)}, bf16[256,128]{1,0:T(8,128)(2,1)S(1)}, u32[]{:S(2)}, u32[]{:S(2)}) collective-permute-start(bf16[256,128]{1,0:T(8,128)(2,1)S(1)} %collective-permute-done.5.refs_2_), channel_id=1, source_target_pairs={{0,1},{1,0},{2,3},{3,2},{4,5},{5,4},{6,7},{7,6},{8,9},{9,8},{10,11... | collective-permute-start | bytes 196616 | tf_op jit(solution)/shard_map/ppermute | solution.py:206
  25.6 5.7 %collective-permute-start.8 = (bf16[256,128]{1,0:T(8,128)(2,1)S(1)}, bf16[256,128]{1,0:T(8,128)(2,1)S(1)}, u32[]{:S(2)}, u32[]{:S(2)}) collective-permute-start(bf16[256,128]{1,0:T(8,128)(2,1)S(1)} %collective-permute-done.4.refs_1_), channel_id=1, source_target_pairs={{0,1},{1,0},{2,3},{3,2},{4,5},{5,4},{6,7},{7,6},{8,9},{9,8},{10,11... | collective-permute-start | bytes 196616 | tf_op jit(solution)/shard_map/ppermute | solution.py:206
  31.3 10.8 %copy-start.1 = (f32[128]{0:T(128)S(1)}, f32[128]{0:T(128)}, u32[]{:S(2)}) copy-start(f32[128]{0:T(128)} %param.14) | copy-start | bytes 1540
  31.3 19.6 %copy-start.4 = (bf16[128,512]{1,0:T(8,128)(2,1)S(1)}, bf16[128,512]{1,0:T(8,128)(2,1)}, u32[]{:S(2)}) copy-start(bf16[128,512]{1,0:T(8,128)(2,1)} %refs_10_.1) | copy-start | bytes 393220
  31.3 20.5 %copy-start.6 = (bf16[128,128]{1,0:T(8,128)(2,1)S(1)}, bf16[128,128]{1,0:T(8,128)(2,1)}, u32[]{:S(2)}) copy-start(bf16[128,128]{1,0:T(8,128)(2,1)} %refs_11_.1) | copy-start | bytes 98308
  33.8 4.3 %collective-permute-start.11 = (bf16[256,128]{1,0:T(8,128)(2,1)S(1)}, bf16[256,128]{1,0:T(8,128)(2,1)S(1)}, u32[]{:S(2)}, u32[]{:S(2)}) collective-permute-start(bf16[256,128]{1,0:T(8,128)(2,1)S(1)} %get-tuple-element.24), channel_id=1, source_target_pairs={{0,8},{8,0},{16,24},{24,16},{1,9},{9,1},{17,25},{25,17},{2,10},{10... | collective-permute-start | bytes 196616 | tf_op jit(solution)/shard_map/ppermute | solution.py:206
  35.4 4.3 %collective-permute-start.12 = (bf16[256,128]{1,0:T(8,128)(2,1)S(1)}, bf16[256,128]{1,0:T(8,128)(2,1)S(1)}, u32[]{:S(2)}, u32[]{:S(2)}) collective-permute-start(bf16[256,128]{1,0:T(8,128)(2,1)S(1)} %get-tuple-element.25), channel_id=1, source_target_pairs={{0,16},{8,24},{16,0},{24,8},{1,17},{9,25},{17,1},{25,9},{2,18},{10... | collective-permute-start | bytes 196616 | tf_op jit(solution)/shard_map/ppermute | solution.py:206
  36.9 5.2 %collective-permute-start.13 = (bf16[256,128]{1,0:T(8,128)(2,1)S(1)}, bf16[256,128]{1,0:T(8,128)(2,1)S(1)}, u32[]{:S(2)}, u32[]{:S(2)}) collective-permute-start(bf16[256,128]{1,0:T(8,128)(2,1)S(1)} %get-tuple-element.26), channel_id=1, source_target_pairs={{0,24},{8,16},{16,8},{24,0},{1,25},{9,17},{17,9},{25,1},{2,26},{10... | collective-permute-start | bytes 196616 | tf_op jit(solution)/shard_map/ppermute | solution.py:206
  42.8 6.2 %collective-permute-start.16 = (bf16[8,32,128]{2,1,0:T(8,128)(2,1)S(1)}, bf16[8,32,128]{2,1,0:T(8,128)(2,1)S(1)}, u32[]{:S(2)}, u32[]{:S(2)}) collective-permute-start(bf16[8,32,128]{2,1,0:T(8,128)(2,1)S(1)} %get-tuple-element.28.normed_ref.refs_0_), channel_id=1, source_target_pairs={{0,6},{1,7},{2,4},{3,5},{4,2},{5,3},{6,0},{7,1},{8,14},{9,15},{10,... | collective-permute-start | bytes 196616 | tf_op jit(solution)/shard_map/ppermute | solution.py:206
  44.7 5.7 %collective-permute-start.15 = (bf16[8,32,128]{2,1,0:T(8,128)(2,1)S(1)}, bf16[8,32,128]{2,1,0:T(8,128)(2,1)S(1)}, u32[]{:S(2)}, u32[]{:S(2)}) collective-permute-start(bf16[8,32,128]{2,1,0:T(8,128)(2,1)S(1)} %get-tuple-element.28.normed_ref.refs_0_), channel_id=1, source_target_pairs={{0,4},{1,5},{2,6},{3,7},{4,0},{5,1},{6,2},{7,3},{8,12},{9,13},{10,... | collective-permute-start | bytes 196616 | tf_op jit(solution)/shard_map/ppermute | solution.py:206
  44.7 5.7 %collective-permute-start.14 = (bf16[8,32,128]{2,1,0:T(8,128)(2,1)S(1)}, bf16[8,32,128]{2,1,0:T(8,128)(2,1)S(1)}, u32[]{:S(2)}, u32[]{:S(2)}) collective-permute-start(bf16[8,32,128]{2,1,0:T(8,128)(2,1)S(1)} %get-tuple-element.28.normed_ref.refs_0_), channel_id=1, source_target_pairs={{0,2},{1,3},{2,0},{3,1},{4,6},{5,7},{6,4},{7,5},{8,10},{9,11},{10,... | collective-permute-start | bytes 196616 | tf_op jit(solution)/shard_map/ppermute | solution.py:206
  47.2 3.9 %collective-permute-start.17 = (bf16[8,32,128]{2,1,0:T(8,128)(2,1)S(1)}, bf16[8,32,128]{2,1,0:T(8,128)(2,1)S(1)}, u32[]{:S(2)}, u32[]{:S(2)}) collective-permute-start(bf16[8,32,128]{2,1,0:T(8,128)(2,1)S(1)} %get-tuple-element.28.normed_ref.refs_0_), channel_id=1, source_target_pairs={{0,1},{1,0},{2,3},{3,2},{4,5},{5,4},{6,7},{7,6},{8,9},{9,8},{10,11... | collective-permute-start | bytes 196616 | tf_op jit(solution)/shard_map/ppermute | solution.py:206
  49.0 2.1 %collective-permute-start.20 = (bf16[8,32,128]{2,1,0:T(8,128)(2,1)S(1)}, bf16[8,32,128]{2,1,0:T(8,128)(2,1)S(1)}, u32[]{:S(2)}, u32[]{:S(2)}) collective-permute-start(bf16[8,32,128]{2,1,0:T(8,128)(2,1)S(1)} %collective-permute-done.16.refs_3_), channel_id=1, source_target_pairs={{0,1},{1,0},{2,3},{3,2},{4,5},{5,4},{6,7},{7,6},{8,9},{9,8},{10,11... | collective-permute-start | bytes 196616 | tf_op jit(solution)/shard_map/ppermute | solution.py:206
  50.4 1.3 %collective-permute-start.19 = (bf16[8,32,128]{2,1,0:T(8,128)(2,1)S(1)}, bf16[8,32,128]{2,1,0:T(8,128)(2,1)S(1)}, u32[]{:S(2)}, u32[]{:S(2)}) collective-permute-start(bf16[8,32,128]{2,1,0:T(8,128)(2,1)S(1)} %collective-permute-done.15.refs_2_), channel_id=1, source_target_pairs={{0,1},{1,0},{2,3},{3,2},{4,5},{5,4},{6,7},{7,6},{8,9},{9,8},{10,11... | collective-permute-start | bytes 196616 | tf_op jit(solution)/shard_map/ppermute | solution.py:206
  50.4 1.4 %collective-permute-start.18 = (bf16[8,32,128]{2,1,0:T(8,128)(2,1)S(1)}, bf16[8,32,128]{2,1,0:T(8,128)(2,1)S(1)}, u32[]{:S(2)}, u32[]{:S(2)}) collective-permute-start(bf16[8,32,128]{2,1,0:T(8,128)(2,1)S(1)} %collective-permute-done.14.refs_1_), channel_id=1, source_target_pairs={{0,1},{1,0},{2,3},{3,2},{4,5},{5,4},{6,7},{7,6},{8,9},{9,8},{10,11... | collective-permute-start | bytes 196616 | tf_op jit(solution)/shard_map/ppermute | solution.py:206
  (7 other events, 5.9 us)

commit v3 on v2

--- a/solution.py
+++ b/solution.py
@@ -22,6 +22,7 @@
 epsilon = 1e-05
 VMEM = pl.BlockSpec(memory_space=pltpu.VMEM)
 SMEM = pl.BlockSpec(memory_space=pltpu.SMEM)
+ANY = pl.BlockSpec(memory_space=pltpu.HBM)
 BF = jnp.bfloat16
 F32 = jnp.float32
 
@@ -31,7 +32,9 @@
         kernel,
         out_shape=outs,
         in_specs=specs,
-        out_specs=[VMEM] * len(outs),
+        out_specs=[
+            SMEM if getattr(o, "memory_space", None) == pltpu.SMEM else VMEM for o in outs
+        ],
         scratch_shapes=list(scratch),
         compiler_params=pltpu.CompilerParams(vmem_limit_bytes=limit << 20),
         cost_estimate=pl.CostEstimate(
@@ -40,16 +43,43 @@
     )
 
 
-def prep_kernel(idx, off, w_ref, tri_ref, chain_ref, right_ref, wbd_ref, bias_ref, copy_ref):
-    copy_ref[...] = right_ref[...]
+def front_kernel(left_ref, starts_ref, sent_ref, kept_ref, table_ref, sem):
+    half = sent_ref.shape[0]
+    core = lax.axis_index("res") % 2
+    sent_at = pl.multiple_of((1 - core) * half, half)
+    kept_at = pl.multiple_of(core * half, half)
+    copies = [
+        pltpu.make_async_copy(left_ref.at[pl.ds(sent_at, half)], sent_ref, sem.at[0]),
+        pltpu.make_async_copy(left_ref.at[pl.ds(kept_at, half)], kept_ref, sem.at[1]),
+        pltpu.make_async_copy(starts_ref, table_ref, sem.at[2]),
+    ]
+    for copy in copies:
+        copy.start()
+    for copy in copies:
+        copy.wait()
+
+
+def prep_kernel(*refs):
+    sources, outs, scratch = refs[:8], refs[8:14], refs[14:]
+    wbd_ref, bias_ref = outs[:2]
+    w_ref, tri_ref, chain_ref, off_ref, sem = scratch
+    targets = [w_ref, tri_ref, chain_ref, off_ref, *outs[2:]]
+    copies = [
+        pltpu.make_async_copy(a, b, sem.at[n])
+        for n, (a, b) in enumerate(zip(sources, targets))
+    ]
+    for copy in copies:
+        copy.start()
     wbd_ref[...] = jnp.zeros_like(wbd_ref)
+    for copy in copies:
+        copy.wait()
     for c in range(PROJ_CHANNELS):
         block = w_ref[c * PROJ_CHANNELS : (c + 1) * PROJ_CHANNELS, :]
         for j in range(PACK):
             row = c * LANES + j * PROJ_CHANNELS
             wbd_ref[row : row + PROJ_CHANNELS, j * CZ : (j + 1) * CZ] = block
     tokens, keys = tri_ref.shape[1:]
-    first = idx[1] * tokens
+    first = lax.axis_index("res") * tokens
     chain = jnp.broadcast_to(chain_ref[...], (tokens, keys))
     rows = lax.broadcasted_iota(jnp.int32, (tokens, keys), 0)
     cols = lax.broadcasted_iota(jnp.int32, (tokens, keys), 1)
@@ -57,22 +87,21 @@
     differ = (chain != own).astype(F32)
     for h in range(H):
         bias_ref[h * tokens : (h + 1) * tokens, :] = (
-            tri_ref[h].astype(F32) + off[h] * differ
-        )
-
-
-def select_kernel(idx, starts, own_ref, recv_ref, *refs):
+            tri_ref[h].astype(F32) + off_ref[h] * differ
+        )
+
+
+def select_kernel(starts, own_ref, recv_ref, *refs):
     outs, chip_ref = refs[:-1], refs[-1]
     chips = len(outs)
-    size, half = outs[0].shape
+    size, _ = outs[0].shape
     width = own_ref.shape[1]
-    res = idx[1]
+    res = lax.axis_index("res")
     core = res % 2
     z = res // 2
     own_at = pl.multiple_of(core * width, LANES)
     recv_at = pl.multiple_of((1 - core) * width, LANES)
-    seq_at = pl.multiple_of(core * half, half)
-    chip_ref[:, pl.ds(own_at, width)] = own_ref[pl.ds(seq_at, half), :]
+    chip_ref[:, pl.ds(own_at, width)] = own_ref[...]
     chip_ref[:, pl.ds(recv_at, width)] = recv_ref[...]
     m = lax.broadcasted_iota(jnp.int32, (size, SPAN), 0)
     lane = lax.broadcasted_iota(jnp.int32, (size, SPAN), 1)
@@ -93,14 +122,14 @@
         ).astype(BF)
 
 
-def outer_kernel(chips, idx, *refs):
+def outer_kernel(chips, *refs):
     mine, theirs = refs[:chips], refs[chips : 2 * chips]
     b_ref, wbd_ref, *outs = refs[2 * chips : -3]
     at_ref, lhs_ref, acc_ref = refs[-3:]
     size, half = mine[0].shape
     groups = len(outs)
-    z = idx[1] // 2
-    core = idx[1] % 2
+    z = lax.axis_index("res") // 2
+    core = lax.axis_index("res") % 2
     mine_at = pl.multiple_of(core * half, LANES)
     theirs_at = pl.multiple_of((1 - core) * half, LANES)
     for k in range(chips):
@@ -126,7 +155,7 @@
     chunks = width // LANES
     acc_ref[...] = acc.reshape(chunks, groups, R_DEV, PACK * CZ)
     for k in range(groups):
-        g = jnp.bitwise_xor(idx[0], k)
+        g = jnp.bitwise_xor(lax.axis_index("depth"), k)
         block = acc_ref[:, g]
         block = jnp.stack(
             [block[:, :, j * CZ : (j + 1) * CZ] for j in range(PACK)], axis=1
@@ -159,12 +188,12 @@
     gate_ref[...] = jax.nn.sigmoid(g.astype(F32))
 
 
-def attend_kernel(chips, idx, *refs):
+def attend_kernel(chips, *refs):
     mine, theirs = refs[:chips], refs[chips : 2 * chips]
     q_ref, gate_ref, w_ref, wo_ref, bias_ref, out_ref, all_ref, gated_ref = refs[2 * chips :]
     tokens = mine[0].shape[1]
-    z = idx[1] // 2
-    core = idx[1] % 2
+    z = lax.axis_index("res") // 2
+    core = lax.axis_index("res") % 2
     for k in range(chips):
         chip = jnp.bitwise_xor(z, k) * 2
         mine_at = pl.multiple_of((chip + core) * tokens, tokens)
@@ -199,6 +228,10 @@
         ).astype(BF)
     out = jnp.dot(gated_ref[...], wo_ref[...], preferred_element_type=F32)
     out_ref[...] = out.astype(BF).reshape(R_DEV, tokens, CZ)
+
+
+def in_hbm(*arrays):
+    return [pltpu.with_memory_space_constraint(a, pltpu.HBM) for a in arrays]
 
 
 def swap(x, axis, mask):
@@ -229,31 +262,58 @@
     tokens = width // PROJ_CHANNELS
     keys = residue_chain.shape[0]
     rows = groups * R_DEV
-    res = lax.axis_index("res")
-    idx = jnp.stack([lax.axis_index("depth"), res]).astype(jnp.int32)
-
-    core = res % 2
-    sent = lax.dynamic_slice_in_dim(alignment_left, (1 - core) * half, half, 0)
+
+    sent, kept, table = call(
+        front_kernel,
+        [
+            pltpu.VMEM((half, width), BF),
+            pltpu.VMEM((half, width), BF),
+            pltpu.SMEM(window_starts.shape, jnp.int32),
+        ],
+        [ANY, ANY],
+        [pltpu.SemaphoreType.DMA((3,))],
+    )(*in_hbm(alignment_left, window_starts))
     recv = swap(sent, "res", 1)
 
-    wbd, bias, right = call(
+    wbd, bias, right, qkvg, wo, shift = call(
         prep_kernel,
         [
             pltpu.VMEM((PROJ_CHANNELS * LANES, PACK * CZ), BF),
             pltpu.VMEM((H * tokens, keys), F32),
             pltpu.VMEM(alignment_right.shape, BF),
-        ],
-        [SMEM, SMEM, VMEM, VMEM, VMEM, VMEM],
+            pltpu.VMEM(query_key_value_gate_weight.shape, BF),
+            pltpu.VMEM(output_weight.shape, BF),
+            pltpu.VMEM((1, CZ), F32),
+        ],
+        [ANY] * 8,
+        [
+            pltpu.VMEM(outer_product_weight.shape, BF),
+            pltpu.VMEM(triangle_pair_bias.shape, BF),
+            pltpu.VMEM((1, keys), jnp.int32),
+            pltpu.SMEM((H,), F32),
+            pltpu.SemaphoreType.DMA((8,)),
+        ],
         flops=1 << 28,
-    )(idx, interchain_offset, outer_product_weight, triangle_pair_bias, residue_chain[None, :], alignment_right)
+    )(
+        *in_hbm(
+            outer_product_weight,
+            triangle_pair_bias,
+            residue_chain[None, :],
+            interchain_offset,
+            alignment_right,
+            query_key_value_gate_weight,
+            output_weight,
+            outer_product_bias[None, :],
+        )
+    )
 
     picked = call(
         select_kernel,
         [pltpu.VMEM((size, half), BF)] * chips,
-        [SMEM, SMEM, VMEM, VMEM],
+        [SMEM, VMEM, VMEM],
         [pltpu.VMEM((half, 2 * width), BF)],
         flops=1 << 28,
-    )(idx, window_starts, alignment_left, recv)
+    )(table, kept, recv)
     piece = picked[0]
     for k in range(1, chips):
         piece = piece + swap(picked[k], "res", 2 * k)
@@ -263,7 +323,7 @@
     partial = call(
         functools.partial(outer_kernel, chips),
         [pltpu.VMEM((R_DEV * tokens, CZ), BF)] * groups,
-        [SMEM] + [VMEM] * (2 * chips + 2),
+        [VMEM] * (2 * chips + 2),
         [
             pltpu.VMEM((groups * WINDOW, seqs), BF),
             pltpu.VMEM((rows * width // LANES, PROJ_CHANNELS * LANES), BF),
@@ -271,7 +331,7 @@
         ],
         flops=1 << 31,
         limit=32,
-    )(idx, *mine, *theirs, right, wbd)
+    )(*mine, *theirs, right, wbd)
     parts = [partial[0]] + [swap(partial[k], "depth", k) for k in range(1, groups)]
 
     pair_strip, normed = call(
@@ -283,7 +343,7 @@
         [VMEM] * (groups + 1),
         [pltpu.VMEM((R_DEV * tokens, CZ), F32)],
         flops=1 << 24,
-    )(*parts, outer_product_bias[None, :])
+    )(*parts, shift)
 
     near = [normed] + [swap(normed, "res", 2 * k) for k in range(1, chips)]
     far = [swap(n, "res", 1) for n in near]
@@ -295,18 +355,18 @@
         ],
         [VMEM] * 2,
         flops=1 << 27,
-    )(normed, query_key_value_gate_weight)
+    )(normed, qkvg)
     (update,) = call(
         functools.partial(attend_kernel, chips),
         [jax.ShapeDtypeStruct((R_DEV, tokens, CZ), BF)],
-        [SMEM] + [VMEM] * (2 * chips + 5),
+        [VMEM] * (2 * chips + 5),
         [
             pltpu.VMEM((R_DEV, keys, CZ), BF),
             pltpu.VMEM((R_DEV * tokens, CZ), BF),
         ],
         flops=1 << 29,
         limit=16,
-    )(idx, *near, *far, queries, gate, query_key_value_gate_weight, output_weight, bias)
+    )(*near, *far, queries, gate, qkvg, wo, bias)
     return (pair_strip, update)
 
 

time: 55.9 us -> 48.7 us (0.87)
  local copies, waits for them, and re-layouts: 6.85 us -> 0 us
    unnamed x20 -> x0, local copies, waits for them, and re-layouts: 5.88 us -> none
    dynamic_slice x1 -> x0, local copies, waits for them, and re-layouts: 0.97 us -> none  [body(): sent = lax.dynamic_slice_in_dim(alignment_left, (1 - core) * half, half, 0)]
    pallas_call x1 -> x2, Pallas kernels: 0.98 us -> 1.5 us  [the longest x1 1.08 us: body(): call(front_kernel, [pltpu.VMEM((half, width), BF), pltpu.VMEM((half, widt...]
  transfers between devices with their start and end apart: 21 -> 21, of which waited for: 12 -> 12; matrix products, arithmetic and copies ran while one was open for 0% -> 0% of each run, Pallas kernels for 2% -> 3%
where the time goes in v3:
time: 48.7 us; the launch traced here: 48.5 us
  starting transfers between devices  19.6 us (40%)
  waiting for transfers between devices  19.3 us (40%)
  Pallas kernels  8.92 us (18%)
  between operations  0.74 us (2%)
    ppermute x21, starting transfers between devices, swap(): return lax.ppermute(x, axis, [(i, i ^ mask) for i in range(n)])  19.6 us
    ppermute x21, waiting for transfers between devices, swap(): return lax.ppermute(x, axis, [(i, i ^ mask) for i in range(n)])  19.3 us
    pallas_call x1, Pallas kernels, body(): call(functools.partial(attend_kernel, chips), [jax.ShapeDtypeStruct((R_DE...  3.15 us
    pallas_call x1, Pallas kernels, body(): call(functools.partial(outer_kernel, chips), [pltpu.VMEM((R_DEV * tokens,...  1.94 us
    pallas_call x1, Pallas kernels, body(): call(prep_kernel, [pltpu.VMEM((PROJ_CHANNELS * LANES, PACK * CZ), BF), pl...  1.46 us
    pallas_call x1, Pallas kernels, body(): call(front_kernel, [pltpu.VMEM((half, width), BF), pltpu.VMEM((half, widt...  1.08 us
  transfers between devices with their start and end apart: 21, of which 12 were waited for; matrix products, arithmetic and copies ran while one was open for 0% of the time, Pallas kernels for 3%

profile of v3, /device:TPU:0, one launch (start us, length us, event | category | flops | bytes accessed | tf_op | source)
XLA Modules:
  0.0 48.5 jit_solution(11087558187984252418)
XLA Ops:
  0.6 1.1 %shard_map.113 = (bf16[128,1024]{1,0:T(8,128)(2,1)S(1)}, bf16[128,1024]{1,0:T(8,128)(2,1)S(1)}, s32[4]{0:T(128)S(4)}) custom-call(bf16[256,1024]{1,0:T(8,128)(2,1)} %left_ref.1, s32[4]{0:T(128)} %starts_ref.1), custom_call_target="tpu_custom_call" | custom-call | bytes 1048576 | tf_op jit(solution)/shard_map/pallas_call | solution.py:266
  1.7 0.6 %collective-permute-start = (bf16[128,1024]{1,0:T(8,128)(2,1)S(1)}, bf16[128,1024]{1,0:T(8,128)(2,1)S(1)}, u32[]{:S(2)}, u32[]{:S(2)}) collective-permute-start(bf16[128,1024]{1,0:T(8,128)(2,1)S(1)} %get-tuple-element.25), channel_id=1, source_target_pairs={{0,1},{1,0},{2,3},{3,2},{4,5},{5,4},{6,7},{7,6},{8,9},{9,8},{10,11... | collective-permute-start | bytes 786440 | tf_op jit(solution)/shard_map/ppermute | solution.py:239
  2.3 1.2 %collective-permute-done.recv_ref = bf16[128,1024]{1,0:T(8,128)(2,1)S(1)} collective-permute-done((bf16[128,1024]{1,0:T(8,128)(2,1)S(1)}, bf16[128,1024]{1,0:T(8,128)(2,1)S(1)}, u32[]{:S(2)}, u32[]{:S(2)}) %collective-permute-start) | collective-permute-done | bytes 262176 | tf_op jit(solution)/shard_map/ppermute | solution.py:239
  3.9 3.0 %collective-permute-start.1 = (bf16[256,128]{1,0:T(8,128)(2,1)S(1)}, bf16[256,128]{1,0:T(8,128)(2,1)S(1)}, u32[]{:S(2)}, u32[]{:S(2)}) collective-permute-start(bf16[256,128]{1,0:T(8,128)(2,1)S(1)} %get-tuple-element.27), channel_id=1, source_target_pairs={{0,2},{1,3},{2,0},{3,1},{4,6},{5,7},{6,4},{7,5},{8,10},{9,11},{10,... | collective-permute-start | bytes 196616 | tf_op jit(solution)/shard_map/ppermute | solution.py:239
  6.9 2.6 %collective-permute-start.2 = (bf16[256,128]{1,0:T(8,128)(2,1)S(1)}, bf16[256,128]{1,0:T(8,128)(2,1)S(1)}, u32[]{:S(2)}, u32[]{:S(2)}) collective-permute-start(bf16[256,128]{1,0:T(8,128)(2,1)S(1)} %get-tuple-element.28), channel_id=1, source_target_pairs={{0,4},{1,5},{2,6},{3,7},{4,0},{5,1},{6,2},{7,3},{8,12},{9,13},{10,... | collective-permute-start | bytes 196616 | tf_op jit(solution)/shard_map/ppermute | solution.py:239
  9.5 4.9 %collective-permute-done.2 = bf16[256,128]{1,0:T(8,128)(2,1)S(1)} collective-permute-done((bf16[256,128]{1,0:T(8,128)(2,1)S(1)}, bf16[256,128]{1,0:T(8,128)(2,1)S(1)}, u32[]{:S(2)}, u32[]{:S(2)}) %collective-permute-start.2) | collective-permute-done | bytes 65568 | tf_op jit(solution)/shard_map/ppermute | solution.py:239
  14.4 1.2 %collective-permute-done.3 = bf16[256,128]{1,0:T(8,128)(2,1)S(1)} collective-permute-done((bf16[256,128]{1,0:T(8,128)(2,1)S(1)}, bf16[256,128]{1,0:T(8,128)(2,1)S(1)}, u32[]{:S(2)}, u32[]{:S(2)}) %collective-permute-start.3) | collective-permute-done | bytes 65568 | tf_op jit(solution)/shard_map/ppermute | solution.py:239
  15.6 2.1 %collective-permute-start.6 = (bf16[256,128]{1,0:T(8,128)(2,1)S(1)}, bf16[256,128]{1,0:T(8,128)(2,1)S(1)}, u32[]{:S(2)}, u32[]{:S(2)}) collective-permute-start(bf16[256,128]{1,0:T(8,128)(2,1)S(1)} %add_add_fusion.refs_0_), channel_id=1, source_target_pairs={{0,6},{1,7},{2,4},{3,5},{4,2},{5,3},{6,0},{7,1},{8,14},{9,15},{10,... | collective-permute-start | bytes 196616 | tf_op jit(solution)/shard_map/ppermute | solution.py:239
  18.0 2.1 %collective-permute-start.4 = (bf16[256,128]{1,0:T(8,128)(2,1)S(1)}, bf16[256,128]{1,0:T(8,128)(2,1)S(1)}, u32[]{:S(2)}, u32[]{:S(2)}) collective-permute-start(bf16[256,128]{1,0:T(8,128)(2,1)S(1)} %add_add_fusion.refs_0_), channel_id=1, source_target_pairs={{0,2},{1,3},{2,0},{3,1},{4,6},{5,7},{6,4},{7,5},{8,10},{9,11},{10,... | collective-permute-start | bytes 196616 | tf_op jit(solution)/shard_map/ppermute | solution.py:239
  20.1 1.8 %collective-permute-done.6.refs_3_ = bf16[256,128]{1,0:T(8,128)(2,1)S(1)} collective-permute-done((bf16[256,128]{1,0:T(8,128)(2,1)S(1)}, bf16[256,128]{1,0:T(8,128)(2,1)S(1)}, u32[]{:S(2)}, u32[]{:S(2)}) %collective-permute-start.6) | collective-permute-done | bytes 65568 | tf_op jit(solution)/shard_map/ppermute | solution.py:239
  21.9 1.5 %collective-permute-done.5.refs_2_ = bf16[256,128]{1,0:T(8,128)(2,1)S(1)} collective-permute-done((bf16[256,128]{1,0:T(8,128)(2,1)S(1)}, bf16[256,128]{1,0:T(8,128)(2,1)S(1)}, u32[]{:S(2)}, u32[]{:S(2)}) %collective-permute-start.5) | collective-permute-done | bytes 65568 | tf_op jit(solution)/shard_map/ppermute | solution.py:239
  24.0 1.5 %shard_map.115 = (bf16[4096,512]{1,0:T(8,128)(2,1)S(1)}, f32[128,256]{1,0:T(8,128)S(1)}, bf16[256,1024]{1,0:T(8,128)(2,1)S(1)}, bf16[128,512]{1,0:T(8,128)(2,1)S...) custom-call(bf16[1024,128]{1,0:T(8,128)(2,1)} %refs_0_.1, bf16[4,32,256]{2,1,0:T(8,128)(2,1)} %refs_1_.1, ...), custom_call_target="tpu_custom_call" | custom-call | flops 268435456 | bytes 1048576 | tf_op jit(solution)/shard_map/pallas_call | solution.py:278
  25.5 1.9 %shard_map.116 = (bf16[256,128]{1,0:T(8,128)(2,1)S(1)}, bf16[256,128]{1,0:T(8,128)(2,1)S(1)}, bf16[256,128]{1,0:T(8,128)(2,1)S(1)}, bf16[256,128]{1,0:T(8,128)(2,1)S(1)}) custom-call(bf16[256,128]{1,0:T(8,128)(2,1)S(1)} %add_add_fusion.refs_0_, bf16[256,128]{1,0:T(8,128)(2,1)S(1)} %collective-permute-done.4.refs_1_, ...), custom_call_target="tpu_custom_call" | custom-call | flops 2147483648 | bytes 1048576 | tf_op jit(solution)/shard_map/pallas_call | solution.py:323
  27.4 1.6 %collective-permute-start.11 = (bf16[256,128]{1,0:T(8,128)(2,1)S(1)}, bf16[256,128]{1,0:T(8,128)(2,1)S(1)}, u32[]{:S(2)}, u32[]{:S(2)}) collective-permute-start(bf16[256,128]{1,0:T(8,128)(2,1)S(1)} %get-tuple-element.33), channel_id=1, source_target_pairs={{0,8},{8,0},{16,24},{24,16},{1,9},{9,1},{17,25},{25,17},{2,10},{10... | collective-permute-start | bytes 196616 | tf_op jit(solution)/shard_map/ppermute | solution.py:239
  29.0 1.5 %collective-permute-start.12 = (bf16[256,128]{1,0:T(8,128)(2,1)S(1)}, bf16[256,128]{1,0:T(8,128)(2,1)S(1)}, u32[]{:S(2)}, u32[]{:S(2)}) collective-permute-start(bf16[256,128]{1,0:T(8,128)(2,1)S(1)} %get-tuple-element.34), channel_id=1, source_target_pairs={{0,16},{8,24},{16,0},{24,8},{1,17},{9,25},{17,1},{25,9},{2,18},{10... | collective-permute-start | bytes 196616 | tf_op jit(solution)/shard_map/ppermute | solution.py:239
  31.0 0.8 %collective-permute-done.11.refs_1_ = bf16[256,128]{1,0:T(8,128)(2,1)S(1)} collective-permute-done((bf16[256,128]{1,0:T(8,128)(2,1)S(1)}, bf16[256,128]{1,0:T(8,128)(2,1)S(1)}, u32[]{:S(2)}, u32[]{:S(2)}) %collective-permute-start.11) | collective-permute-done | bytes 65568 | tf_op jit(solution)/shard_map/ppermute | solution.py:239
  31.7 1.5 %collective-permute-done.12.refs_2_ = bf16[256,128]{1,0:T(8,128)(2,1)S(1)} collective-permute-done((bf16[256,128]{1,0:T(8,128)(2,1)S(1)}, bf16[256,128]{1,0:T(8,128)(2,1)S(1)}, u32[]{:S(2)}, u32[]{:S(2)}) %collective-permute-start.12) | collective-permute-done | bytes 65568 | tf_op jit(solution)/shard_map/ppermute | solution.py:239
  33.2 2.4 %collective-permute-done.13.refs_3_ = bf16[256,128]{1,0:T(8,128)(2,1)S(1)} collective-permute-done((bf16[256,128]{1,0:T(8,128)(2,1)S(1)}, bf16[256,128]{1,0:T(8,128)(2,1)S(1)}, u32[]{:S(2)}, u32[]{:S(2)}) %collective-permute-start.13) | collective-permute-done | bytes 65568 | tf_op jit(solution)/shard_map/ppermute | solution.py:239
  35.7 0.7 %shard_map.117 = (bf16[8,32,128]{2,1,0:T(8,128)(2,1)}, bf16[8,32,128]{2,1,0:T(8,128)(2,1)S(1)}) custom-call(bf16[256,128]{1,0:T(8,128)(2,1)S(1)} %get-tuple-element.32.refs_0_, bf16[256,128]{1,0:T(8,128)(2,1)S(1)} %collective-permute-done.11.refs_1_, bf16[256,128]{1,0:T(8,128)(2,1)S(1)} %collective-permute-done.12.refs_2_, ...), custom_call_target="tpu_custom_call" | custom-call | flops 16777216 | bytes 1048576 | tf_op jit(solution)/shard_map/pallas_call | solution.py:337
  36.4 1.9 %collective-permute-start.16 = (bf16[8,32,128]{2,1,0:T(8,128)(2,1)S(1)}, bf16[8,32,128]{2,1,0:T(8,128)(2,1)S(1)}, u32[]{:S(2)}, u32[]{:S(2)}) collective-permute-start(bf16[8,32,128]{2,1,0:T(8,128)(2,1)S(1)} %get-tuple-element.38.normed_ref.refs_0_), channel_id=1, source_target_pairs={{0,6},{1,7},{2,4},{3,5},{4,2},{5,3},{6,0},{7,1},{8,14},{9,15},{10,... | collective-permute-start | bytes 196616 | tf_op jit(solution)/shard_map/ppermute | solution.py:239
  38.3 2.4 %collective-permute-start.14 = (bf16[8,32,128]{2,1,0:T(8,128)(2,1)S(1)}, bf16[8,32,128]{2,1,0:T(8,128)(2,1)S(1)}, u32[]{:S(2)}, u32[]{:S(2)}) collective-permute-start(bf16[8,32,128]{2,1,0:T(8,128)(2,1)S(1)} %get-tuple-element.38.normed_ref.refs_0_), channel_id=1, source_target_pairs={{0,2},{1,3},{2,0},{3,1},{4,6},{5,7},{6,4},{7,5},{8,10},{9,11},{10,... | collective-permute-start | bytes 196616 | tf_op jit(solution)/shard_map/ppermute | solution.py:239
  40.8 1.8 %collective-permute-done.16.refs_3_ = bf16[8,32,128]{2,1,0:T(8,128)(2,1)S(1)} collective-permute-done((bf16[8,32,128]{2,1,0:T(8,128)(2,1)S(1)}, bf16[8,32,128]{2,1,0:T(8,128)(2,1)S(1)}, u32[]{:S(2)}, u32[]{:S(2)}) %collective-permute-start.16) | collective-permute-done | bytes 65568 | tf_op jit(solution)/shard_map/ppermute | solution.py:239
  42.5 1.4 %collective-permute-done.15.refs_2_ = bf16[8,32,128]{2,1,0:T(8,128)(2,1)S(1)} collective-permute-done((bf16[8,32,128]{2,1,0:T(8,128)(2,1)S(1)}, bf16[8,32,128]{2,1,0:T(8,128)(2,1)S(1)}, u32[]{:S(2)}, u32[]{:S(2)}) %collective-permute-start.15) | collective-permute-done | bytes 65568 | tf_op jit(solution)/shard_map/ppermute | solution.py:239
  45.4 3.1 %shard_map.119 = bf16[8,32,128]{2,1,0:T(8,128)(2,1)} custom-call(bf16[8,32,128]{2,1,0:T(8,128)(2,1)S(1)} %get-tuple-element.38.normed_ref.refs_0_, bf16[8,32,128]{2,1,0:T(8,128)(2,1)S(1)} %collective-permute-done.14.refs_1_, bf16[8,32,128]{2,1,0:T(8,128)(2,1)S(1)} %collective-permute-done.15.refs_2_, ...), custom_call_target="tpu_custom_call" | custom-call | flops 536870912 | bytes 1048576 | tf_op jit(solution)/shard_map/pallas_call | solution.py:359
  (26 shorter events, 3.1 us)
Async XLA Ops:
  1.7 1.7 %collective-permute-start = (bf16[128,1024]{1,0:T(8,128)(2,1)S(1)}, bf16[128,1024]{1,0:T(8,128)(2,1)S(1)}, u32[]{:S(2)}, u32[]{:S(2)}) collective-permute-start(bf16[128,1024]{1,0:T(8,128)(2,1)S(1)} %get-tuple-element.25), channel_id=1, source_target_pairs={{0,1},{1,0},{2,3},{3,2},{4,5},{5,4},{6,7},{7,6},{8,9},{9,8},{10,11... | collective-permute-start | bytes 786440 | tf_op jit(solution)/shard_map/ppermute | solution.py:239
  3.9 5.6 %collective-permute-start.1 = (bf16[256,128]{1,0:T(8,128)(2,1)S(1)}, bf16[256,128]{1,0:T(8,128)(2,1)S(1)}, u32[]{:S(2)}, u32[]{:S(2)}) collective-permute-start(bf16[256,128]{1,0:T(8,128)(2,1)S(1)} %get-tuple-element.27), channel_id=1, source_target_pairs={{0,2},{1,3},{2,0},{3,1},{4,6},{5,7},{6,4},{7,5},{8,10},{9,11},{10,... | collective-permute-start | bytes 196616 | tf_op jit(solution)/shard_map/ppermute | solution.py:239
  6.9 7.5 %collective-permute-start.2 = (bf16[256,128]{1,0:T(8,128)(2,1)S(1)}, bf16[256,128]{1,0:T(8,128)(2,1)S(1)}, u32[]{:S(2)}, u32[]{:S(2)}) collective-permute-start(bf16[256,128]{1,0:T(8,128)(2,1)S(1)} %get-tuple-element.28), channel_id=1, source_target_pairs={{0,4},{1,5},{2,6},{3,7},{4,0},{5,1},{6,2},{7,3},{8,12},{9,13},{10,... | collective-permute-start | bytes 196616 | tf_op jit(solution)/shard_map/ppermute | solution.py:239
  9.5 6.2 %collective-permute-start.3 = (bf16[256,128]{1,0:T(8,128)(2,1)S(1)}, bf16[256,128]{1,0:T(8,128)(2,1)S(1)}, u32[]{:S(2)}, u32[]{:S(2)}) collective-permute-start(bf16[256,128]{1,0:T(8,128)(2,1)S(1)} %get-tuple-element.29), channel_id=1, source_target_pairs={{0,6},{1,7},{2,4},{3,5},{4,2},{5,3},{6,0},{7,1},{8,14},{9,15},{10,... | collective-permute-start | bytes 196616 | tf_op jit(solution)/shard_map/ppermute | solution.py:239
  15.6 6.3 %collective-permute-start.6 = (bf16[256,128]{1,0:T(8,128)(2,1)S(1)}, bf16[256,128]{1,0:T(8,128)(2,1)S(1)}, u32[]{:S(2)}, u32[]{:S(2)}) collective-permute-start(bf16[256,128]{1,0:T(8,128)(2,1)S(1)} %add_add_fusion.refs_0_), channel_id=1, source_target_pairs={{0,6},{1,7},{2,4},{3,5},{4,2},{5,3},{6,0},{7,1},{8,14},{9,15},{10,... | collective-permute-start | bytes 196616 | tf_op jit(solution)/shard_map/ppermute | solution.py:239
  17.7 5.7 %collective-permute-start.5 = (bf16[256,128]{1,0:T(8,128)(2,1)S(1)}, bf16[256,128]{1,0:T(8,128)(2,1)S(1)}, u32[]{:S(2)}, u32[]{:S(2)}) collective-permute-start(bf16[256,128]{1,0:T(8,128)(2,1)S(1)} %add_add_fusion.refs_0_), channel_id=1, source_target_pairs={{0,4},{1,5},{2,6},{3,7},{4,0},{5,1},{6,2},{7,3},{8,12},{9,13},{10,... | collective-permute-start | bytes 196616 | tf_op jit(solution)/shard_map/ppermute | solution.py:239
  18.0 5.5 %collective-permute-start.4 = (bf16[256,128]{1,0:T(8,128)(2,1)S(1)}, bf16[256,128]{1,0:T(8,128)(2,1)S(1)}, u32[]{:S(2)}, u32[]{:S(2)}) collective-permute-start(bf16[256,128]{1,0:T(8,128)(2,1)S(1)} %add_add_fusion.refs_0_), channel_id=1, source_target_pairs={{0,2},{1,3},{2,0},{3,1},{4,6},{5,7},{6,4},{7,5},{8,10},{9,11},{10,... | collective-permute-start | bytes 196616 | tf_op jit(solution)/shard_map/ppermute | solution.py:239
  20.1 5.3 %collective-permute-start.7 = (bf16[256,128]{1,0:T(8,128)(2,1)S(1)}, bf16[256,128]{1,0:T(8,128)(2,1)S(1)}, u32[]{:S(2)}, u32[]{:S(2)}) collective-permute-start(bf16[256,128]{1,0:T(8,128)(2,1)S(1)} %add_add_fusion.refs_0_), channel_id=1, source_target_pairs={{0,1},{1,0},{2,3},{3,2},{4,5},{5,4},{6,7},{7,6},{8,9},{9,8},{10,11... | collective-permute-start | bytes 196616 | tf_op jit(solution)/shard_map/ppermute | solution.py:239
  21.9 3.5 %collective-permute-start.10 = (bf16[256,128]{1,0:T(8,128)(2,1)S(1)}, bf16[256,128]{1,0:T(8,128)(2,1)S(1)}, u32[]{:S(2)}, u32[]{:S(2)}) collective-permute-start(bf16[256,128]{1,0:T(8,128)(2,1)S(1)} %collective-permute-done.6.refs_3_), channel_id=1, source_target_pairs={{0,1},{1,0},{2,3},{3,2},{4,5},{5,4},{6,7},{7,6},{8,9},{9,8},{10,11... | collective-permute-start | bytes 196616 | tf_op jit(solution)/shard_map/ppermute | solution.py:239
  23.4 2.0 %collective-permute-start.9 = (bf16[256,128]{1,0:T(8,128)(2,1)S(1)}, bf16[256,128]{1,0:T(8,128)(2,1)S(1)}, u32[]{:S(2)}, u32[]{:S(2)}) collective-permute-start(bf16[256,128]{1,0:T(8,128)(2,1)S(1)} %collective-permute-done.5.refs_2_), channel_id=1, source_target_pairs={{0,1},{1,0},{2,3},{3,2},{4,5},{5,4},{6,7},{7,6},{8,9},{9,8},{10,11... | collective-permute-start | bytes 196616 | tf_op jit(solution)/shard_map/ppermute | solution.py:239
  23.4 2.0 %collective-permute-start.8 = (bf16[256,128]{1,0:T(8,128)(2,1)S(1)}, bf16[256,128]{1,0:T(8,128)(2,1)S(1)}, u32[]{:S(2)}, u32[]{:S(2)}) collective-permute-start(bf16[256,128]{1,0:T(8,128)(2,1)S(1)} %collective-permute-done.4.refs_1_), channel_id=1, source_target_pairs={{0,1},{1,0},{2,3},{3,2},{4,5},{5,4},{6,7},{7,6},{8,9},{9,8},{10,11... | collective-permute-start | bytes 196616 | tf_op jit(solution)/shard_map/ppermute | solution.py:239
  27.4 4.3 %collective-permute-start.11 = (bf16[256,128]{1,0:T(8,128)(2,1)S(1)}, bf16[256,128]{1,0:T(8,128)(2,1)S(1)}, u32[]{:S(2)}, u32[]{:S(2)}) collective-permute-start(bf16[256,128]{1,0:T(8,128)(2,1)S(1)} %get-tuple-element.33), channel_id=1, source_target_pairs={{0,8},{8,0},{16,24},{24,16},{1,9},{9,1},{17,25},{25,17},{2,10},{10... | collective-permute-start | bytes 196616 | tf_op jit(solution)/shard_map/ppermute | solution.py:239
  29.0 4.3 %collective-permute-start.12 = (bf16[256,128]{1,0:T(8,128)(2,1)S(1)}, bf16[256,128]{1,0:T(8,128)(2,1)S(1)}, u32[]{:S(2)}, u32[]{:S(2)}) collective-permute-start(bf16[256,128]{1,0:T(8,128)(2,1)S(1)} %get-tuple-element.34), channel_id=1, source_target_pairs={{0,16},{8,24},{16,0},{24,8},{1,17},{9,25},{17,1},{25,9},{2,18},{10... | collective-permute-start | bytes 196616 | tf_op jit(solution)/shard_map/ppermute | solution.py:239
  30.5 5.2 %collective-permute-start.13 = (bf16[256,128]{1,0:T(8,128)(2,1)S(1)}, bf16[256,128]{1,0:T(8,128)(2,1)S(1)}, u32[]{:S(2)}, u32[]{:S(2)}) collective-permute-start(bf16[256,128]{1,0:T(8,128)(2,1)S(1)} %get-tuple-element.35), channel_id=1, source_target_pairs={{0,24},{8,16},{16,8},{24,0},{1,25},{9,17},{17,9},{25,1},{2,26},{10... | collective-permute-start | bytes 196616 | tf_op jit(solution)/shard_map/ppermute | solution.py:239
  36.4 6.2 %collective-permute-start.16 = (bf16[8,32,128]{2,1,0:T(8,128)(2,1)S(1)}, bf16[8,32,128]{2,1,0:T(8,128)(2,1)S(1)}, u32[]{:S(2)}, u32[]{:S(2)}) collective-permute-start(bf16[8,32,128]{2,1,0:T(8,128)(2,1)S(1)} %get-tuple-element.38.normed_ref.refs_0_), channel_id=1, source_target_pairs={{0,6},{1,7},{2,4},{3,5},{4,2},{5,3},{6,0},{7,1},{8,14},{9,15},{10,... | collective-permute-start | bytes 196616 | tf_op jit(solution)/shard_map/ppermute | solution.py:239
  38.3 5.7 %collective-permute-start.15 = (bf16[8,32,128]{2,1,0:T(8,128)(2,1)S(1)}, bf16[8,32,128]{2,1,0:T(8,128)(2,1)S(1)}, u32[]{:S(2)}, u32[]{:S(2)}) collective-permute-start(bf16[8,32,128]{2,1,0:T(8,128)(2,1)S(1)} %get-tuple-element.38.normed_ref.refs_0_), channel_id=1, source_target_pairs={{0,4},{1,5},{2,6},{3,7},{4,0},{5,1},{6,2},{7,3},{8,12},{9,13},{10,... | collective-permute-start | bytes 196616 | tf_op jit(solution)/shard_map/ppermute | solution.py:239
  38.3 5.7 %collective-permute-start.14 = (bf16[8,32,128]{2,1,0:T(8,128)(2,1)S(1)}, bf16[8,32,128]{2,1,0:T(8,128)(2,1)S(1)}, u32[]{:S(2)}, u32[]{:S(2)}) collective-permute-start(bf16[8,32,128]{2,1,0:T(8,128)(2,1)S(1)} %get-tuple-element.38.normed_ref.refs_0_), channel_id=1, source_target_pairs={{0,2},{1,3},{2,0},{3,1},{4,6},{5,7},{6,4},{7,5},{8,10},{9,11},{10,... | collective-permute-start | bytes 196616 | tf_op jit(solution)/shard_map/ppermute | solution.py:239
  40.7 3.9 %collective-permute-start.17 = (bf16[8,32,128]{2,1,0:T(8,128)(2,1)S(1)}, bf16[8,32,128]{2,1,0:T(8,128)(2,1)S(1)}, u32[]{:S(2)}, u32[]{:S(2)}) collective-permute-start(bf16[8,32,128]{2,1,0:T(8,128)(2,1)S(1)} %get-tuple-element.38.normed_ref.refs_0_), channel_id=1, source_target_pairs={{0,1},{1,0},{2,3},{3,2},{4,5},{5,4},{6,7},{7,6},{8,9},{9,8},{10,11... | collective-permute-start | bytes 196616 | tf_op jit(solution)/shard_map/ppermute | solution.py:239
  42.5 2.1 %collective-permute-start.20 = (bf16[8,32,128]{2,1,0:T(8,128)(2,1)S(1)}, bf16[8,32,128]{2,1,0:T(8,128)(2,1)S(1)}, u32[]{:S(2)}, u32[]{:S(2)}) collective-permute-start(bf16[8,32,128]{2,1,0:T(8,128)(2,1)S(1)} %collective-permute-done.16.refs_3_), channel_id=1, source_target_pairs={{0,1},{1,0},{2,3},{3,2},{4,5},{5,4},{6,7},{7,6},{8,9},{9,8},{10,11... | collective-permute-start | bytes 196616 | tf_op jit(solution)/shard_map/ppermute | solution.py:239
  44.0 1.3 %collective-permute-start.19 = (bf16[8,32,128]{2,1,0:T(8,128)(2,1)S(1)}, bf16[8,32,128]{2,1,0:T(8,128)(2,1)S(1)}, u32[]{:S(2)}, u32[]{:S(2)}) collective-permute-start(bf16[8,32,128]{2,1,0:T(8,128)(2,1)S(1)} %collective-permute-done.15.refs_2_), channel_id=1, source_target_pairs={{0,1},{1,0},{2,3},{3,2},{4,5},{5,4},{6,7},{7,6},{8,9},{9,8},{10,11... | collective-permute-start | bytes 196616 | tf_op jit(solution)/shard_map/ppermute | solution.py:239
  44.0 1.4 %collective-permute-start.18 = (bf16[8,32,128]{2,1,0:T(8,128)(2,1)S(1)}, bf16[8,32,128]{2,1,0:T(8,128)(2,1)S(1)}, u32[]{:S(2)}, u32[]{:S(2)}) collective-permute-start(bf16[8,32,128]{2,1,0:T(8,128)(2,1)S(1)} %collective-permute-done.14.refs_1_), channel_id=1, source_target_pairs={{0,1},{1,0},{2,3},{3,2},{4,5},{5,4},{6,7},{7,6},{8,9},{9,8},{10,11... | collective-permute-start | bytes 196616 | tf_op jit(solution)/shard_map/ppermute | solution.py:239

commit v4 on v3

--- a/solution.py
+++ b/solution.py
@@ -1,4 +1,5 @@
 import functools
+import itertools
 
 import jax
 import jax.numpy as jnp
@@ -43,19 +44,56 @@
     )
 
 
-def front_kernel(left_ref, starts_ref, sent_ref, kept_ref, table_ref, sem):
+def front_kernel(adaptive, chip_tokens, left_ref, starts_ref, sent_ref, kept_ref, table_ref, need_ref, raw_ref, sem):
     half = sent_ref.shape[0]
     core = lax.axis_index("res") % 2
     sent_at = pl.multiple_of((1 - core) * half, half)
     kept_at = pl.multiple_of(core * half, half)
     copies = [
-        pltpu.make_async_copy(left_ref.at[pl.ds(sent_at, half)], sent_ref, sem.at[0]),
-        pltpu.make_async_copy(left_ref.at[pl.ds(kept_at, half)], kept_ref, sem.at[1]),
-        pltpu.make_async_copy(starts_ref, table_ref, sem.at[2]),
+        pltpu.make_async_copy(starts_ref, raw_ref, sem.at[0]),
+        pltpu.make_async_copy(left_ref.at[pl.ds(sent_at, half)], sent_ref, sem.at[1]),
+        pltpu.make_async_copy(left_ref.at[pl.ds(kept_at, half)], kept_ref, sem.at[2]),
     ]
     for copy in copies:
         copy.start()
-    for copy in copies:
+    copies[0].wait()
+    groups = starts_ref.shape[0]
+    need_ref[0] = 0
+    for g in range(groups):
+        table_ref[g] = g
+    if adaptive:
+        starts = [raw_ref[g] for g in range(groups)]
+        reach = []
+        for start in starts:
+            low = start // chip_tokens
+            high = (start + (R_DEV - 1)) // chip_tokens
+            reach.append(
+                [
+                    jnp.left_shift(1, jnp.bitwise_xor(low, h))
+                    | jnp.left_shift(1, jnp.bitwise_xor(high, h))
+                    for h in range(groups)
+                ]
+            )
+        best = cost = homes = None
+        for order in itertools.permutations(range(groups)):
+            mask = functools.reduce(
+                jnp.bitwise_or, [reach[w][h] for h, w in enumerate(order)]
+            )
+            price = sum((jnp.right_shift(mask, k) & 1) * (4 if k == 1 else 5) for k in range(1, groups))
+            packed = jnp.int32(sum(w << (4 * h) for h, w in enumerate(order)))
+            if best is None:
+                best, cost, homes = mask, price, packed
+            else:
+                better = price < cost
+                best = jnp.where(better, mask, best)
+                homes = jnp.where(better, packed, homes)
+                cost = jnp.where(better, price, cost)
+        need_ref[0] = jnp.right_shift(best, 1)
+        for h in range(groups):
+            table_ref[h] = jnp.right_shift(homes, 4 * h) & 15
+    for g in range(groups):
+        table_ref[groups + g] = raw_ref[table_ref[g]]
+    for copy in copies[1:]:
         copy.wait()
 
 
@@ -91,7 +129,7 @@
         )
 
 
-def select_kernel(starts, own_ref, recv_ref, *refs):
+def select_kernel(table, own_ref, recv_ref, *refs):
     outs, chip_ref = refs[:-1], refs[-1]
     chips = len(outs)
     size, _ = outs[0].shape
@@ -106,11 +144,12 @@
     m = lax.broadcasted_iota(jnp.int32, (size, SPAN), 0)
     lane = lax.broadcasted_iota(jnp.int32, (size, SPAN), 1)
     delta = lane - (m % R_DEV) * PROJ_CHANNELS - m // R_DEV
+    split = WINDOW // size
+    groups = chips // split
     for k in range(chips):
-        g = jnp.bitwise_xor(z, k)
-        split = WINDOW // size
-        first = g % split * (size // R_DEV)
-        start = starts[g // split] * PROJ_CHANNELS - z * (2 * width)
+        at = jnp.bitwise_xor(z, k)
+        first = at % split * (size // R_DEV)
+        start = table[groups + at // split] * PROJ_CHANNELS - z * (2 * width)
         base = jnp.clip(start, 0, 2 * width - SPAN) // LANES * LANES
         base = pl.multiple_of(base, LANES)
         pick = (delta == start + first - base).astype(F32).astype(BF)
@@ -122,7 +161,7 @@
         ).astype(BF)
 
 
-def outer_kernel(chips, *refs):
+def outer_kernel(chips, table, *refs):
     mine, theirs = refs[:chips], refs[chips : 2 * chips]
     b_ref, wbd_ref, *outs = refs[2 * chips : -3]
     at_ref, lhs_ref, acc_ref = refs[-3:]
@@ -133,7 +172,9 @@
     mine_at = pl.multiple_of(core * half, LANES)
     theirs_at = pl.multiple_of((1 - core) * half, LANES)
     for k in range(chips):
-        row = pl.multiple_of(jnp.bitwise_xor(z, k) * size, size)
+        at = jnp.bitwise_xor(z, k)
+        split = WINDOW // size
+        row = pl.multiple_of(table[at // split] * WINDOW + at % split * size, size)
         at_ref[pl.ds(row, size), pl.ds(mine_at, half)] = mine[k][...]
         at_ref[pl.ds(row, size), pl.ds(theirs_at, half)] = theirs[k][...]
     width = b_ref.shape[1]
@@ -263,15 +304,17 @@
     keys = residue_chain.shape[0]
     rows = groups * R_DEV
 
-    sent, kept, table = call(
-        front_kernel,
+    adaptive = chips == groups == 4
+    sent, kept, table, need = call(
+        functools.partial(front_kernel, adaptive, 2 * tokens),
         [
             pltpu.VMEM((half, width), BF),
             pltpu.VMEM((half, width), BF),
-            pltpu.SMEM(window_starts.shape, jnp.int32),
+            pltpu.SMEM((2 * groups,), jnp.int32),
+            pltpu.SMEM((1,), jnp.int32),
         ],
         [ANY, ANY],
-        [pltpu.SemaphoreType.DMA((3,))],
+        [pltpu.SMEM(window_starts.shape, jnp.int32), pltpu.SemaphoreType.DMA((3,))],
     )(*in_hbm(alignment_left, window_starts))
     recv = swap(sent, "res", 1)
 
@@ -314,16 +357,30 @@
         [pltpu.VMEM((half, 2 * width), BF)],
         flops=1 << 28,
     )(table, kept, recv)
-    piece = picked[0]
-    for k in range(1, chips):
-        piece = piece + swap(picked[k], "res", 2 * k)
+
+    def collect(wanted, *picked):
+        return functools.reduce(
+            jnp.add,
+            [picked[0]] + [swap(picked[k], "res", 2 * k) for k in wanted],
+        )
+
+    every = range(1, chips)
+    if adaptive:
+        subsets = [
+            [k for k in every if bits >> (k - 1) & 1] for bits in range(1 << len(every))
+        ]
+        piece = lax.switch(
+            need[0], [functools.partial(collect, wanted) for wanted in subsets], *picked
+        )
+    else:
+        piece = collect(every, *picked)
     mine = [piece] + [swap(piece, "res", 2 * k) for k in range(1, chips)]
     theirs = [swap(m, "res", 1) for m in mine]
 
     partial = call(
         functools.partial(outer_kernel, chips),
         [pltpu.VMEM((R_DEV * tokens, CZ), BF)] * groups,
-        [VMEM] * (2 * chips + 2),
+        [SMEM] + [VMEM] * (2 * chips + 2),
         [
             pltpu.VMEM((groups * WINDOW, seqs), BF),
             pltpu.VMEM((rows * width // LANES, PROJ_CHANNELS * LANES), BF),
@@ -331,7 +388,7 @@
         ],
         flops=1 << 31,
         limit=32,
-    )(*mine, *theirs, right, wbd)
+    )(table, *mine, *theirs, right, wbd)
     parts = [partial[0]] + [swap(partial[k], "depth", k) for k in range(1, groups)]
 
     pair_strip, normed = call(

time: 48.7 us -> 44.1 us (0.906)
  starting transfers between devices: 19.6 us -> 17.1 us
  waiting for transfers between devices: 19.3 us -> 17 us
    ppermute x21 -> x19, starting transfers between devices: 19.6 us -> 17.1 us  [swap(): return lax.ppermute(x, axis, [(i, i ^ mask) for i in range(n)])]
    ppermute x21 -> x19, waiting for transfers between devices: 19.3 us -> 17 us  [swap(): return lax.ppermute(x, axis, [(i, i ^ mask) for i in range(n)])]
  transfers between devices with their start and end apart: 21 -> 19, of which waited for: 12 -> 11; matrix products, arithmetic and copies ran while one was open for 0% -> 0% of each run, Pallas kernels for 3% -> 4%
where the time goes in v4:
time: 44.1 us; the launch traced here: 43.9 us
  starting transfers between devices  17.1 us (39%)
  waiting for transfers between devices  17 us (39%)
  Pallas kernels  8.94 us (20%)
  between operations  0.74 us (2%)
    ppermute x19, starting transfers between devices, swap(): return lax.ppermute(x, axis, [(i, i ^ mask) for i in range(n)])  17.1 us
    ppermute x19, waiting for transfers between devices, swap(): return lax.ppermute(x, axis, [(i, i ^ mask) for i in range(n)])  17 us
    pallas_call x1, Pallas kernels, body(): call(functools.partial(attend_kernel, chips), [jax.ShapeDtypeStruct((R_DE...  3.15 us
    pallas_call x1, Pallas kernels, body(): call(functools.partial(outer_kernel, chips), [pltpu.VMEM((R_DEV * tokens,...  1.94 us
    pallas_call x1, Pallas kernels, body(): call(prep_kernel, [pltpu.VMEM((PROJ_CHANNELS * LANES, PACK * CZ), BF), pl...  1.46 us
    pallas_call x1, Pallas kernels, body(): call(functools.partial(front_kernel, adaptive, 2 * tokens), [pltpu.VMEM((...  1.07 us
  transfers between devices with their start and end apart: 19, of which 11 were waited for; matrix products, arithmetic and copies ran while one was open for 0% of the time, Pallas kernels for 4%

profile of v4, /device:TPU:0, one launch (start us, length us, event | category | flops | bytes accessed | tf_op | source)
XLA Modules:
  0.0 43.9 jit_solution(6783545531356571204)
XLA Ops:
  0.6 1.1 %shard_map.113 = (bf16[128,1024]{1,0:T(8,128)(2,1)S(1)}, bf16[128,1024]{1,0:T(8,128)(2,1)S(1)}, s32[8]{0:T(128)S(4)}, s32[1]{0:T(128)S(4)}) custom-call(bf16[256,1024]{1,0:T(8,128)(2,1)} %left_ref.1, s32[4]{0:T(128)} %starts_ref.1), custom_call_target="tpu_custom_call" | custom-call | bytes 1048576 | tf_op jit(solution)/shard_map/pallas_call | solution.py:308
  1.7 0.6 %collective-permute-start.12 = (bf16[128,1024]{1,0:T(8,128)(2,1)S(1)}, bf16[128,1024]{1,0:T(8,128)(2,1)S(1)}, u32[]{:S(2)}, u32[]{:S(2)}) collective-permute-start(bf16[128,1024]{1,0:T(8,128)(2,1)S(1)} %get-tuple-element.94), channel_id=1, source_target_pairs={{0,1},{1,0},{2,3},{3,2},{4,5},{5,4},{6,7},{7,6},{8,9},{9,8},{10,11... | collective-permute-start | bytes 786440 | tf_op jit(solution)/shard_map/ppermute | solution.py:280
  2.3 1.2 %collective-permute-done.12.recv_ref = bf16[128,1024]{1,0:T(8,128)(2,1)S(1)} collective-permute-done((bf16[128,1024]{1,0:T(8,128)(2,1)S(1)}, bf16[128,1024]{1,0:T(8,128)(2,1)S(1)}, u32[]{:S(2)}, u32[]{:S(2)}) %collective-permute-start.12) | collective-permute-done | bytes 262176 | tf_op jit(solution)/shard_map/ppermute | solution.py:280
  3.9 5.5 %conditional.1 = (bf16[256,128]{1,0:T(8,128)(2,1)S(1)}) conditional(s32[]{:T(128)} %bitcast, bf16[256,128]{1,0:T(8,128)(2,1)S(1)} %get-tuple-element.95, (bf16[256,128]{1,0:T(8,128)(2,1)S(1)}, bf16[256,128]{1,0:T(8,128)(2,1)S(1)}) %tuple.32, (bf16[256,128]{1,0:T(8,128)(2,1)S(1)}, ...), branch_computations={%region_0.0_spmd, %region_1.0_spmd, %region_2.0_spmd, %region_3.0_... | conditional | flops 98304 | bytes 1114240 | solution.py:372
  3.9 3.0 %collective-permute-start = (bf16[256,128]{1,0:T(8,128)(2,1)S(1)}, bf16[256,128]{1,0:T(8,128)(2,1)S(1)}, u32[]{:S(2)}, u32[]{:S(2)}) collective-permute-start(bf16[256,128]{1,0:T(8,128)(2,1)S(1)} %get-tuple-element.44), channel_id=1, source_target_pairs={{0,2},{1,3},{2,0},{3,1},{4,6},{5,7},{6,4},{7,5},{8,10},{9,11},{10,... | collective-permute-start | bytes 196616 | tf_op jit(solution)/shard_map/cond/branch_1_fun/ppermute | solution.py:280
  6.9 2.4 %collective-permute-done = bf16[256,128]{1,0:T(8,128)(2,1)S(1)} collective-permute-done((bf16[256,128]{1,0:T(8,128)(2,1)S(1)}, bf16[256,128]{1,0:T(8,128)(2,1)S(1)}, u32[]{:S(2)}, u32[]{:S(2)}) %collective-permute-start) | collective-permute-done | bytes 65568 | tf_op jit(solution)/shard_map/cond/branch_1_fun/ppermute | solution.py:280
  9.3 4.0 %collective-permute-start.15 = (bf16[256,128]{1,0:T(8,128)(2,1)S(1)}, bf16[256,128]{1,0:T(8,128)(2,1)S(1)}, u32[]{:S(2)}, u32[]{:S(2)}) collective-permute-start(bf16[256,128]{1,0:T(8,128)(2,1)S(1)} %get-tuple-element.113.refs_0_), channel_id=1, source_target_pairs={{0,6},{1,7},{2,4},{3,5},{4,2},{5,3},{6,0},{7,1},{8,14},{9,15},{10,... | collective-permute-start | bytes 196616 | tf_op jit(solution)/shard_map/ppermute | solution.py:280
  13.3 0.6 %collective-permute-start.13 = (bf16[256,128]{1,0:T(8,128)(2,1)S(1)}, bf16[256,128]{1,0:T(8,128)(2,1)S(1)}, u32[]{:S(2)}, u32[]{:S(2)}) collective-permute-start(bf16[256,128]{1,0:T(8,128)(2,1)S(1)} %get-tuple-element.113.refs_0_), channel_id=1, source_target_pairs={{0,2},{1,3},{2,0},{3,1},{4,6},{5,7},{6,4},{7,5},{8,10},{9,11},{10,... | collective-permute-start | bytes 196616 | tf_op jit(solution)/shard_map/ppermute | solution.py:280
  14.0 2.1 %collective-permute-done.15.refs_3_ = bf16[256,128]{1,0:T(8,128)(2,1)S(1)} collective-permute-done((bf16[256,128]{1,0:T(8,128)(2,1)S(1)}, bf16[256,128]{1,0:T(8,128)(2,1)S(1)}, u32[]{:S(2)}, u32[]{:S(2)}) %collective-permute-start.15) | collective-permute-done | bytes 65568 | tf_op jit(solution)/shard_map/ppermute | solution.py:280
  16.0 2.7 %collective-permute-done.14.refs_2_ = bf16[256,128]{1,0:T(8,128)(2,1)S(1)} collective-permute-done((bf16[256,128]{1,0:T(8,128)(2,1)S(1)}, bf16[256,128]{1,0:T(8,128)(2,1)S(1)}, u32[]{:S(2)}, u32[]{:S(2)}) %collective-permute-start.14) | collective-permute-done | bytes 65568 | tf_op jit(solution)/shard_map/ppermute | solution.py:280
  19.2 1.5 %shard_map.115 = (bf16[4096,512]{1,0:T(8,128)(2,1)S(1)}, f32[128,256]{1,0:T(8,128)S(1)}, bf16[256,1024]{1,0:T(8,128)(2,1)S(1)}, bf16[128,512]{1,0:T(8,128)(2,1)S...) custom-call(bf16[1024,128]{1,0:T(8,128)(2,1)} %refs_0_.1, bf16[4,32,256]{2,1,0:T(8,128)(2,1)} %refs_1_.1, ...), custom_call_target="tpu_custom_call" | custom-call | flops 268435456 | bytes 1048576 | tf_op jit(solution)/shard_map/pallas_call | solution.py:321
  20.7 1.9 %shard_map.116 = (bf16[256,128]{1,0:T(8,128)(2,1)S(1)}, bf16[256,128]{1,0:T(8,128)(2,1)S(1)}, bf16[256,128]{1,0:T(8,128)(2,1)S(1)}, bf16[256,128]{1,0:T(8,128)(2,1)S(1)}) custom-call(s32[8]{0:T(128)S(4)} %get-tuple-element.91.table, bf16[256,128]{1,0:T(8,128)(2,1)S(1)} %get-tuple-element.113.refs_0_, bf16[256,128]{1,0:T(8,128)(2,1)S(1)} %collective-permute-done.13.refs_1_, ...), custom_call_target="tpu_custom_call" | custom-call | flops 2147483648 | bytes 1048576 | tf_op jit(solution)/shard_map/pallas_call | solution.py:380
  22.7 1.6 %collective-permute-start.20 = (bf16[256,128]{1,0:T(8,128)(2,1)S(1)}, bf16[256,128]{1,0:T(8,128)(2,1)S(1)}, u32[]{:S(2)}, u32[]{:S(2)}) collective-permute-start(bf16[256,128]{1,0:T(8,128)(2,1)S(1)} %get-tuple-element.102), channel_id=1, source_target_pairs={{0,8},{8,0},{16,24},{24,16},{1,9},{9,1},{17,25},{25,17},{2,10},{10... | collective-permute-start | bytes 196616 | tf_op jit(solution)/shard_map/ppermute | solution.py:280
  24.2 1.5 %collective-permute-start.21 = (bf16[256,128]{1,0:T(8,128)(2,1)S(1)}, bf16[256,128]{1,0:T(8,128)(2,1)S(1)}, u32[]{:S(2)}, u32[]{:S(2)}) collective-permute-start(bf16[256,128]{1,0:T(8,128)(2,1)S(1)} %get-tuple-element.103), channel_id=1, source_target_pairs={{0,16},{8,24},{16,0},{24,8},{1,17},{9,25},{17,1},{25,9},{2,18},{10... | collective-permute-start | bytes 196616 | tf_op jit(solution)/shard_map/ppermute | solution.py:280
  26.2 0.8 %collective-permute-done.20.refs_1_ = bf16[256,128]{1,0:T(8,128)(2,1)S(1)} collective-permute-done((bf16[256,128]{1,0:T(8,128)(2,1)S(1)}, bf16[256,128]{1,0:T(8,128)(2,1)S(1)}, u32[]{:S(2)}, u32[]{:S(2)}) %collective-permute-start.20) | collective-permute-done | bytes 65568 | tf_op jit(solution)/shard_map/ppermute | solution.py:280
  27.0 1.5 %collective-permute-done.21.refs_2_ = bf16[256,128]{1,0:T(8,128)(2,1)S(1)} collective-permute-done((bf16[256,128]{1,0:T(8,128)(2,1)S(1)}, bf16[256,128]{1,0:T(8,128)(2,1)S(1)}, u32[]{:S(2)}, u32[]{:S(2)}) %collective-permute-start.21) | collective-permute-done | bytes 65568 | tf_op jit(solution)/shard_map/ppermute | solution.py:280
  28.5 2.4 %collective-permute-done.22.refs_3_ = bf16[256,128]{1,0:T(8,128)(2,1)S(1)} collective-permute-done((bf16[256,128]{1,0:T(8,128)(2,1)S(1)}, bf16[256,128]{1,0:T(8,128)(2,1)S(1)}, u32[]{:S(2)}, u32[]{:S(2)}) %collective-permute-start.22) | collective-permute-done | bytes 65568 | tf_op jit(solution)/shard_map/ppermute | solution.py:280
  30.9 0.7 %shard_map.117 = (bf16[8,32,128]{2,1,0:T(8,128)(2,1)}, bf16[8,32,128]{2,1,0:T(8,128)(2,1)S(1)}) custom-call(bf16[256,128]{1,0:T(8,128)(2,1)S(1)} %get-tuple-element.101.refs_0_, bf16[256,128]{1,0:T(8,128)(2,1)S(1)} %collective-permute-done.20.refs_1_, bf16[256,128]{1,0:T(8,128)(2,1)S(1)} %collective-permute-done.21.refs_2_, ...), custom_call_target="tpu_custom_call" | custom-call | flops 16777216 | bytes 1048576 | tf_op jit(solution)/shard_map/pallas_call | solution.py:394
  31.6 2.2 %collective-permute-start.25 = (bf16[8,32,128]{2,1,0:T(8,128)(2,1)S(1)}, bf16[8,32,128]{2,1,0:T(8,128)(2,1)S(1)}, u32[]{:S(2)}, u32[]{:S(2)}) collective-permute-start(bf16[8,32,128]{2,1,0:T(8,128)(2,1)S(1)} %get-tuple-element.107.normed_ref.refs_0_), channel_id=1, source_target_pairs={{0,6},{1,7},{2,4},{3,5},{4,2},{5,3},{6,0},{7,1},{8,14},{9,15},{10,... | collective-permute-start | bytes 196616 | tf_op jit(solution)/shard_map/ppermute | solution.py:280
  33.8 2.2 %collective-permute-start.23 = (bf16[8,32,128]{2,1,0:T(8,128)(2,1)S(1)}, bf16[8,32,128]{2,1,0:T(8,128)(2,1)S(1)}, u32[]{:S(2)}, u32[]{:S(2)}) collective-permute-start(bf16[8,32,128]{2,1,0:T(8,128)(2,1)S(1)} %get-tuple-element.107.normed_ref.refs_0_), channel_id=1, source_target_pairs={{0,2},{1,3},{2,0},{3,1},{4,6},{5,7},{6,4},{7,5},{8,10},{9,11},{10,... | collective-permute-start | bytes 196616 | tf_op jit(solution)/shard_map/ppermute | solution.py:280
  36.0 1.9 %collective-permute-done.25.refs_3_ = bf16[8,32,128]{2,1,0:T(8,128)(2,1)S(1)} collective-permute-done((bf16[8,32,128]{2,1,0:T(8,128)(2,1)S(1)}, bf16[8,32,128]{2,1,0:T(8,128)(2,1)S(1)}, u32[]{:S(2)}, u32[]{:S(2)}) %collective-permute-start.25) | collective-permute-done | bytes 65568 | tf_op jit(solution)/shard_map/ppermute | solution.py:280
  37.9 1.4 %collective-permute-done.24.refs_2_ = bf16[8,32,128]{2,1,0:T(8,128)(2,1)S(1)} collective-permute-done((bf16[8,32,128]{2,1,0:T(8,128)(2,1)S(1)}, bf16[8,32,128]{2,1,0:T(8,128)(2,1)S(1)}, u32[]{:S(2)}, u32[]{:S(2)}) %collective-permute-start.24) | collective-permute-done | bytes 65568 | tf_op jit(solution)/shard_map/ppermute | solution.py:280
  40.0 0.5 %collective-permute-done.28.refs_6_ = bf16[8,32,128]{2,1,0:T(8,128)(2,1)S(1)} collective-permute-done((bf16[8,32,128]{2,1,0:T(8,128)(2,1)S(1)}, bf16[8,32,128]{2,1,0:T(8,128)(2,1)S(1)}, u32[]{:S(2)}, u32[]{:S(2)}) %collective-permute-start.28) | collective-permute-done | bytes 65568 | tf_op jit(solution)/shard_map/ppermute | solution.py:280
  40.7 3.2 %shard_map.119 = bf16[8,32,128]{2,1,0:T(8,128)(2,1)} custom-call(bf16[8,32,128]{2,1,0:T(8,128)(2,1)S(1)} %get-tuple-element.107.normed_ref.refs_0_, bf16[8,32,128]{2,1,0:T(8,128)(2,1)S(1)} %collective-permute-done.23.refs_1_, bf16[8,32,128]{2,1,0:T(8,128)(2,1)S(1)} %collective-permute-done.24.refs_2_, ...), custom_call_target="tpu_custom_call" | custom-call | flops 536870912 | bytes 1048576 | tf_op jit(solution)/shard_map/pallas_call | solution.py:416
  (23 shorter events, 2.4 us)
Async XLA Ops:
  1.7 1.7 %collective-permute-start.12 = (bf16[128,1024]{1,0:T(8,128)(2,1)S(1)}, bf16[128,1024]{1,0:T(8,128)(2,1)S(1)}, u32[]{:S(2)}, u32[]{:S(2)}) collective-permute-start(bf16[128,1024]{1,0:T(8,128)(2,1)S(1)} %get-tuple-element.94), channel_id=1, source_target_pairs={{0,1},{1,0},{2,3},{3,2},{4,5},{5,4},{6,7},{7,6},{8,9},{9,8},{10,11... | collective-permute-start | bytes 786440 | tf_op jit(solution)/shard_map/ppermute | solution.py:280
  3.9 5.4 %collective-permute-start = (bf16[256,128]{1,0:T(8,128)(2,1)S(1)}, bf16[256,128]{1,0:T(8,128)(2,1)S(1)}, u32[]{:S(2)}, u32[]{:S(2)}) collective-permute-start(bf16[256,128]{1,0:T(8,128)(2,1)S(1)} %get-tuple-element.44), channel_id=1, source_target_pairs={{0,2},{1,3},{2,0},{3,1},{4,6},{5,7},{6,4},{7,5},{8,10},{9,11},{10,... | collective-permute-start | bytes 196616 | tf_op jit(solution)/shard_map/cond/branch_1_fun/ppermute | solution.py:280
  9.3 6.7 %collective-permute-start.15 = (bf16[256,128]{1,0:T(8,128)(2,1)S(1)}, bf16[256,128]{1,0:T(8,128)(2,1)S(1)}, u32[]{:S(2)}, u32[]{:S(2)}) collective-permute-start(bf16[256,128]{1,0:T(8,128)(2,1)S(1)} %get-tuple-element.113.refs_0_), channel_id=1, source_target_pairs={{0,6},{1,7},{2,4},{3,5},{4,2},{5,3},{6,0},{7,1},{8,14},{9,15},{10,... | collective-permute-start | bytes 196616 | tf_op jit(solution)/shard_map/ppermute | solution.py:280
  13.3 5.4 %collective-permute-start.14 = (bf16[256,128]{1,0:T(8,128)(2,1)S(1)}, bf16[256,128]{1,0:T(8,128)(2,1)S(1)}, u32[]{:S(2)}, u32[]{:S(2)}) collective-permute-start(bf16[256,128]{1,0:T(8,128)(2,1)S(1)} %get-tuple-element.113.refs_0_), channel_id=1, source_target_pairs={{0,4},{1,5},{2,6},{3,7},{4,0},{5,1},{6,2},{7,3},{8,12},{9,13},{10,... | collective-permute-start | bytes 196616 | tf_op jit(solution)/shard_map/ppermute | solution.py:280
  13.3 5.4 %collective-permute-start.13 = (bf16[256,128]{1,0:T(8,128)(2,1)S(1)}, bf16[256,128]{1,0:T(8,128)(2,1)S(1)}, u32[]{:S(2)}, u32[]{:S(2)}) collective-permute-start(bf16[256,128]{1,0:T(8,128)(2,1)S(1)} %get-tuple-element.113.refs_0_), channel_id=1, source_target_pairs={{0,2},{1,3},{2,0},{3,1},{4,6},{5,7},{6,4},{7,5},{8,10},{9,11},{10,... | collective-permute-start | bytes 196616 | tf_op jit(solution)/shard_map/ppermute | solution.py:280
  14.0 6.7 %collective-permute-start.16 = (bf16[256,128]{1,0:T(8,128)(2,1)S(1)}, bf16[256,128]{1,0:T(8,128)(2,1)S(1)}, u32[]{:S(2)}, u32[]{:S(2)}) collective-permute-start(bf16[256,128]{1,0:T(8,128)(2,1)S(1)} %get-tuple-element.113.refs_0_), channel_id=1, source_target_pairs={{0,1},{1,0},{2,3},{3,2},{4,5},{5,4},{6,7},{7,6},{8,9},{9,8},{10,11... | collective-permute-start | bytes 196616 | tf_op jit(solution)/shard_map/ppermute | solution.py:280
  16.0 4.7 %collective-permute-start.19 = (bf16[256,128]{1,0:T(8,128)(2,1)S(1)}, bf16[256,128]{1,0:T(8,128)(2,1)S(1)}, u32[]{:S(2)}, u32[]{:S(2)}) collective-permute-start(bf16[256,128]{1,0:T(8,128)(2,1)S(1)} %collective-permute-done.15.refs_3_), channel_id=1, source_target_pairs={{0,1},{1,0},{2,3},{3,2},{4,5},{5,4},{6,7},{7,6},{8,9},{9,8},{10,11... | collective-permute-start | bytes 196616 | tf_op jit(solution)/shard_map/ppermute | solution.py:280
  18.7 2.0 %collective-permute-start.18 = (bf16[256,128]{1,0:T(8,128)(2,1)S(1)}, bf16[256,128]{1,0:T(8,128)(2,1)S(1)}, u32[]{:S(2)}, u32[]{:S(2)}) collective-permute-start(bf16[256,128]{1,0:T(8,128)(2,1)S(1)} %collective-permute-done.14.refs_2_), channel_id=1, source_target_pairs={{0,1},{1,0},{2,3},{3,2},{4,5},{5,4},{6,7},{7,6},{8,9},{9,8},{10,11... | collective-permute-start | bytes 196616 | tf_op jit(solution)/shard_map/ppermute | solution.py:280
  18.7 2.0 %collective-permute-start.17 = (bf16[256,128]{1,0:T(8,128)(2,1)S(1)}, bf16[256,128]{1,0:T(8,128)(2,1)S(1)}, u32[]{:S(2)}, u32[]{:S(2)}) collective-permute-start(bf16[256,128]{1,0:T(8,128)(2,1)S(1)} %collective-permute-done.13.refs_1_), channel_id=1, source_target_pairs={{0,1},{1,0},{2,3},{3,2},{4,5},{5,4},{6,7},{7,6},{8,9},{9,8},{10,11... | collective-permute-start | bytes 196616 | tf_op jit(solution)/shard_map/ppermute | solution.py:280
  22.7 4.3 %collective-permute-start.20 = (bf16[256,128]{1,0:T(8,128)(2,1)S(1)}, bf16[256,128]{1,0:T(8,128)(2,1)S(1)}, u32[]{:S(2)}, u32[]{:S(2)}) collective-permute-start(bf16[256,128]{1,0:T(8,128)(2,1)S(1)} %get-tuple-element.102), channel_id=1, source_target_pairs={{0,8},{8,0},{16,24},{24,16},{1,9},{9,1},{17,25},{25,17},{2,10},{10... | collective-permute-start | bytes 196616 | tf_op jit(solution)/shard_map/ppermute | solution.py:280
  24.2 4.3 %collective-permute-start.21 = (bf16[256,128]{1,0:T(8,128)(2,1)S(1)}, bf16[256,128]{1,0:T(8,128)(2,1)S(1)}, u32[]{:S(2)}, u32[]{:S(2)}) collective-permute-start(bf16[256,128]{1,0:T(8,128)(2,1)S(1)} %get-tuple-element.103), channel_id=1, source_target_pairs={{0,16},{8,24},{16,0},{24,8},{1,17},{9,25},{17,1},{25,9},{2,18},{10... | collective-permute-start | bytes 196616 | tf_op jit(solution)/shard_map/ppermute | solution.py:280
  25.7 5.2 %collective-permute-start.22 = (bf16[256,128]{1,0:T(8,128)(2,1)S(1)}, bf16[256,128]{1,0:T(8,128)(2,1)S(1)}, u32[]{:S(2)}, u32[]{:S(2)}) collective-permute-start(bf16[256,128]{1,0:T(8,128)(2,1)S(1)} %get-tuple-element.104), channel_id=1, source_target_pairs={{0,24},{8,16},{16,8},{24,0},{1,25},{9,17},{17,9},{25,1},{2,26},{10... | collective-permute-start | bytes 196616 | tf_op jit(solution)/shard_map/ppermute | solution.py:280
  31.6 6.3 %collective-permute-start.25 = (bf16[8,32,128]{2,1,0:T(8,128)(2,1)S(1)}, bf16[8,32,128]{2,1,0:T(8,128)(2,1)S(1)}, u32[]{:S(2)}, u32[]{:S(2)}) collective-permute-start(bf16[8,32,128]{2,1,0:T(8,128)(2,1)S(1)} %get-tuple-element.107.normed_ref.refs_0_), channel_id=1, source_target_pairs={{0,6},{1,7},{2,4},{3,5},{4,2},{5,3},{6,0},{7,1},{8,14},{9,15},{10,... | collective-permute-start | bytes 196616 | tf_op jit(solution)/shard_map/ppermute | solution.py:280
  33.8 5.5 %collective-permute-start.24 = (bf16[8,32,128]{2,1,0:T(8,128)(2,1)S(1)}, bf16[8,32,128]{2,1,0:T(8,128)(2,1)S(1)}, u32[]{:S(2)}, u32[]{:S(2)}) collective-permute-start(bf16[8,32,128]{2,1,0:T(8,128)(2,1)S(1)} %get-tuple-element.107.normed_ref.refs_0_), channel_id=1, source_target_pairs={{0,4},{1,5},{2,6},{3,7},{4,0},{5,1},{6,2},{7,3},{8,12},{9,13},{10,... | collective-permute-start | bytes 196616 | tf_op jit(solution)/shard_map/ppermute | solution.py:280
  33.8 5.5 %collective-permute-start.23 = (bf16[8,32,128]{2,1,0:T(8,128)(2,1)S(1)}, bf16[8,32,128]{2,1,0:T(8,128)(2,1)S(1)}, u32[]{:S(2)}, u32[]{:S(2)}) collective-permute-start(bf16[8,32,128]{2,1,0:T(8,128)(2,1)S(1)} %get-tuple-element.107.normed_ref.refs_0_), channel_id=1, source_target_pairs={{0,2},{1,3},{2,0},{3,1},{4,6},{5,7},{6,4},{7,5},{8,10},{9,11},{10,... | collective-permute-start | bytes 196616 | tf_op jit(solution)/shard_map/ppermute | solution.py:280
  36.0 4.0 %collective-permute-start.26 = (bf16[8,32,128]{2,1,0:T(8,128)(2,1)S(1)}, bf16[8,32,128]{2,1,0:T(8,128)(2,1)S(1)}, u32[]{:S(2)}, u32[]{:S(2)}) collective-permute-start(bf16[8,32,128]{2,1,0:T(8,128)(2,1)S(1)} %get-tuple-element.107.normed_ref.refs_0_), channel_id=1, source_target_pairs={{0,1},{1,0},{2,3},{3,2},{4,5},{5,4},{6,7},{7,6},{8,9},{9,8},{10,11... | collective-permute-start | bytes 196616 | tf_op jit(solution)/shard_map/ppermute | solution.py:280
  37.9 2.1 %collective-permute-start.29 = (bf16[8,32,128]{2,1,0:T(8,128)(2,1)S(1)}, bf16[8,32,128]{2,1,0:T(8,128)(2,1)S(1)}, u32[]{:S(2)}, u32[]{:S(2)}) collective-permute-start(bf16[8,32,128]{2,1,0:T(8,128)(2,1)S(1)} %collective-permute-done.25.refs_3_), channel_id=1, source_target_pairs={{0,1},{1,0},{2,3},{3,2},{4,5},{5,4},{6,7},{7,6},{8,9},{9,8},{10,11... | collective-permute-start | bytes 196616 | tf_op jit(solution)/shard_map/ppermute | solution.py:280
  39.3 1.3 %collective-permute-start.28 = (bf16[8,32,128]{2,1,0:T(8,128)(2,1)S(1)}, bf16[8,32,128]{2,1,0:T(8,128)(2,1)S(1)}, u32[]{:S(2)}, u32[]{:S(2)}) collective-permute-start(bf16[8,32,128]{2,1,0:T(8,128)(2,1)S(1)} %collective-permute-done.24.refs_2_), channel_id=1, source_target_pairs={{0,1},{1,0},{2,3},{3,2},{4,5},{5,4},{6,7},{7,6},{8,9},{9,8},{10,11... | collective-permute-start | bytes 196616 | tf_op jit(solution)/shard_map/ppermute | solution.py:280
  39.3 1.4 %collective-permute-start.27 = (bf16[8,32,128]{2,1,0:T(8,128)(2,1)S(1)}, bf16[8,32,128]{2,1,0:T(8,128)(2,1)S(1)}, u32[]{:S(2)}, u32[]{:S(2)}) collective-permute-start(bf16[8,32,128]{2,1,0:T(8,128)(2,1)S(1)} %collective-permute-done.23.refs_1_), channel_id=1, source_target_pairs={{0,1},{1,0},{2,3},{3,2},{4,5},{5,4},{6,7},{7,6},{8,9},{9,8},{10,11... | collective-permute-start | bytes 196616 | tf_op jit(solution)/shard_map/ppermute | solution.py:280

commit v5 on v4

--- a/solution.py
+++ b/solution.py
@@ -231,7 +231,8 @@
 
 def attend_kernel(chips, *refs):
     mine, theirs = refs[:chips], refs[chips : 2 * chips]
-    q_ref, gate_ref, w_ref, wo_ref, bias_ref, out_ref, all_ref, gated_ref = refs[2 * chips :]
+    q_ref, gate_ref, w_ref, wo_ref, bias_ref, out_ref = refs[2 * chips : -4]
+    all_ref, kv_ref, scores_ref, gated_ref = refs[-4:]
     tokens = mine[0].shape[1]
     z = lax.axis_index("res") // 2
     core = lax.axis_index("res") % 2
@@ -243,21 +244,26 @@
         all_ref[:, pl.ds(theirs_at, tokens), :] = theirs[k][...]
     scale = DH ** (-0.5)
     lane_head = lax.broadcasted_iota(jnp.int32, (tokens, CZ), 1) // DH
+    kv = jnp.dot(
+        all_ref[...].reshape(-1, CZ), w_ref[:, CZ : 3 * CZ], preferred_element_type=F32
+    )
+    kv_ref[...] = kv.astype(BF).reshape(kv_ref.shape)
     for u in range(R_DEV):
-        kv = jnp.dot(
-            all_ref[u], w_ref[:, CZ : 3 * CZ], preferred_element_type=F32
-        ).astype(BF)
         q = q_ref[u * tokens : (u + 1) * tokens, :]
         spread = jnp.concatenate(
             [jnp.where(lane_head == h, q, jnp.zeros_like(q)) for h in range(H)], axis=0
         )
         scores = lax.dot_general(
-            spread, kv[:, :CZ], (((1,), (1,)), ((), ())), preferred_element_type=F32
-        )
-        scores = scores * scale + bias_ref[...]
+            spread, kv_ref[u, :, :CZ], (((1,), (1,)), ((), ())), preferred_element_type=F32
+        )
+        scores_ref[u] = scores * scale + bias_ref[...]
+    for u in range(R_DEV):
+        scores = scores_ref[u]
         weights = jnp.exp(scores - jnp.max(scores, axis=-1, keepdims=True))
         denom = jnp.sum(weights, axis=-1, keepdims=True)
-        value = jnp.dot(weights.astype(BF), kv[:, CZ:], preferred_element_type=F32)
+        value = jnp.dot(
+            weights.astype(BF), kv_ref[u, :, CZ:], preferred_element_type=F32
+        )
         value = value / denom
         attended = jnp.zeros((tokens, CZ), F32)
         for h in range(H):
@@ -419,10 +425,12 @@
         [VMEM] * (2 * chips + 5),
         [
             pltpu.VMEM((R_DEV, keys, CZ), BF),
+            pltpu.VMEM((R_DEV, keys, 2 * CZ), BF),
+            pltpu.VMEM((R_DEV, H * tokens, keys), F32),
             pltpu.VMEM((R_DEV * tokens, CZ), BF),
         ],
         flops=1 << 29,
-        limit=16,
+        limit=24,
     )(*near, *far, queries, gate, qkvg, wo, bias)
     return (pair_strip, update)
 

time: 44.1 us -> 43 us (0.975)
  Pallas kernels: 8.94 us -> 7.85 us
    pallas_call x1, Pallas kernels: 3.15 us -> 2.07 us  [body(): call(functools.partial(attend_kernel, chips), [jax.ShapeDtypeStruct((R_DE...]
where the time goes in v5:
time: 43 us; the launch traced here: 42.8 us
  starting transfers between devices  17.1 us (40%)
  waiting for transfers between devices  17 us (40%)
  Pallas kernels  7.85 us (18%)
  between operations  0.74 us (2%)
    ppermute x19, starting transfers between devices, swap(): return lax.ppermute(x, axis, [(i, i ^ mask) for i in range(n)])  17.1 us
    ppermute x19, waiting for transfers between devices, swap(): return lax.ppermute(x, axis, [(i, i ^ mask) for i in range(n)])  17 us
    pallas_call x1, Pallas kernels, body(): call(functools.partial(attend_kernel, chips), [jax.ShapeDtypeStruct((R_DE...  2.07 us
    pallas_call x1, Pallas kernels, body(): call(functools.partial(outer_kernel, chips), [pltpu.VMEM((R_DEV * tokens,...  1.94 us
    pallas_call x1, Pallas kernels, body(): call(prep_kernel, [pltpu.VMEM((PROJ_CHANNELS * LANES, PACK * CZ), BF), pl...  1.46 us
    pallas_call x1, Pallas kernels, body(): call(functools.partial(front_kernel, adaptive, 2 * tokens), [pltpu.VMEM((...  1.07 us
  transfers between devices with their start and end apart: 19, of which 11 were waited for; matrix products, arithmetic and copies ran while one was open for 0% of the time, Pallas kernels for 4%

profile of v5, /device:TPU:0, one launch (start us, length us, event | category | flops | bytes accessed | tf_op | source)
XLA Modules:
  0.0 42.8 jit_solution(421090505168891001)
XLA Ops:
  0.6 1.1 %shard_map.113 = (bf16[128,1024]{1,0:T(8,128)(2,1)S(1)}, bf16[128,1024]{1,0:T(8,128)(2,1)S(1)}, s32[8]{0:T(128)S(4)}, s32[1]{0:T(128)S(4)}) custom-call(bf16[256,1024]{1,0:T(8,128)(2,1)} %left_ref.1, s32[4]{0:T(128)} %starts_ref.1), custom_call_target="tpu_custom_call" | custom-call | bytes 1048576 | tf_op jit(solution)/shard_map/pallas_call | solution.py:314
  1.7 0.6 %collective-permute-start.12 = (bf16[128,1024]{1,0:T(8,128)(2,1)S(1)}, bf16[128,1024]{1,0:T(8,128)(2,1)S(1)}, u32[]{:S(2)}, u32[]{:S(2)}) collective-permute-start(bf16[128,1024]{1,0:T(8,128)(2,1)S(1)} %get-tuple-element.94), channel_id=1, source_target_pairs={{0,1},{1,0},{2,3},{3,2},{4,5},{5,4},{6,7},{7,6},{8,9},{9,8},{10,11... | collective-permute-start | bytes 786440 | tf_op jit(solution)/shard_map/ppermute | solution.py:286
  2.3 1.2 %collective-permute-done.12.recv_ref = bf16[128,1024]{1,0:T(8,128)(2,1)S(1)} collective-permute-done((bf16[128,1024]{1,0:T(8,128)(2,1)S(1)}, bf16[128,1024]{1,0:T(8,128)(2,1)S(1)}, u32[]{:S(2)}, u32[]{:S(2)}) %collective-permute-start.12) | collective-permute-done | bytes 262176 | tf_op jit(solution)/shard_map/ppermute | solution.py:286
  3.9 5.5 %conditional.1 = (bf16[256,128]{1,0:T(8,128)(2,1)S(1)}) conditional(s32[]{:T(128)} %bitcast, bf16[256,128]{1,0:T(8,128)(2,1)S(1)} %get-tuple-element.95, (bf16[256,128]{1,0:T(8,128)(2,1)S(1)}, bf16[256,128]{1,0:T(8,128)(2,1)S(1)}) %tuple.32, (bf16[256,128]{1,0:T(8,128)(2,1)S(1)}, ...), branch_computations={%region_0.0_spmd, %region_1.0_spmd, %region_2.0_spmd, %region_3.0_... | conditional | flops 98304 | bytes 1114240 | solution.py:378
  3.9 3.0 %collective-permute-start = (bf16[256,128]{1,0:T(8,128)(2,1)S(1)}, bf16[256,128]{1,0:T(8,128)(2,1)S(1)}, u32[]{:S(2)}, u32[]{:S(2)}) collective-permute-start(bf16[256,128]{1,0:T(8,128)(2,1)S(1)} %get-tuple-element.44), channel_id=1, source_target_pairs={{0,2},{1,3},{2,0},{3,1},{4,6},{5,7},{6,4},{7,5},{8,10},{9,11},{10,... | collective-permute-start | bytes 196616 | tf_op jit(solution)/shard_map/cond/branch_1_fun/ppermute | solution.py:286
  6.9 2.4 %collective-permute-done = bf16[256,128]{1,0:T(8,128)(2,1)S(1)} collective-permute-done((bf16[256,128]{1,0:T(8,128)(2,1)S(1)}, bf16[256,128]{1,0:T(8,128)(2,1)S(1)}, u32[]{:S(2)}, u32[]{:S(2)}) %collective-permute-start) | collective-permute-done | bytes 65568 | tf_op jit(solution)/shard_map/cond/branch_1_fun/ppermute | solution.py:286
  9.3 4.0 %collective-permute-start.15 = (bf16[256,128]{1,0:T(8,128)(2,1)S(1)}, bf16[256,128]{1,0:T(8,128)(2,1)S(1)}, u32[]{:S(2)}, u32[]{:S(2)}) collective-permute-start(bf16[256,128]{1,0:T(8,128)(2,1)S(1)} %get-tuple-element.113.refs_0_), channel_id=1, source_target_pairs={{0,6},{1,7},{2,4},{3,5},{4,2},{5,3},{6,0},{7,1},{8,14},{9,15},{10,... | collective-permute-start | bytes 196616 | tf_op jit(solution)/shard_map/ppermute | solution.py:286
  13.3 0.6 %collective-permute-start.13 = (bf16[256,128]{1,0:T(8,128)(2,1)S(1)}, bf16[256,128]{1,0:T(8,128)(2,1)S(1)}, u32[]{:S(2)}, u32[]{:S(2)}) collective-permute-start(bf16[256,128]{1,0:T(8,128)(2,1)S(1)} %get-tuple-element.113.refs_0_), channel_id=1, source_target_pairs={{0,2},{1,3},{2,0},{3,1},{4,6},{5,7},{6,4},{7,5},{8,10},{9,11},{10,... | collective-permute-start | bytes 196616 | tf_op jit(solution)/shard_map/ppermute | solution.py:286
  14.0 2.1 %collective-permute-done.15.refs_3_ = bf16[256,128]{1,0:T(8,128)(2,1)S(1)} collective-permute-done((bf16[256,128]{1,0:T(8,128)(2,1)S(1)}, bf16[256,128]{1,0:T(8,128)(2,1)S(1)}, u32[]{:S(2)}, u32[]{:S(2)}) %collective-permute-start.15) | collective-permute-done | bytes 65568 | tf_op jit(solution)/shard_map/ppermute | solution.py:286
  16.0 2.7 %collective-permute-done.14.refs_2_ = bf16[256,128]{1,0:T(8,128)(2,1)S(1)} collective-permute-done((bf16[256,128]{1,0:T(8,128)(2,1)S(1)}, bf16[256,128]{1,0:T(8,128)(2,1)S(1)}, u32[]{:S(2)}, u32[]{:S(2)}) %collective-permute-start.14) | collective-permute-done | bytes 65568 | tf_op jit(solution)/shard_map/ppermute | solution.py:286
  19.2 1.5 %shard_map.115 = (bf16[4096,512]{1,0:T(8,128)(2,1)S(1)}, f32[128,256]{1,0:T(8,128)S(1)}, bf16[256,1024]{1,0:T(8,128)(2,1)S(1)}, bf16[128,512]{1,0:T(8,128)(2,1)S...) custom-call(bf16[1024,128]{1,0:T(8,128)(2,1)} %refs_0_.1, bf16[4,32,256]{2,1,0:T(8,128)(2,1)} %refs_1_.1, ...), custom_call_target="tpu_custom_call" | custom-call | flops 268435456 | bytes 1048576 | tf_op jit(solution)/shard_map/pallas_call | solution.py:327
  20.7 1.9 %shard_map.116 = (bf16[256,128]{1,0:T(8,128)(2,1)S(1)}, bf16[256,128]{1,0:T(8,128)(2,1)S(1)}, bf16[256,128]{1,0:T(8,128)(2,1)S(1)}, bf16[256,128]{1,0:T(8,128)(2,1)S(1)}) custom-call(s32[8]{0:T(128)S(4)} %get-tuple-element.91.table, bf16[256,128]{1,0:T(8,128)(2,1)S(1)} %get-tuple-element.113.refs_0_, bf16[256,128]{1,0:T(8,128)(2,1)S(1)} %collective-permute-done.13.refs_1_, ...), custom_call_target="tpu_custom_call" | custom-call | flops 2147483648 | bytes 1048576 | tf_op jit(solution)/shard_map/pallas_call | solution.py:386
  22.7 1.6 %collective-permute-start.20 = (bf16[256,128]{1,0:T(8,128)(2,1)S(1)}, bf16[256,128]{1,0:T(8,128)(2,1)S(1)}, u32[]{:S(2)}, u32[]{:S(2)}) collective-permute-start(bf16[256,128]{1,0:T(8,128)(2,1)S(1)} %get-tuple-element.102), channel_id=1, source_target_pairs={{0,8},{8,0},{16,24},{24,16},{1,9},{9,1},{17,25},{25,17},{2,10},{10... | collective-permute-start | bytes 196616 | tf_op jit(solution)/shard_map/ppermute | solution.py:286
  24.2 1.5 %collective-permute-start.21 = (bf16[256,128]{1,0:T(8,128)(2,1)S(1)}, bf16[256,128]{1,0:T(8,128)(2,1)S(1)}, u32[]{:S(2)}, u32[]{:S(2)}) collective-permute-start(bf16[256,128]{1,0:T(8,128)(2,1)S(1)} %get-tuple-element.103), channel_id=1, source_target_pairs={{0,16},{8,24},{16,0},{24,8},{1,17},{9,25},{17,1},{25,9},{2,18},{10... | collective-permute-start | bytes 196616 | tf_op jit(solution)/shard_map/ppermute | solution.py:286
  26.2 0.8 %collective-permute-done.20.refs_1_ = bf16[256,128]{1,0:T(8,128)(2,1)S(1)} collective-permute-done((bf16[256,128]{1,0:T(8,128)(2,1)S(1)}, bf16[256,128]{1,0:T(8,128)(2,1)S(1)}, u32[]{:S(2)}, u32[]{:S(2)}) %collective-permute-start.20) | collective-permute-done | bytes 65568 | tf_op jit(solution)/shard_map/ppermute | solution.py:286
  27.0 1.5 %collective-permute-done.21.refs_2_ = bf16[256,128]{1,0:T(8,128)(2,1)S(1)} collective-permute-done((bf16[256,128]{1,0:T(8,128)(2,1)S(1)}, bf16[256,128]{1,0:T(8,128)(2,1)S(1)}, u32[]{:S(2)}, u32[]{:S(2)}) %collective-permute-start.21) | collective-permute-done | bytes 65568 | tf_op jit(solution)/shard_map/ppermute | solution.py:286
  28.5 2.4 %collective-permute-done.22.refs_3_ = bf16[256,128]{1,0:T(8,128)(2,1)S(1)} collective-permute-done((bf16[256,128]{1,0:T(8,128)(2,1)S(1)}, bf16[256,128]{1,0:T(8,128)(2,1)S(1)}, u32[]{:S(2)}, u32[]{:S(2)}) %collective-permute-start.22) | collective-permute-done | bytes 65568 | tf_op jit(solution)/shard_map/ppermute | solution.py:286
  30.9 0.7 %shard_map.117 = (bf16[8,32,128]{2,1,0:T(8,128)(2,1)}, bf16[8,32,128]{2,1,0:T(8,128)(2,1)S(1)}) custom-call(bf16[256,128]{1,0:T(8,128)(2,1)S(1)} %get-tuple-element.101.refs_0_, bf16[256,128]{1,0:T(8,128)(2,1)S(1)} %collective-permute-done.20.refs_1_, bf16[256,128]{1,0:T(8,128)(2,1)S(1)} %collective-permute-done.21.refs_2_, ...), custom_call_target="tpu_custom_call" | custom-call | flops 16777216 | bytes 1048576 | tf_op jit(solution)/shard_map/pallas_call | solution.py:400
  31.6 2.2 %collective-permute-start.25 = (bf16[8,32,128]{2,1,0:T(8,128)(2,1)S(1)}, bf16[8,32,128]{2,1,0:T(8,128)(2,1)S(1)}, u32[]{:S(2)}, u32[]{:S(2)}) collective-permute-start(bf16[8,32,128]{2,1,0:T(8,128)(2,1)S(1)} %get-tuple-element.107.normed_ref.refs_0_), channel_id=1, source_target_pairs={{0,6},{1,7},{2,4},{3,5},{4,2},{5,3},{6,0},{7,1},{8,14},{9,15},{10,... | collective-permute-start | bytes 196616 | tf_op jit(solution)/shard_map/ppermute | solution.py:286
  33.8 2.2 %collective-permute-start.23 = (bf16[8,32,128]{2,1,0:T(8,128)(2,1)S(1)}, bf16[8,32,128]{2,1,0:T(8,128)(2,1)S(1)}, u32[]{:S(2)}, u32[]{:S(2)}) collective-permute-start(bf16[8,32,128]{2,1,0:T(8,128)(2,1)S(1)} %get-tuple-element.107.normed_ref.refs_0_), channel_id=1, source_target_pairs={{0,2},{1,3},{2,0},{3,1},{4,6},{5,7},{6,4},{7,5},{8,10},{9,11},{10,... | collective-permute-start | bytes 196616 | tf_op jit(solution)/shard_map/ppermute | solution.py:286
  36.0 1.9 %collective-permute-done.25.refs_3_ = bf16[8,32,128]{2,1,0:T(8,128)(2,1)S(1)} collective-permute-done((bf16[8,32,128]{2,1,0:T(8,128)(2,1)S(1)}, bf16[8,32,128]{2,1,0:T(8,128)(2,1)S(1)}, u32[]{:S(2)}, u32[]{:S(2)}) %collective-permute-start.25) | collective-permute-done | bytes 65568 | tf_op jit(solution)/shard_map/ppermute | solution.py:286
  37.9 1.4 %collective-permute-done.24.refs_2_ = bf16[8,32,128]{2,1,0:T(8,128)(2,1)S(1)} collective-permute-done((bf16[8,32,128]{2,1,0:T(8,128)(2,1)S(1)}, bf16[8,32,128]{2,1,0:T(8,128)(2,1)S(1)}, u32[]{:S(2)}, u32[]{:S(2)}) %collective-permute-start.24) | collective-permute-done | bytes 65568 | tf_op jit(solution)/shard_map/ppermute | solution.py:286
  40.0 0.5 %collective-permute-done.28.refs_6_ = bf16[8,32,128]{2,1,0:T(8,128)(2,1)S(1)} collective-permute-done((bf16[8,32,128]{2,1,0:T(8,128)(2,1)S(1)}, bf16[8,32,128]{2,1,0:T(8,128)(2,1)S(1)}, u32[]{:S(2)}, u32[]{:S(2)}) %collective-permute-start.28) | collective-permute-done | bytes 65568 | tf_op jit(solution)/shard_map/ppermute | solution.py:286
  40.7 2.1 %shard_map.119 = bf16[8,32,128]{2,1,0:T(8,128)(2,1)} custom-call(bf16[8,32,128]{2,1,0:T(8,128)(2,1)S(1)} %get-tuple-element.107.normed_ref.refs_0_, bf16[8,32,128]{2,1,0:T(8,128)(2,1)S(1)} %collective-permute-done.23.refs_1_, bf16[8,32,128]{2,1,0:T(8,128)(2,1)S(1)} %collective-permute-done.24.refs_2_, ...), custom_call_target="tpu_custom_call" | custom-call | flops 536870912 | bytes 1048576 | tf_op jit(solution)/shard_map/pallas_call | solution.py:422
  (23 shorter events, 2.4 us)
Async XLA Ops:
  1.7 1.7 %collective-permute-start.12 = (bf16[128,1024]{1,0:T(8,128)(2,1)S(1)}, bf16[128,1024]{1,0:T(8,128)(2,1)S(1)}, u32[]{:S(2)}, u32[]{:S(2)}) collective-permute-start(bf16[128,1024]{1,0:T(8,128)(2,1)S(1)} %get-tuple-element.94), channel_id=1, source_target_pairs={{0,1},{1,0},{2,3},{3,2},{4,5},{5,4},{6,7},{7,6},{8,9},{9,8},{10,11... | collective-permute-start | bytes 786440 | tf_op jit(solution)/shard_map/ppermute | solution.py:286
  3.9 5.4 %collective-permute-start = (bf16[256,128]{1,0:T(8,128)(2,1)S(1)}, bf16[256,128]{1,0:T(8,128)(2,1)S(1)}, u32[]{:S(2)}, u32[]{:S(2)}) collective-permute-start(bf16[256,128]{1,0:T(8,128)(2,1)S(1)} %get-tuple-element.44), channel_id=1, source_target_pairs={{0,2},{1,3},{2,0},{3,1},{4,6},{5,7},{6,4},{7,5},{8,10},{9,11},{10,... | collective-permute-start | bytes 196616 | tf_op jit(solution)/shard_map/cond/branch_1_fun/ppermute | solution.py:286
  9.3 6.7 %collective-permute-start.15 = (bf16[256,128]{1,0:T(8,128)(2,1)S(1)}, bf16[256,128]{1,0:T(8,128)(2,1)S(1)}, u32[]{:S(2)}, u32[]{:S(2)}) collective-permute-start(bf16[256,128]{1,0:T(8,128)(2,1)S(1)} %get-tuple-element.113.refs_0_), channel_id=1, source_target_pairs={{0,6},{1,7},{2,4},{3,5},{4,2},{5,3},{6,0},{7,1},{8,14},{9,15},{10,... | collective-permute-start | bytes 196616 | tf_op jit(solution)/shard_map/ppermute | solution.py:286
  13.3 5.4 %collective-permute-start.14 = (bf16[256,128]{1,0:T(8,128)(2,1)S(1)}, bf16[256,128]{1,0:T(8,128)(2,1)S(1)}, u32[]{:S(2)}, u32[]{:S(2)}) collective-permute-start(bf16[256,128]{1,0:T(8,128)(2,1)S(1)} %get-tuple-element.113.refs_0_), channel_id=1, source_target_pairs={{0,4},{1,5},{2,6},{3,7},{4,0},{5,1},{6,2},{7,3},{8,12},{9,13},{10,... | collective-permute-start | bytes 196616 | tf_op jit(solution)/shard_map/ppermute | solution.py:286
  13.3 5.4 %collective-permute-start.13 = (bf16[256,128]{1,0:T(8,128)(2,1)S(1)}, bf16[256,128]{1,0:T(8,128)(2,1)S(1)}, u32[]{:S(2)}, u32[]{:S(2)}) collective-permute-start(bf16[256,128]{1,0:T(8,128)(2,1)S(1)} %get-tuple-element.113.refs_0_), channel_id=1, source_target_pairs={{0,2},{1,3},{2,0},{3,1},{4,6},{5,7},{6,4},{7,5},{8,10},{9,11},{10,... | collective-permute-start | bytes 196616 | tf_op jit(solution)/shard_map/ppermute | solution.py:286
  14.0 6.7 %collective-permute-start.16 = (bf16[256,128]{1,0:T(8,128)(2,1)S(1)}, bf16[256,128]{1,0:T(8,128)(2,1)S(1)}, u32[]{:S(2)}, u32[]{:S(2)}) collective-permute-start(bf16[256,128]{1,0:T(8,128)(2,1)S(1)} %get-tuple-element.113.refs_0_), channel_id=1, source_target_pairs={{0,1},{1,0},{2,3},{3,2},{4,5},{5,4},{6,7},{7,6},{8,9},{9,8},{10,11... | collective-permute-start | bytes 196616 | tf_op jit(solution)/shard_map/ppermute | solution.py:286
  16.0 4.7 %collective-permute-start.19 = (bf16[256,128]{1,0:T(8,128)(2,1)S(1)}, bf16[256,128]{1,0:T(8,128)(2,1)S(1)}, u32[]{:S(2)}, u32[]{:S(2)}) collective-permute-start(bf16[256,128]{1,0:T(8,128)(2,1)S(1)} %collective-permute-done.15.refs_3_), channel_id=1, source_target_pairs={{0,1},{1,0},{2,3},{3,2},{4,5},{5,4},{6,7},{7,6},{8,9},{9,8},{10,11... | collective-permute-start | bytes 196616 | tf_op jit(solution)/shard_map/ppermute | solution.py:286
  18.7 2.0 %collective-permute-start.18 = (bf16[256,128]{1,0:T(8,128)(2,1)S(1)}, bf16[256,128]{1,0:T(8,128)(2,1)S(1)}, u32[]{:S(2)}, u32[]{:S(2)}) collective-permute-start(bf16[256,128]{1,0:T(8,128)(2,1)S(1)} %collective-permute-done.14.refs_2_), channel_id=1, source_target_pairs={{0,1},{1,0},{2,3},{3,2},{4,5},{5,4},{6,7},{7,6},{8,9},{9,8},{10,11... | collective-permute-start | bytes 196616 | tf_op jit(solution)/shard_map/ppermute | solution.py:286
  18.7 2.0 %collective-permute-start.17 = (bf16[256,128]{1,0:T(8,128)(2,1)S(1)}, bf16[256,128]{1,0:T(8,128)(2,1)S(1)}, u32[]{:S(2)}, u32[]{:S(2)}) collective-permute-start(bf16[256,128]{1,0:T(8,128)(2,1)S(1)} %collective-permute-done.13.refs_1_), channel_id=1, source_target_pairs={{0,1},{1,0},{2,3},{3,2},{4,5},{5,4},{6,7},{7,6},{8,9},{9,8},{10,11... | collective-permute-start | bytes 196616 | tf_op jit(solution)/shard_map/ppermute | solution.py:286
  22.7 4.3 %collective-permute-start.20 = (bf16[256,128]{1,0:T(8,128)(2,1)S(1)}, bf16[256,128]{1,0:T(8,128)(2,1)S(1)}, u32[]{:S(2)}, u32[]{:S(2)}) collective-permute-start(bf16[256,128]{1,0:T(8,128)(2,1)S(1)} %get-tuple-element.102), channel_id=1, source_target_pairs={{0,8},{8,0},{16,24},{24,16},{1,9},{9,1},{17,25},{25,17},{2,10},{10... | collective-permute-start | bytes 196616 | tf_op jit(solution)/shard_map/ppermute | solution.py:286
  24.2 4.3 %collective-permute-start.21 = (bf16[256,128]{1,0:T(8,128)(2,1)S(1)}, bf16[256,128]{1,0:T(8,128)(2,1)S(1)}, u32[]{:S(2)}, u32[]{:S(2)}) collective-permute-start(bf16[256,128]{1,0:T(8,128)(2,1)S(1)} %get-tuple-element.103), channel_id=1, source_target_pairs={{0,16},{8,24},{16,0},{24,8},{1,17},{9,25},{17,1},{25,9},{2,18},{10... | collective-permute-start | bytes 196616 | tf_op jit(solution)/shard_map/ppermute | solution.py:286
  25.7 5.2 %collective-permute-start.22 = (bf16[256,128]{1,0:T(8,128)(2,1)S(1)}, bf16[256,128]{1,0:T(8,128)(2,1)S(1)}, u32[]{:S(2)}, u32[]{:S(2)}) collective-permute-start(bf16[256,128]{1,0:T(8,128)(2,1)S(1)} %get-tuple-element.104), channel_id=1, source_target_pairs={{0,24},{8,16},{16,8},{24,0},{1,25},{9,17},{17,9},{25,1},{2,26},{10... | collective-permute-start | bytes 196616 | tf_op jit(solution)/shard_map/ppermute | solution.py:286
  31.6 6.3 %collective-permute-start.25 = (bf16[8,32,128]{2,1,0:T(8,128)(2,1)S(1)}, bf16[8,32,128]{2,1,0:T(8,128)(2,1)S(1)}, u32[]{:S(2)}, u32[]{:S(2)}) collective-permute-start(bf16[8,32,128]{2,1,0:T(8,128)(2,1)S(1)} %get-tuple-element.107.normed_ref.refs_0_), channel_id=1, source_target_pairs={{0,6},{1,7},{2,4},{3,5},{4,2},{5,3},{6,0},{7,1},{8,14},{9,15},{10,... | collective-permute-start | bytes 196616 | tf_op jit(solution)/shard_map/ppermute | solution.py:286
  33.8 5.5 %collective-permute-start.24 = (bf16[8,32,128]{2,1,0:T(8,128)(2,1)S(1)}, bf16[8,32,128]{2,1,0:T(8,128)(2,1)S(1)}, u32[]{:S(2)}, u32[]{:S(2)}) collective-permute-start(bf16[8,32,128]{2,1,0:T(8,128)(2,1)S(1)} %get-tuple-element.107.normed_ref.refs_0_), channel_id=1, source_target_pairs={{0,4},{1,5},{2,6},{3,7},{4,0},{5,1},{6,2},{7,3},{8,12},{9,13},{10,... | collective-permute-start | bytes 196616 | tf_op jit(solution)/shard_map/ppermute | solution.py:286
  33.8 5.5 %collective-permute-start.23 = (bf16[8,32,128]{2,1,0:T(8,128)(2,1)S(1)}, bf16[8,32,128]{2,1,0:T(8,128)(2,1)S(1)}, u32[]{:S(2)}, u32[]{:S(2)}) collective-permute-start(bf16[8,32,128]{2,1,0:T(8,128)(2,1)S(1)} %get-tuple-element.107.normed_ref.refs_0_), channel_id=1, source_target_pairs={{0,2},{1,3},{2,0},{3,1},{4,6},{5,7},{6,4},{7,5},{8,10},{9,11},{10,... | collective-permute-start | bytes 196616 | tf_op jit(solution)/shard_map/ppermute | solution.py:286
  36.0 4.0 %collective-permute-start.26 = (bf16[8,32,128]{2,1,0:T(8,128)(2,1)S(1)}, bf16[8,32,128]{2,1,0:T(8,128)(2,1)S(1)}, u32[]{:S(2)}, u32[]{:S(2)}) collective-permute-start(bf16[8,32,128]{2,1,0:T(8,128)(2,1)S(1)} %get-tuple-element.107.normed_ref.refs_0_), channel_id=1, source_target_pairs={{0,1},{1,0},{2,3},{3,2},{4,5},{5,4},{6,7},{7,6},{8,9},{9,8},{10,11... | collective-permute-start | bytes 196616 | tf_op jit(solution)/shard_map/ppermute | solution.py:286
  37.9 2.1 %collective-permute-start.29 = (bf16[8,32,128]{2,1,0:T(8,128)(2,1)S(1)}, bf16[8,32,128]{2,1,0:T(8,128)(2,1)S(1)}, u32[]{:S(2)}, u32[]{:S(2)}) collective-permute-start(bf16[8,32,128]{2,1,0:T(8,128)(2,1)S(1)} %collective-permute-done.25.refs_3_), channel_id=1, source_target_pairs={{0,1},{1,0},{2,3},{3,2},{4,5},{5,4},{6,7},{7,6},{8,9},{9,8},{10,11... | collective-permute-start | bytes 196616 | tf_op jit(solution)/shard_map/ppermute | solution.py:286
  39.3 1.3 %collective-permute-start.28 = (bf16[8,32,128]{2,1,0:T(8,128)(2,1)S(1)}, bf16[8,32,128]{2,1,0:T(8,128)(2,1)S(1)}, u32[]{:S(2)}, u32[]{:S(2)}) collective-permute-start(bf16[8,32,128]{2,1,0:T(8,128)(2,1)S(1)} %collective-permute-done.24.refs_2_), channel_id=1, source_target_pairs={{0,1},{1,0},{2,3},{3,2},{4,5},{5,4},{6,7},{7,6},{8,9},{9,8},{10,11... | collective-permute-start | bytes 196616 | tf_op jit(solution)/shard_map/ppermute | solution.py:286
  39.3 1.4 %collective-permute-start.27 = (bf16[8,32,128]{2,1,0:T(8,128)(2,1)S(1)}, bf16[8,32,128]{2,1,0:T(8,128)(2,1)S(1)}, u32[]{:S(2)}, u32[]{:S(2)}) collective-permute-start(bf16[8,32,128]{2,1,0:T(8,128)(2,1)S(1)} %collective-permute-done.23.refs_1_), channel_id=1, source_target_pairs={{0,1},{1,0},{2,3},{3,2},{4,5},{5,4},{6,7},{7,6},{8,9},{9,8},{10,11... | collective-permute-start | bytes 196616 | tf_op jit(solution)/shard_map/ppermute | solution.py:286

commit v6 on v5

--- a/solution.py
+++ b/solution.py
@@ -42,6 +42,19 @@
             flops=flops, bytes_accessed=1 << 20, transcendentals=0
         ),
     )
+
+
+INNER, FAR = 16, 32
+
+
+def near_price(mask):
+    one, inner, far = (jnp.right_shift(mask, n) & 1 for n in (1, 4, 5))
+    return one * 5 + inner * 6 + far * 100
+
+
+def swap_price(mask):
+    one, two, three = (jnp.right_shift(mask, n) & 1 for n in (1, 2, 3))
+    return one * 5 + two * 12 + three * 10
 
 
 def front_kernel(adaptive, chip_tokens, left_ref, starts_ref, sent_ref, kept_ref, table_ref, need_ref, raw_ref, sem):
@@ -65,21 +78,23 @@
         starts = [raw_ref[g] for g in range(groups)]
         reach = []
         for start in starts:
-            low = start // chip_tokens
-            high = (start + (R_DEV - 1)) // chip_tokens
-            reach.append(
-                [
-                    jnp.left_shift(1, jnp.bitwise_xor(low, h))
-                    | jnp.left_shift(1, jnp.bitwise_xor(high, h))
-                    for h in range(groups)
-                ]
-            )
+            ends = [start // chip_tokens, (start + (R_DEV - 1)) // chip_tokens]
+            reach.append([])
+            for h in range(groups):
+                bits = 0
+                for end in ends:
+                    step = jnp.abs(h - end)
+                    swap_bits = jnp.bitwise_xor(end, h)
+                    bits |= jnp.left_shift(1, swap_bits)
+                    bits |= jnp.where((swap_bits == 3) & (step == 1), INNER, 0)
+                    bits |= jnp.where(step > 1, FAR, 0)
+                reach[-1].append(bits)
         best = cost = homes = None
         for order in itertools.permutations(range(groups)):
             mask = functools.reduce(
                 jnp.bitwise_or, [reach[w][h] for h, w in enumerate(order)]
             )
-            price = sum((jnp.right_shift(mask, k) & 1) * (4 if k == 1 else 5) for k in range(1, groups))
+            price = jnp.minimum(near_price(mask), swap_price(mask))
             packed = jnp.int32(sum(w << (4 * h) for h, w in enumerate(order)))
             if best is None:
                 best, cost, homes = mask, price, packed
@@ -88,7 +103,10 @@
                 best = jnp.where(better, mask, best)
                 homes = jnp.where(better, packed, homes)
                 cost = jnp.where(better, price, cost)
-        need_ref[0] = jnp.right_shift(best, 1)
+        inner = (best & INNER) > 0
+        near = inner & (near_price(best) <= swap_price(best))
+        one = jnp.right_shift(best, 1) & 1
+        need_ref[0] = jnp.where(near, 8 + one, jnp.right_shift(best, 1) & 7)
         for h in range(groups):
             table_ref[h] = jnp.right_shift(homes, 4 * h) & 15
     for g in range(groups):
@@ -221,7 +239,8 @@
         normed_ref[u] = (centred * lax.rsqrt(variance + epsilon)).astype(BF)
 
 
-def query_kernel(normed_ref, w_ref, q_ref, gate_ref):
+def query_kernel(normed_ref, w_ref, pair_ref, q_ref, gate_ref, strip_ref):
+    strip_ref[...] = pair_ref[...]
     rows = R_DEV * normed_ref.shape[1]
     x = normed_ref[...].reshape(rows, CZ)
     q_ref[...] = jnp.dot(x, w_ref[:, :CZ], preferred_element_type=F32).astype(BF)
@@ -370,14 +389,22 @@
             [picked[0]] + [swap(picked[k], "res", 2 * k) for k in wanted],
         )
 
+    def collect_near(one, *picked):
+        inner = [r for r in range(res_count) if abs(r // 2 - (r ^ 6) // 2) == 1]
+        pairs = [(r, r ^ 6 if r in inner else r ^ 1) for r in range(res_count)]
+        moved = [picked[0], lax.ppermute(picked[3], "res", pairs)]
+        if one:
+            moved.append(swap(picked[1], "res", 2))
+        return functools.reduce(jnp.add, moved)
+
     every = range(1, chips)
     if adaptive:
         subsets = [
             [k for k in every if bits >> (k - 1) & 1] for bits in range(1 << len(every))
         ]
-        piece = lax.switch(
-            need[0], [functools.partial(collect, wanted) for wanted in subsets], *picked
-        )
+        branches = [functools.partial(collect, wanted) for wanted in subsets]
+        branches += [functools.partial(collect_near, one) for one in (False, True)]
+        piece = lax.switch(need[0], branches, *picked)
     else:
         piece = collect(every, *picked)
     mine = [piece] + [swap(piece, "res", 2 * k) for k in range(1, chips)]
@@ -397,12 +424,9 @@
     )(table, *mine, *theirs, right, wbd)
     parts = [partial[0]] + [swap(partial[k], "depth", k) for k in range(1, groups)]
 
-    pair_strip, normed = call(
+    pair, normed = call(
         functools.partial(norm_kernel, 1.0 / (seqs * depth_count)),
-        [
-            jax.ShapeDtypeStruct((R_DEV, tokens, CZ), BF),
-            pltpu.VMEM((R_DEV, tokens, CZ), BF),
-        ],
+        [pltpu.VMEM((R_DEV, tokens, CZ), BF)] * 2,
         [VMEM] * (groups + 1),
         [pltpu.VMEM((R_DEV * tokens, CZ), F32)],
         flops=1 << 24,
@@ -410,15 +434,16 @@
 
     near = [normed] + [swap(normed, "res", 2 * k) for k in range(1, chips)]
     far = [swap(n, "res", 1) for n in near]
-    queries, gate = call(
+    queries, gate, pair_strip = call(
         query_kernel,
         [
             pltpu.VMEM((R_DEV * tokens, CZ), BF),
             pltpu.VMEM((R_DEV * tokens, CZ), F32),
-        ],
-        [VMEM] * 2,
+            jax.ShapeDtypeStruct((R_DEV, tokens, CZ), BF),
+        ],
+        [VMEM] * 3,
         flops=1 << 27,
-    )(normed, qkvg)
+    )(normed, qkvg, pair)
     (update,) = call(
         functools.partial(attend_kernel, chips),
         [jax.ShapeDtypeStruct((R_DEV, tokens, CZ), BF)],

time: 43 us -> 42.6 us (level)
    pallas_call x1, Pallas kernels: 0.18 us -> 0.65 us  [body(): call(query_kernel, [pltpu.VMEM((R_DEV * tokens, CZ), BF), pltpu.VMEM((R_D...]
    pallas_call x1, Pallas kernels: 0.69 us -> 0.24 us  [body(): call(functools.partial(norm_kernel, 1.0 / (seqs * depth_count)), [pltpu.V...]
    ppermute x19, waiting for transfers between devices: 17 us -> 16.6 us  [swap(): return lax.ppermute(x, axis, [(i, i ^ mask) for i in range(n)])]
  transfers between devices with their start and end apart: 19 -> 19, of which waited for: 11 -> 11; matrix products, arithmetic and copies ran while one was open for 0% -> 0% of each run, Pallas kernels for 4% -> 5%
where the time goes in v6:
time: 42.6 us; the launch traced here: 42.5 us
  starting transfers between devices  17.2 us (40%)
  waiting for transfers between devices  16.6 us (39%)
  Pallas kernels  7.9 us (19%)
  between operations  0.72 us (2%)
    ppermute x19, starting transfers between devices, swap(): return lax.ppermute(x, axis, [(i, i ^ mask) for i in range(n)])  17.2 us
    ppermute x19, waiting for transfers between devices, swap(): return lax.ppermute(x, axis, [(i, i ^ mask) for i in range(n)])  16.6 us
    pallas_call x1, Pallas kernels, body(): call(functools.partial(attend_kernel, chips), [jax.ShapeDtypeStruct((R_DE...  2.07 us
    pallas_call x1, Pallas kernels, body(): call(functools.partial(outer_kernel, chips), [pltpu.VMEM((R_DEV * tokens,...  1.95 us
    pallas_call x1, Pallas kernels, body(): call(prep_kernel, [pltpu.VMEM((PROJ_CHANNELS * LANES, PACK * CZ), BF), pl...  1.46 us
    pallas_call x1, Pallas kernels, body(): call(functools.partial(front_kernel, adaptive, 2 * tokens), [pltpu.VMEM((...  1.09 us
  transfers between devices with their start and end apart: 19, of which 11 were waited for; matrix products, arithmetic and copies ran while one was open for 0% of the time, Pallas kernels for 5%

profile of v6, /device:TPU:0, one launch (start us, length us, event | category | flops | bytes accessed | tf_op | source)
XLA Modules:
  0.0 42.5 jit_solution(2684613141267775990)
XLA Ops:
  0.6 1.1 %shard_map.113 = (bf16[128,1024]{1,0:T(8,128)(2,1)S(1)}, bf16[128,1024]{1,0:T(8,128)(2,1)S(1)}, s32[8]{0:T(128)S(4)}, s32[1]{0:T(128)S(4)}) custom-call(bf16[256,1024]{1,0:T(8,128)(2,1)} %left_ref.1, s32[4]{0:T(128)} %starts_ref.1), custom_call_target="tpu_custom_call" | custom-call | bytes 1048576 | tf_op jit(solution)/shard_map/pallas_call | solution.py:333
  1.7 0.6 %collective-permute-start.15 = (bf16[128,1024]{1,0:T(8,128)(2,1)S(1)}, bf16[128,1024]{1,0:T(8,128)(2,1)S(1)}, u32[]{:S(2)}, u32[]{:S(2)}) collective-permute-start(bf16[128,1024]{1,0:T(8,128)(2,1)S(1)} %get-tuple-element.112), channel_id=1, source_target_pairs={{0,1},{1,0},{2,3},{3,2},{4,5},{5,4},{6,7},{7,6},{8,9},{9,8},{10,11... | collective-permute-start | bytes 786440 | tf_op jit(solution)/shard_map/ppermute | solution.py:305
  2.3 1.2 %collective-permute-done.15.recv_ref = bf16[128,1024]{1,0:T(8,128)(2,1)S(1)} collective-permute-done((bf16[128,1024]{1,0:T(8,128)(2,1)S(1)}, bf16[128,1024]{1,0:T(8,128)(2,1)S(1)}, u32[]{:S(2)}, u32[]{:S(2)}) %collective-permute-start.15) | collective-permute-done | bytes 262176 | tf_op jit(solution)/shard_map/ppermute | solution.py:305
  3.9 5.5 %conditional.1 = (bf16[256,128]{1,0:T(8,128)(2,1)S(1)}) conditional(s32[]{:T(128)} %bitcast, bf16[256,128]{1,0:T(8,128)(2,1)S(1)} %get-tuple-element.113, (bf16[256,128]{1,0:T(8,128)(2,1)S(1)}, bf16[256,128]{1,0:T(8,128)(2,1)S(1)}) %tuple.38, (bf16[256,128]{1,0:T(8,128)(2,1)S(1)}, ...), branch_computations={%region_0.0_spmd, %region_1.0_spmd, %region_2.0_spmd, %region_3.0_... | conditional | flops 98304 | bytes 1114240 | solution.py:407
  3.9 3.0 %collective-permute-start = (bf16[256,128]{1,0:T(8,128)(2,1)S(1)}, bf16[256,128]{1,0:T(8,128)(2,1)S(1)}, u32[]{:S(2)}, u32[]{:S(2)}) collective-permute-start(bf16[256,128]{1,0:T(8,128)(2,1)S(1)} %get-tuple-element.54), channel_id=1, source_target_pairs={{0,2},{1,3},{2,0},{3,1},{4,6},{5,7},{6,4},{7,5},{8,10},{9,11},{10,... | collective-permute-start | bytes 196616 | tf_op jit(solution)/shard_map/cond/branch_1_fun/ppermute | solution.py:305
  6.9 2.4 %collective-permute-done = bf16[256,128]{1,0:T(8,128)(2,1)S(1)} collective-permute-done((bf16[256,128]{1,0:T(8,128)(2,1)S(1)}, bf16[256,128]{1,0:T(8,128)(2,1)S(1)}, u32[]{:S(2)}, u32[]{:S(2)}) %collective-permute-start) | collective-permute-done | bytes 65568 | tf_op jit(solution)/shard_map/cond/branch_1_fun/ppermute | solution.py:305
  9.4 4.0 %collective-permute-start.18 = (bf16[256,128]{1,0:T(8,128)(2,1)S(1)}, bf16[256,128]{1,0:T(8,128)(2,1)S(1)}, u32[]{:S(2)}, u32[]{:S(2)}) collective-permute-start(bf16[256,128]{1,0:T(8,128)(2,1)S(1)} %get-tuple-element.132.refs_0_), channel_id=1, source_target_pairs={{0,6},{1,7},{2,4},{3,5},{4,2},{5,3},{6,0},{7,1},{8,14},{9,15},{10,... | collective-permute-start | bytes 196616 | tf_op jit(solution)/shard_map/ppermute | solution.py:305
  13.3 0.6 %collective-permute-start.16 = (bf16[256,128]{1,0:T(8,128)(2,1)S(1)}, bf16[256,128]{1,0:T(8,128)(2,1)S(1)}, u32[]{:S(2)}, u32[]{:S(2)}) collective-permute-start(bf16[256,128]{1,0:T(8,128)(2,1)S(1)} %get-tuple-element.132.refs_0_), channel_id=1, source_target_pairs={{0,2},{1,3},{2,0},{3,1},{4,6},{5,7},{6,4},{7,5},{8,10},{9,11},{10,... | collective-permute-start | bytes 196616 | tf_op jit(solution)/shard_map/ppermute | solution.py:305
  14.0 2.1 %collective-permute-done.18.refs_3_ = bf16[256,128]{1,0:T(8,128)(2,1)S(1)} collective-permute-done((bf16[256,128]{1,0:T(8,128)(2,1)S(1)}, bf16[256,128]{1,0:T(8,128)(2,1)S(1)}, u32[]{:S(2)}, u32[]{:S(2)}) %collective-permute-start.18) | collective-permute-done | bytes 65568 | tf_op jit(solution)/shard_map/ppermute | solution.py:305
  16.0 2.6 %collective-permute-done.17.refs_2_ = bf16[256,128]{1,0:T(8,128)(2,1)S(1)} collective-permute-done((bf16[256,128]{1,0:T(8,128)(2,1)S(1)}, bf16[256,128]{1,0:T(8,128)(2,1)S(1)}, u32[]{:S(2)}, u32[]{:S(2)}) %collective-permute-start.17) | collective-permute-done | bytes 65568 | tf_op jit(solution)/shard_map/ppermute | solution.py:305
  18.7 0.5 %collective-permute-start.20 = (bf16[256,128]{1,0:T(8,128)(2,1)S(1)}, bf16[256,128]{1,0:T(8,128)(2,1)S(1)}, u32[]{:S(2)}, u32[]{:S(2)}) collective-permute-start(bf16[256,128]{1,0:T(8,128)(2,1)S(1)} %collective-permute-done.16.refs_1_), channel_id=1, source_target_pairs={{0,1},{1,0},{2,3},{3,2},{4,5},{5,4},{6,7},{7,6},{8,9},{9,8},{10,11... | collective-permute-start | bytes 196616 | tf_op jit(solution)/shard_map/ppermute | solution.py:305
  19.2 1.5 %shard_map.115 = (bf16[4096,512]{1,0:T(8,128)(2,1)S(1)}, f32[128,256]{1,0:T(8,128)S(1)}, bf16[256,1024]{1,0:T(8,128)(2,1)S(1)}, bf16[128,512]{1,0:T(8,128)(2,1)S...) custom-call(bf16[1024,128]{1,0:T(8,128)(2,1)} %refs_0_.1, bf16[4,32,256]{2,1,0:T(8,128)(2,1)} %refs_1_.1, ...), custom_call_target="tpu_custom_call" | custom-call | flops 268435456 | bytes 1048576 | tf_op jit(solution)/shard_map/pallas_call | solution.py:346
  20.7 1.9 %shard_map.116 = (bf16[256,128]{1,0:T(8,128)(2,1)S(1)}, bf16[256,128]{1,0:T(8,128)(2,1)S(1)}, bf16[256,128]{1,0:T(8,128)(2,1)S(1)}, bf16[256,128]{1,0:T(8,128)(2,1)S(1)}) custom-call(s32[8]{0:T(128)S(4)} %get-tuple-element.109.table, bf16[256,128]{1,0:T(8,128)(2,1)S(1)} %get-tuple-element.132.refs_0_, bf16[256,128]{1,0:T(8,128)(2,1)S(1)} %collective-permute-done.16.refs_1_, ...), custom_call_target="tpu_custom_call" | custom-call | flops 2147483648 | bytes 1048576 | tf_op jit(solution)/shard_map/pallas_call | solution.py:413
  22.7 1.6 %collective-permute-start.23 = (bf16[256,128]{1,0:T(8,128)(2,1)S(1)}, bf16[256,128]{1,0:T(8,128)(2,1)S(1)}, u32[]{:S(2)}, u32[]{:S(2)}) collective-permute-start(bf16[256,128]{1,0:T(8,128)(2,1)S(1)} %get-tuple-element.120), channel_id=1, source_target_pairs={{0,8},{8,0},{16,24},{24,16},{1,9},{9,1},{17,25},{25,17},{2,10},{10... | collective-permute-start | bytes 196616 | tf_op jit(solution)/shard_map/ppermute | solution.py:305
  24.2 1.5 %collective-permute-start.24 = (bf16[256,128]{1,0:T(8,128)(2,1)S(1)}, bf16[256,128]{1,0:T(8,128)(2,1)S(1)}, u32[]{:S(2)}, u32[]{:S(2)}) collective-permute-start(bf16[256,128]{1,0:T(8,128)(2,1)S(1)} %get-tuple-element.121), channel_id=1, source_target_pairs={{0,16},{8,24},{16,0},{24,8},{1,17},{9,25},{17,1},{25,9},{2,18},{10... | collective-permute-start | bytes 196616 | tf_op jit(solution)/shard_map/ppermute | solution.py:305
  26.2 0.8 %collective-permute-done.23.refs_1_ = bf16[256,128]{1,0:T(8,128)(2,1)S(1)} collective-permute-done((bf16[256,128]{1,0:T(8,128)(2,1)S(1)}, bf16[256,128]{1,0:T(8,128)(2,1)S(1)}, u32[]{:S(2)}, u32[]{:S(2)}) %collective-permute-start.23) | collective-permute-done | bytes 65568 | tf_op jit(solution)/shard_map/ppermute | solution.py:305
  27.0 1.5 %collective-permute-done.24.refs_2_ = bf16[256,128]{1,0:T(8,128)(2,1)S(1)} collective-permute-done((bf16[256,128]{1,0:T(8,128)(2,1)S(1)}, bf16[256,128]{1,0:T(8,128)(2,1)S(1)}, u32[]{:S(2)}, u32[]{:S(2)}) %collective-permute-start.24) | collective-permute-done | bytes 65568 | tf_op jit(solution)/shard_map/ppermute | solution.py:305
  28.5 2.4 %collective-permute-done.25.refs_3_ = bf16[256,128]{1,0:T(8,128)(2,1)S(1)} collective-permute-done((bf16[256,128]{1,0:T(8,128)(2,1)S(1)}, bf16[256,128]{1,0:T(8,128)(2,1)S(1)}, u32[]{:S(2)}, u32[]{:S(2)}) %collective-permute-start.25) | collective-permute-done | bytes 65568 | tf_op jit(solution)/shard_map/ppermute | solution.py:305
  31.2 2.3 %collective-permute-start.28 = (bf16[8,32,128]{2,1,0:T(8,128)(2,1)S(1)}, bf16[8,32,128]{2,1,0:T(8,128)(2,1)S(1)}, u32[]{:S(2)}, u32[]{:S(2)}) collective-permute-start(bf16[8,32,128]{2,1,0:T(8,128)(2,1)S(1)} %get-tuple-element.124.normed_ref.refs_0_), channel_id=1, source_target_pairs={{0,6},{1,7},{2,4},{3,5},{4,2},{5,3},{6,0},{7,1},{8,14},{9,15},{10,... | collective-permute-start | bytes 196616 | tf_op jit(solution)/shard_map/ppermute | solution.py:305
  33.5 2.2 %collective-permute-start.26 = (bf16[8,32,128]{2,1,0:T(8,128)(2,1)S(1)}, bf16[8,32,128]{2,1,0:T(8,128)(2,1)S(1)}, u32[]{:S(2)}, u32[]{:S(2)}) collective-permute-start(bf16[8,32,128]{2,1,0:T(8,128)(2,1)S(1)} %get-tuple-element.124.normed_ref.refs_0_), channel_id=1, source_target_pairs={{0,2},{1,3},{2,0},{3,1},{4,6},{5,7},{6,4},{7,5},{8,10},{9,11},{10,... | collective-permute-start | bytes 196616 | tf_op jit(solution)/shard_map/ppermute | solution.py:305
  35.6 1.9 %collective-permute-done.28.refs_3_ = bf16[8,32,128]{2,1,0:T(8,128)(2,1)S(1)} collective-permute-done((bf16[8,32,128]{2,1,0:T(8,128)(2,1)S(1)}, bf16[8,32,128]{2,1,0:T(8,128)(2,1)S(1)}, u32[]{:S(2)}, u32[]{:S(2)}) %collective-permute-start.28) | collective-permute-done | bytes 65568 | tf_op jit(solution)/shard_map/ppermute | solution.py:305
  37.6 1.4 %collective-permute-done.27.refs_2_ = bf16[8,32,128]{2,1,0:T(8,128)(2,1)S(1)} collective-permute-done((bf16[8,32,128]{2,1,0:T(8,128)(2,1)S(1)}, bf16[8,32,128]{2,1,0:T(8,128)(2,1)S(1)}, u32[]{:S(2)}, u32[]{:S(2)}) %collective-permute-start.27) | collective-permute-done | bytes 65568 | tf_op jit(solution)/shard_map/ppermute | solution.py:305
  39.5 0.7 %shard_map.118 = (bf16[256,128]{1,0:T(8,128)(2,1)S(1)}, f32[256,128]{1,0:T(8,128)S(1)}, bf16[8,32,128]{2,1,0:T(8,128)(2,1)}) custom-call(bf16[8,32,128]{2,1,0:T(8,128)(2,1)S(1)} %get-tuple-element.124.normed_ref.refs_0_, bf16[128,512]{1,0:T(8,128)(2,1)S(1)} %get-tuple-element.125.w_ref.refs_10_, bf16[8,32,128]{2,1,0:T(8,128)(2,1)S(1)} %get-tuple-element.126.pair_ref), custom_call_target="tpu_custom_call" | custom-call | flops 134217728 | bytes 1048576 | tf_op jit(solution)/shard_map/pallas_call | solution.py:437
  40.4 2.1 %shard_map.119 = bf16[8,32,128]{2,1,0:T(8,128)(2,1)} custom-call(bf16[8,32,128]{2,1,0:T(8,128)(2,1)S(1)} %get-tuple-element.124.normed_ref.refs_0_, bf16[8,32,128]{2,1,0:T(8,128)(2,1)S(1)} %collective-permute-done.26.refs_1_, bf16[8,32,128]{2,1,0:T(8,128)(2,1)S(1)} %collective-permute-done.27.refs_2_, ...), custom_call_target="tpu_custom_call" | custom-call | flops 536870912 | bytes 1048576 | tf_op jit(solution)/shard_map/pallas_call | solution.py:447
  (23 shorter events, 2.0 us)
Async XLA Ops:
  1.7 1.7 %collective-permute-start.15 = (bf16[128,1024]{1,0:T(8,128)(2,1)S(1)}, bf16[128,1024]{1,0:T(8,128)(2,1)S(1)}, u32[]{:S(2)}, u32[]{:S(2)}) collective-permute-start(bf16[128,1024]{1,0:T(8,128)(2,1)S(1)} %get-tuple-element.112), channel_id=1, source_target_pairs={{0,1},{1,0},{2,3},{3,2},{4,5},{5,4},{6,7},{7,6},{8,9},{9,8},{10,11... | collective-permute-start | bytes 786440 | tf_op jit(solution)/shard_map/ppermute | solution.py:305
  3.9 5.4 %collective-permute-start = (bf16[256,128]{1,0:T(8,128)(2,1)S(1)}, bf16[256,128]{1,0:T(8,128)(2,1)S(1)}, u32[]{:S(2)}, u32[]{:S(2)}) collective-permute-start(bf16[256,128]{1,0:T(8,128)(2,1)S(1)} %get-tuple-element.54), channel_id=1, source_target_pairs={{0,2},{1,3},{2,0},{3,1},{4,6},{5,7},{6,4},{7,5},{8,10},{9,11},{10,... | collective-permute-start | bytes 196616 | tf_op jit(solution)/shard_map/cond/branch_1_fun/ppermute | solution.py:305
  9.4 6.7 %collective-permute-start.18 = (bf16[256,128]{1,0:T(8,128)(2,1)S(1)}, bf16[256,128]{1,0:T(8,128)(2,1)S(1)}, u32[]{:S(2)}, u32[]{:S(2)}) collective-permute-start(bf16[256,128]{1,0:T(8,128)(2,1)S(1)} %get-tuple-element.132.refs_0_), channel_id=1, source_target_pairs={{0,6},{1,7},{2,4},{3,5},{4,2},{5,3},{6,0},{7,1},{8,14},{9,15},{10,... | collective-permute-start | bytes 196616 | tf_op jit(solution)/shard_map/ppermute | solution.py:305
  13.3 5.4 %collective-permute-start.17 = (bf16[256,128]{1,0:T(8,128)(2,1)S(1)}, bf16[256,128]{1,0:T(8,128)(2,1)S(1)}, u32[]{:S(2)}, u32[]{:S(2)}) collective-permute-start(bf16[256,128]{1,0:T(8,128)(2,1)S(1)} %get-tuple-element.132.refs_0_), channel_id=1, source_target_pairs={{0,4},{1,5},{2,6},{3,7},{4,0},{5,1},{6,2},{7,3},{8,12},{9,13},{10,... | collective-permute-start | bytes 196616 | tf_op jit(solution)/shard_map/ppermute | solution.py:305
  13.3 5.4 %collective-permute-start.16 = (bf16[256,128]{1,0:T(8,128)(2,1)S(1)}, bf16[256,128]{1,0:T(8,128)(2,1)S(1)}, u32[]{:S(2)}, u32[]{:S(2)}) collective-permute-start(bf16[256,128]{1,0:T(8,128)(2,1)S(1)} %get-tuple-element.132.refs_0_), channel_id=1, source_target_pairs={{0,2},{1,3},{2,0},{3,1},{4,6},{5,7},{6,4},{7,5},{8,10},{9,11},{10,... | collective-permute-start | bytes 196616 | tf_op jit(solution)/shard_map/ppermute | solution.py:305
  14.0 6.7 %collective-permute-start.19 = (bf16[256,128]{1,0:T(8,128)(2,1)S(1)}, bf16[256,128]{1,0:T(8,128)(2,1)S(1)}, u32[]{:S(2)}, u32[]{:S(2)}) collective-permute-start(bf16[256,128]{1,0:T(8,128)(2,1)S(1)} %get-tuple-element.132.refs_0_), channel_id=1, source_target_pairs={{0,1},{1,0},{2,3},{3,2},{4,5},{5,4},{6,7},{7,6},{8,9},{9,8},{10,11... | collective-permute-start | bytes 196616 | tf_op jit(solution)/shard_map/ppermute | solution.py:305
  16.0 4.7 %collective-permute-start.22 = (bf16[256,128]{1,0:T(8,128)(2,1)S(1)}, bf16[256,128]{1,0:T(8,128)(2,1)S(1)}, u32[]{:S(2)}, u32[]{:S(2)}) collective-permute-start(bf16[256,128]{1,0:T(8,128)(2,1)S(1)} %collective-permute-done.18.refs_3_), channel_id=1, source_target_pairs={{0,1},{1,0},{2,3},{3,2},{4,5},{5,4},{6,7},{7,6},{8,9},{9,8},{10,11... | collective-permute-start | bytes 196616 | tf_op jit(solution)/shard_map/ppermute | solution.py:305
  18.7 2.0 %collective-permute-start.21 = (bf16[256,128]{1,0:T(8,128)(2,1)S(1)}, bf16[256,128]{1,0:T(8,128)(2,1)S(1)}, u32[]{:S(2)}, u32[]{:S(2)}) collective-permute-start(bf16[256,128]{1,0:T(8,128)(2,1)S(1)} %collective-permute-done.17.refs_2_), channel_id=1, source_target_pairs={{0,1},{1,0},{2,3},{3,2},{4,5},{5,4},{6,7},{7,6},{8,9},{9,8},{10,11... | collective-permute-start | bytes 196616 | tf_op jit(solution)/shard_map/ppermute | solution.py:305
  18.7 2.0 %collective-permute-start.20 = (bf16[256,128]{1,0:T(8,128)(2,1)S(1)}, bf16[256,128]{1,0:T(8,128)(2,1)S(1)}, u32[]{:S(2)}, u32[]{:S(2)}) collective-permute-start(bf16[256,128]{1,0:T(8,128)(2,1)S(1)} %collective-permute-done.16.refs_1_), channel_id=1, source_target_pairs={{0,1},{1,0},{2,3},{3,2},{4,5},{5,4},{6,7},{7,6},{8,9},{9,8},{10,11... | collective-permute-start | bytes 196616 | tf_op jit(solution)/shard_map/ppermute | solution.py:305
  22.7 4.3 %collective-permute-start.23 = (bf16[256,128]{1,0:T(8,128)(2,1)S(1)}, bf16[256,128]{1,0:T(8,128)(2,1)S(1)}, u32[]{:S(2)}, u32[]{:S(2)}) collective-permute-start(bf16[256,128]{1,0:T(8,128)(2,1)S(1)} %get-tuple-element.120), channel_id=1, source_target_pairs={{0,8},{8,0},{16,24},{24,16},{1,9},{9,1},{17,25},{25,17},{2,10},{10... | collective-permute-start | bytes 196616 | tf_op jit(solution)/shard_map/ppermute | solution.py:305
  24.2 4.3 %collective-permute-start.24 = (bf16[256,128]{1,0:T(8,128)(2,1)S(1)}, bf16[256,128]{1,0:T(8,128)(2,1)S(1)}, u32[]{:S(2)}, u32[]{:S(2)}) collective-permute-start(bf16[256,128]{1,0:T(8,128)(2,1)S(1)} %get-tuple-element.121), channel_id=1, source_target_pairs={{0,16},{8,24},{16,0},{24,8},{1,17},{9,25},{17,1},{25,9},{2,18},{10... | collective-permute-start | bytes 196616 | tf_op jit(solution)/shard_map/ppermute | solution.py:305
  25.8 5.2 %collective-permute-start.25 = (bf16[256,128]{1,0:T(8,128)(2,1)S(1)}, bf16[256,128]{1,0:T(8,128)(2,1)S(1)}, u32[]{:S(2)}, u32[]{:S(2)}) collective-permute-start(bf16[256,128]{1,0:T(8,128)(2,1)S(1)} %get-tuple-element.122), channel_id=1, source_target_pairs={{0,24},{8,16},{16,8},{24,0},{1,25},{9,17},{17,9},{25,1},{2,26},{10... | collective-permute-start | bytes 196616 | tf_op jit(solution)/shard_map/ppermute | solution.py:305
  31.2 6.4 %collective-permute-start.28 = (bf16[8,32,128]{2,1,0:T(8,128)(2,1)S(1)}, bf16[8,32,128]{2,1,0:T(8,128)(2,1)S(1)}, u32[]{:S(2)}, u32[]{:S(2)}) collective-permute-start(bf16[8,32,128]{2,1,0:T(8,128)(2,1)S(1)} %get-tuple-element.124.normed_ref.refs_0_), channel_id=1, source_target_pairs={{0,6},{1,7},{2,4},{3,5},{4,2},{5,3},{6,0},{7,1},{8,14},{9,15},{10,... | collective-permute-start | bytes 196616 | tf_op jit(solution)/shard_map/ppermute | solution.py:305
  33.5 5.5 %collective-permute-start.27 = (bf16[8,32,128]{2,1,0:T(8,128)(2,1)S(1)}, bf16[8,32,128]{2,1,0:T(8,128)(2,1)S(1)}, u32[]{:S(2)}, u32[]{:S(2)}) collective-permute-start(bf16[8,32,128]{2,1,0:T(8,128)(2,1)S(1)} %get-tuple-element.124.normed_ref.refs_0_), channel_id=1, source_target_pairs={{0,4},{1,5},{2,6},{3,7},{4,0},{5,1},{6,2},{7,3},{8,12},{9,13},{10,... | collective-permute-start | bytes 196616 | tf_op jit(solution)/shard_map/ppermute | solution.py:305
  33.5 5.5 %collective-permute-start.26 = (bf16[8,32,128]{2,1,0:T(8,128)(2,1)S(1)}, bf16[8,32,128]{2,1,0:T(8,128)(2,1)S(1)}, u32[]{:S(2)}, u32[]{:S(2)}) collective-permute-start(bf16[8,32,128]{2,1,0:T(8,128)(2,1)S(1)} %get-tuple-element.124.normed_ref.refs_0_), channel_id=1, source_target_pairs={{0,2},{1,3},{2,0},{3,1},{4,6},{5,7},{6,4},{7,5},{8,10},{9,11},{10,... | collective-permute-start | bytes 196616 | tf_op jit(solution)/shard_map/ppermute | solution.py:305
  35.6 4.5 %collective-permute-start.29 = (bf16[8,32,128]{2,1,0:T(8,128)(2,1)S(1)}, bf16[8,32,128]{2,1,0:T(8,128)(2,1)S(1)}, u32[]{:S(2)}, u32[]{:S(2)}) collective-permute-start(bf16[8,32,128]{2,1,0:T(8,128)(2,1)S(1)} %get-tuple-element.124.normed_ref.refs_0_), channel_id=1, source_target_pairs={{0,1},{1,0},{2,3},{3,2},{4,5},{5,4},{6,7},{7,6},{8,9},{9,8},{10,11... | collective-permute-start | bytes 196616 | tf_op jit(solution)/shard_map/ppermute | solution.py:305
  37.6 2.6 %collective-permute-start.32 = (bf16[8,32,128]{2,1,0:T(8,128)(2,1)S(1)}, bf16[8,32,128]{2,1,0:T(8,128)(2,1)S(1)}, u32[]{:S(2)}, u32[]{:S(2)}) collective-permute-start(bf16[8,32,128]{2,1,0:T(8,128)(2,1)S(1)} %collective-permute-done.28.refs_3_), channel_id=1, source_target_pairs={{0,1},{1,0},{2,3},{3,2},{4,5},{5,4},{6,7},{7,6},{8,9},{9,8},{10,11... | collective-permute-start | bytes 196616 | tf_op jit(solution)/shard_map/ppermute | solution.py:305
  39.0 1.3 %collective-permute-start.31 = (bf16[8,32,128]{2,1,0:T(8,128)(2,1)S(1)}, bf16[8,32,128]{2,1,0:T(8,128)(2,1)S(1)}, u32[]{:S(2)}, u32[]{:S(2)}) collective-permute-start(bf16[8,32,128]{2,1,0:T(8,128)(2,1)S(1)} %collective-permute-done.27.refs_2_), channel_id=1, source_target_pairs={{0,1},{1,0},{2,3},{3,2},{4,5},{5,4},{6,7},{7,6},{8,9},{9,8},{10,11... | collective-permute-start | bytes 196616 | tf_op jit(solution)/shard_map/ppermute | solution.py:305
  39.0 1.4 %collective-permute-start.30 = (bf16[8,32,128]{2,1,0:T(8,128)(2,1)S(1)}, bf16[8,32,128]{2,1,0:T(8,128)(2,1)S(1)}, u32[]{:S(2)}, u32[]{:S(2)}) collective-permute-start(bf16[8,32,128]{2,1,0:T(8,128)(2,1)S(1)} %collective-permute-done.26.refs_1_), channel_id=1, source_target_pairs={{0,1},{1,0},{2,3},{3,2},{4,5},{5,4},{6,7},{7,6},{8,9},{9,8},{10,11... | collective-permute-start | bytes 196616 | tf_op jit(solution)/shard_map/ppermute | solution.py:305

commit v7 on v6

--- a/solution.py
+++ b/solution.py
@@ -28,7 +28,7 @@
 F32 = jnp.float32
 
 
-def call(kernel, outs, specs, scratch=(), flops=0, limit=8):
+def call(kernel, outs, specs, scratch=(), flops=0, limit=8, aliases=None):
     return pl.pallas_call(
         kernel,
         out_shape=outs,
@@ -37,6 +37,7 @@
             SMEM if getattr(o, "memory_space", None) == pltpu.SMEM else VMEM for o in outs
         ],
         scratch_shapes=list(scratch),
+        input_output_aliases=aliases or {},
         compiler_params=pltpu.CompilerParams(vmem_limit_bytes=limit << 20),
         cost_estimate=pl.CostEstimate(
             flops=flops, bytes_accessed=1 << 20, transcendentals=0
@@ -57,15 +58,13 @@
     return one * 5 + two * 12 + three * 10
 
 
-def front_kernel(adaptive, chip_tokens, left_ref, starts_ref, sent_ref, kept_ref, table_ref, need_ref, raw_ref, sem):
-    half = sent_ref.shape[0]
+def front_kernel(adaptive, chip_tokens, left_ref, starts_ref, kept_ref, table_ref, need_ref, raw_ref, sem):
+    half = kept_ref.shape[0]
     core = lax.axis_index("res") % 2
-    sent_at = pl.multiple_of((1 - core) * half, half)
     kept_at = pl.multiple_of(core * half, half)
     copies = [
         pltpu.make_async_copy(starts_ref, raw_ref, sem.at[0]),
-        pltpu.make_async_copy(left_ref.at[pl.ds(sent_at, half)], sent_ref, sem.at[1]),
-        pltpu.make_async_copy(left_ref.at[pl.ds(kept_at, half)], kept_ref, sem.at[2]),
+        pltpu.make_async_copy(left_ref.at[pl.ds(kept_at, half)], kept_ref, sem.at[1]),
     ]
     for copy in copies:
         copy.start()
@@ -150,7 +149,7 @@
 def select_kernel(table, own_ref, recv_ref, *refs):
     outs, chip_ref = refs[:-1], refs[-1]
     chips = len(outs)
-    size, _ = outs[0].shape
+    size, half = outs[0].shape
     width = own_ref.shape[1]
     res = lax.axis_index("res")
     core = res % 2
@@ -158,7 +157,7 @@
     own_at = pl.multiple_of(core * width, LANES)
     recv_at = pl.multiple_of((1 - core) * width, LANES)
     chip_ref[:, pl.ds(own_at, width)] = own_ref[...]
-    chip_ref[:, pl.ds(recv_at, width)] = recv_ref[...]
+    chip_ref[:, pl.ds(recv_at, width)] = recv_ref[pl.ds(pl.multiple_of(core * half, half), half), :]
     m = lax.broadcasted_iota(jnp.int32, (size, SPAN), 0)
     lane = lax.broadcasted_iota(jnp.int32, (size, SPAN), 1)
     delta = lane - (m % R_DEV) * PROJ_CHANNELS - m // R_DEV
@@ -248,25 +247,34 @@
     gate_ref[...] = jax.nn.sigmoid(g.astype(F32))
 
 
+def near_kernel(chips, *refs):
+    near, w_ref, kv_ref = refs[:chips], refs[chips], refs[chips + 1]
+    fill(near, w_ref, kv_ref, lax.axis_index("res") % 2)
+
+
+def fill(pieces, w_ref, kv_ref, core):
+    tokens = pieces[0].shape[1]
+    z = lax.axis_index("res") // 2
+    for k, piece in enumerate(pieces):
+        at = (jnp.bitwise_xor(z, k) * 2 + core) * tokens
+        kv = jnp.dot(
+            piece[...].reshape(R_DEV * tokens, CZ),
+            w_ref[:, CZ : 3 * CZ],
+            preferred_element_type=F32,
+        )
+        kv_ref[:, pl.ds(pl.multiple_of(at, tokens), tokens), :] = kv.astype(BF).reshape(
+            R_DEV, tokens, 2 * CZ
+        )
+
+
 def attend_kernel(chips, *refs):
-    mine, theirs = refs[:chips], refs[chips : 2 * chips]
-    q_ref, gate_ref, w_ref, wo_ref, bias_ref, out_ref = refs[2 * chips : -4]
-    all_ref, kv_ref, scores_ref, gated_ref = refs[-4:]
-    tokens = mine[0].shape[1]
-    z = lax.axis_index("res") // 2
-    core = lax.axis_index("res") % 2
-    for k in range(chips):
-        chip = jnp.bitwise_xor(z, k) * 2
-        mine_at = pl.multiple_of((chip + core) * tokens, tokens)
-        theirs_at = pl.multiple_of((chip + 1 - core) * tokens, tokens)
-        all_ref[:, pl.ds(mine_at, tokens), :] = mine[k][...]
-        all_ref[:, pl.ds(theirs_at, tokens), :] = theirs[k][...]
+    far = refs[:chips]
+    _, q_ref, gate_ref, w_ref, wo_ref, bias_ref, out_ref, kv_ref = refs[chips:-2]
+    scores_ref, gated_ref = refs[-2:]
+    tokens = far[0].shape[1]
+    fill(far, w_ref, kv_ref, 1 - lax.axis_index("res") % 2)
     scale = DH ** (-0.5)
     lane_head = lax.broadcasted_iota(jnp.int32, (tokens, CZ), 1) // DH
-    kv = jnp.dot(
-        all_ref[...].reshape(-1, CZ), w_ref[:, CZ : 3 * CZ], preferred_element_type=F32
-    )
-    kv_ref[...] = kv.astype(BF).reshape(kv_ref.shape)
     for u in range(R_DEV):
         q = q_ref[u * tokens : (u + 1) * tokens, :]
         spread = jnp.concatenate(
@@ -330,18 +338,17 @@
     rows = groups * R_DEV
 
     adaptive = chips == groups == 4
-    sent, kept, table, need = call(
+    kept, table, need = call(
         functools.partial(front_kernel, adaptive, 2 * tokens),
         [
-            pltpu.VMEM((half, width), BF),
             pltpu.VMEM((half, width), BF),
             pltpu.SMEM((2 * groups,), jnp.int32),
             pltpu.SMEM((1,), jnp.int32),
         ],
         [ANY, ANY],
-        [pltpu.SMEM(window_starts.shape, jnp.int32), pltpu.SemaphoreType.DMA((3,))],
+        [pltpu.SMEM(window_starts.shape, jnp.int32), pltpu.SemaphoreType.DMA((2,))],
     )(*in_hbm(alignment_left, window_starts))
-    recv = swap(sent, "res", 1)
+    recv = swap(alignment_left, "res", 1)
 
     wbd, bias, right, qkvg, wo, shift = call(
         prep_kernel,
@@ -444,19 +451,22 @@
         [VMEM] * 3,
         flops=1 << 27,
     )(normed, qkvg, pair)
-    (update,) = call(
+    kv = pltpu.VMEM((R_DEV, keys, 2 * CZ), BF)
+    (half_kv,) = call(
+        functools.partial(near_kernel, chips), [kv], [VMEM] * (chips + 1), flops=1 << 28
+    )(*near, qkvg)
+    update, _ = call(
         functools.partial(attend_kernel, chips),
-        [jax.ShapeDtypeStruct((R_DEV, tokens, CZ), BF)],
-        [VMEM] * (2 * chips + 5),
-        [
-            pltpu.VMEM((R_DEV, keys, CZ), BF),
-            pltpu.VMEM((R_DEV, keys, 2 * CZ), BF),
+        [jax.ShapeDtypeStruct((R_DEV, tokens, CZ), BF), kv],
+        [VMEM] * (chips + 6),
+        [
             pltpu.VMEM((R_DEV, H * tokens, keys), F32),
             pltpu.VMEM((R_DEV * tokens, CZ), BF),
         ],
         flops=1 << 29,
         limit=24,
-    )(*near, *far, queries, gate, qkvg, wo, bias)
+        aliases={chips: 1},
+    )(*far, half_kv, queries, gate, qkvg, wo, bias)
     return (pair_strip, update)
 
 

time: 42.6 us -> 41.8 us (0.981)
  waiting for transfers between devices: 16.6 us -> 15.8 us
    ppermute x19, waiting for transfers between devices: 16.6 us -> 15.8 us  [swap(): return lax.ppermute(x, axis, [(i, i ^ mask) for i in range(n)])]
  transfers between devices with their start and end apart: 19 -> 19, of which waited for: 11 -> 9; matrix products, arithmetic and copies ran while one was open for 0% -> 0% of each run, Pallas kernels for 5% -> 8%
where the time goes in v7:
time: 41.8 us; the launch traced here: 41.6 us
  starting transfers between devices  17.2 us (41%)
  waiting for transfers between devices  15.8 us (38%)
  Pallas kernels  7.75 us (19%)
  between operations  0.77 us (2%)
    ppermute x19, starting transfers between devices, swap(): return lax.ppermute(x, axis, [(i, i ^ mask) for i in range(n)])  17.2 us
    ppermute x19, waiting for transfers between devices, swap(): return lax.ppermute(x, axis, [(i, i ^ mask) for i in range(n)])  15.8 us
    pallas_call x1, Pallas kernels, body(): call(functools.partial(outer_kernel, chips), [pltpu.VMEM((R_DEV * tokens,...  1.94 us
    pallas_call x1, Pallas kernels, body(): call(functools.partial(attend_kernel, chips), [jax.ShapeDtypeStruct((R_DE...  1.66 us
    pallas_call x1, Pallas kernels, body(): call(prep_kernel, [pltpu.VMEM((PROJ_CHANNELS * LANES, PACK * CZ), BF), pl...  1.46 us
    pallas_call x1, Pallas kernels, body(): call(functools.partial(front_kernel, adaptive, 2 * tokens), [pltpu.VMEM((...  1.08 us
  transfers between devices with their start and end apart: 19, of which 9 were waited for; matrix products, arithmetic and copies ran while one was open for 0% of the time, Pallas kernels for 8%

profile of v7, /device:TPU:0, one launch (start us, length us, event | category | flops | bytes accessed | tf_op | source)
XLA Modules:
  0.0 41.6 jit_solution(6311761263585131599)
XLA Ops:
  0.6 0.6 %collective-permute-start.15 = (bf16[256,1024]{1,0:T(8,128)(2,1)}, bf16[256,1024]{1,0:T(8,128)(2,1)S(1)}, u32[]{:S(2)}, u32[]{:S(2)}) collective-permute-start(bf16[256,1024]{1,0:T(8,128)(2,1)} %left_ref.1), channel_id=1, source_target_pairs={{0,1},{1,0},{2,3},{3,2},{4,5},{5,4},{6,7},{7,6},{8,9},{9,8},{10,11... | collective-permute-start | bytes 1572872 | tf_op jit(solution)/shard_map/ppermute | solution.py:313
  1.2 1.1 %shard_map.113 = (bf16[128,1024]{1,0:T(8,128)(2,1)S(1)}, s32[8]{0:T(128)S(4)}, s32[1]{0:T(128)S(4)}) custom-call(bf16[256,1024]{1,0:T(8,128)(2,1)} %left_ref.1, s32[4]{0:T(128)} %starts_ref.1), custom_call_target="tpu_custom_call" | custom-call | bytes 1048576 | tf_op jit(solution)/shard_map/pallas_call | solution.py:341
  2.3 0.7 %collective-permute-done.15.recv_ref = bf16[256,1024]{1,0:T(8,128)(2,1)S(1)} collective-permute-done((bf16[256,1024]{1,0:T(8,128)(2,1)}, bf16[256,1024]{1,0:T(8,128)(2,1)S(1)}, u32[]{:S(2)}, u32[]{:S(2)}) %collective-permute-start.15) | collective-permute-done | bytes 524320 | tf_op jit(solution)/shard_map/ppermute | solution.py:313
  3.4 5.5 %conditional.1 = (bf16[256,128]{1,0:T(8,128)(2,1)S(1)}) conditional(s32[]{:T(128)} %bitcast, bf16[256,128]{1,0:T(8,128)(2,1)S(1)} %get-tuple-element.112, (bf16[256,128]{1,0:T(8,128)(2,1)S(1)}, bf16[256,128]{1,0:T(8,128)(2,1)S(1)}) %tuple.38, (bf16[256,128]{1,0:T(8,128)(2,1)S(1)}, ...), branch_computations={%region_0.0_spmd, %region_1.0_spmd, %region_2.0_spmd, %region_3.0_... | conditional | flops 98304 | bytes 1114240 | solution.py:414
  3.4 3.0 %collective-permute-start = (bf16[256,128]{1,0:T(8,128)(2,1)S(1)}, bf16[256,128]{1,0:T(8,128)(2,1)S(1)}, u32[]{:S(2)}, u32[]{:S(2)}) collective-permute-start(bf16[256,128]{1,0:T(8,128)(2,1)S(1)} %get-tuple-element.54), channel_id=1, source_target_pairs={{0,2},{1,3},{2,0},{3,1},{4,6},{5,7},{6,4},{7,5},{8,10},{9,11},{10,... | collective-permute-start | bytes 196616 | tf_op jit(solution)/shard_map/cond/branch_1_fun/ppermute | solution.py:313
  6.4 2.4 %collective-permute-done = bf16[256,128]{1,0:T(8,128)(2,1)S(1)} collective-permute-done((bf16[256,128]{1,0:T(8,128)(2,1)S(1)}, bf16[256,128]{1,0:T(8,128)(2,1)S(1)}, u32[]{:S(2)}, u32[]{:S(2)}) %collective-permute-start) | collective-permute-done | bytes 65568 | tf_op jit(solution)/shard_map/cond/branch_1_fun/ppermute | solution.py:313
  8.9 4.0 %collective-permute-start.18 = (bf16[256,128]{1,0:T(8,128)(2,1)S(1)}, bf16[256,128]{1,0:T(8,128)(2,1)S(1)}, u32[]{:S(2)}, u32[]{:S(2)}) collective-permute-start(bf16[256,128]{1,0:T(8,128)(2,1)S(1)} %get-tuple-element.132.refs_0_), channel_id=1, source_target_pairs={{0,6},{1,7},{2,4},{3,5},{4,2},{5,3},{6,0},{7,1},{8,14},{9,15},{10,... | collective-permute-start | bytes 196616 | tf_op jit(solution)/shard_map/ppermute | solution.py:313
  12.8 0.6 %collective-permute-start.16 = (bf16[256,128]{1,0:T(8,128)(2,1)S(1)}, bf16[256,128]{1,0:T(8,128)(2,1)S(1)}, u32[]{:S(2)}, u32[]{:S(2)}) collective-permute-start(bf16[256,128]{1,0:T(8,128)(2,1)S(1)} %get-tuple-element.132.refs_0_), channel_id=1, source_target_pairs={{0,2},{1,3},{2,0},{3,1},{4,6},{5,7},{6,4},{7,5},{8,10},{9,11},{10,... | collective-permute-start | bytes 196616 | tf_op jit(solution)/shard_map/ppermute | solution.py:313
  13.5 2.1 %collective-permute-done.18.refs_3_ = bf16[256,128]{1,0:T(8,128)(2,1)S(1)} collective-permute-done((bf16[256,128]{1,0:T(8,128)(2,1)S(1)}, bf16[256,128]{1,0:T(8,128)(2,1)S(1)}, u32[]{:S(2)}, u32[]{:S(2)}) %collective-permute-start.18) | collective-permute-done | bytes 65568 | tf_op jit(solution)/shard_map/ppermute | solution.py:313
  15.5 2.6 %collective-permute-done.17.refs_2_ = bf16[256,128]{1,0:T(8,128)(2,1)S(1)} collective-permute-done((bf16[256,128]{1,0:T(8,128)(2,1)S(1)}, bf16[256,128]{1,0:T(8,128)(2,1)S(1)}, u32[]{:S(2)}, u32[]{:S(2)}) %collective-permute-start.17) | collective-permute-done | bytes 65568 | tf_op jit(solution)/shard_map/ppermute | solution.py:313
  18.2 0.5 %collective-permute-start.20 = (bf16[256,128]{1,0:T(8,128)(2,1)S(1)}, bf16[256,128]{1,0:T(8,128)(2,1)S(1)}, u32[]{:S(2)}, u32[]{:S(2)}) collective-permute-start(bf16[256,128]{1,0:T(8,128)(2,1)S(1)} %collective-permute-done.16.refs_1_), channel_id=1, source_target_pairs={{0,1},{1,0},{2,3},{3,2},{4,5},{5,4},{6,7},{7,6},{8,9},{9,8},{10,11... | collective-permute-start | bytes 196616 | tf_op jit(solution)/shard_map/ppermute | solution.py:313
  18.7 1.5 %shard_map.115 = (bf16[4096,512]{1,0:T(8,128)(2,1)S(1)}, f32[128,256]{1,0:T(8,128)S(1)}, bf16[256,1024]{1,0:T(8,128)(2,1)S(1)}, bf16[128,512]{1,0:T(8,128)(2,1)S...) custom-call(bf16[1024,128]{1,0:T(8,128)(2,1)} %refs_0_.1, bf16[4,32,256]{2,1,0:T(8,128)(2,1)} %refs_1_.1, ...), custom_call_target="tpu_custom_call" | custom-call | flops 268435456 | bytes 1048576 | tf_op jit(solution)/shard_map/pallas_call | solution.py:353
  20.2 1.9 %shard_map.116 = (bf16[256,128]{1,0:T(8,128)(2,1)S(1)}, bf16[256,128]{1,0:T(8,128)(2,1)S(1)}, bf16[256,128]{1,0:T(8,128)(2,1)S(1)}, bf16[256,128]{1,0:T(8,128)(2,1)S(1)}) custom-call(s32[8]{0:T(128)S(4)} %get-tuple-element.109.table, bf16[256,128]{1,0:T(8,128)(2,1)S(1)} %get-tuple-element.132.refs_0_, bf16[256,128]{1,0:T(8,128)(2,1)S(1)} %collective-permute-done.16.refs_1_, ...), custom_call_target="tpu_custom_call" | custom-call | flops 2147483648 | bytes 1048576 | tf_op jit(solution)/shard_map/pallas_call | solution.py:420
  22.2 1.6 %collective-permute-start.23 = (bf16[256,128]{1,0:T(8,128)(2,1)S(1)}, bf16[256,128]{1,0:T(8,128)(2,1)S(1)}, u32[]{:S(2)}, u32[]{:S(2)}) collective-permute-start(bf16[256,128]{1,0:T(8,128)(2,1)S(1)} %get-tuple-element.119), channel_id=1, source_target_pairs={{0,8},{8,0},{16,24},{24,16},{1,9},{9,1},{17,25},{25,17},{2,10},{10... | collective-permute-start | bytes 196616 | tf_op jit(solution)/shard_map/ppermute | solution.py:313
  23.7 1.5 %collective-permute-start.24 = (bf16[256,128]{1,0:T(8,128)(2,1)S(1)}, bf16[256,128]{1,0:T(8,128)(2,1)S(1)}, u32[]{:S(2)}, u32[]{:S(2)}) collective-permute-start(bf16[256,128]{1,0:T(8,128)(2,1)S(1)} %get-tuple-element.120), channel_id=1, source_target_pairs={{0,16},{8,24},{16,0},{24,8},{1,17},{9,25},{17,1},{25,9},{2,18},{10... | collective-permute-start | bytes 196616 | tf_op jit(solution)/shard_map/ppermute | solution.py:313
  25.7 0.8 %collective-permute-done.23.refs_1_ = bf16[256,128]{1,0:T(8,128)(2,1)S(1)} collective-permute-done((bf16[256,128]{1,0:T(8,128)(2,1)S(1)}, bf16[256,128]{1,0:T(8,128)(2,1)S(1)}, u32[]{:S(2)}, u32[]{:S(2)}) %collective-permute-start.23) | collective-permute-done | bytes 65568 | tf_op jit(solution)/shard_map/ppermute | solution.py:313
  26.5 1.5 %collective-permute-done.24.refs_2_ = bf16[256,128]{1,0:T(8,128)(2,1)S(1)} collective-permute-done((bf16[256,128]{1,0:T(8,128)(2,1)S(1)}, bf16[256,128]{1,0:T(8,128)(2,1)S(1)}, u32[]{:S(2)}, u32[]{:S(2)}) %collective-permute-start.24) | collective-permute-done | bytes 65568 | tf_op jit(solution)/shard_map/ppermute | solution.py:313
  28.0 2.4 %collective-permute-done.25.refs_3_ = bf16[256,128]{1,0:T(8,128)(2,1)S(1)} collective-permute-done((bf16[256,128]{1,0:T(8,128)(2,1)S(1)}, bf16[256,128]{1,0:T(8,128)(2,1)S(1)}, u32[]{:S(2)}, u32[]{:S(2)}) %collective-permute-start.25) | collective-permute-done | bytes 65568 | tf_op jit(solution)/shard_map/ppermute | solution.py:313
  30.7 2.3 %collective-permute-start.31 = (bf16[8,32,128]{2,1,0:T(8,128)(2,1)S(1)}, bf16[8,32,128]{2,1,0:T(8,128)(2,1)S(1)}, u32[]{:S(2)}, u32[]{:S(2)}) collective-permute-start(bf16[8,32,128]{2,1,0:T(8,128)(2,1)S(1)} %get-tuple-element.123.normed_ref.refs_0_), channel_id=1, source_target_pairs={{0,6},{1,7},{2,4},{3,5},{4,2},{5,3},{6,0},{7,1},{8,14},{9,15},{10,... | collective-permute-start | bytes 196616 | tf_op jit(solution)/shard_map/ppermute | solution.py:313
  33.0 2.2 %collective-permute-start.27 = (bf16[8,32,128]{2,1,0:T(8,128)(2,1)S(1)}, bf16[8,32,128]{2,1,0:T(8,128)(2,1)S(1)}, u32[]{:S(2)}, u32[]{:S(2)}) collective-permute-start(bf16[8,32,128]{2,1,0:T(8,128)(2,1)S(1)} %get-tuple-element.123.normed_ref.refs_0_), channel_id=1, source_target_pairs={{0,2},{1,3},{2,0},{3,1},{4,6},{5,7},{6,4},{7,5},{8,10},{9,11},{10,... | collective-permute-start | bytes 196616 | tf_op jit(solution)/shard_map/ppermute | solution.py:313
  35.1 1.9 %collective-permute-done.31.refs_3_ = bf16[8,32,128]{2,1,0:T(8,128)(2,1)S(1)} collective-permute-done((bf16[8,32,128]{2,1,0:T(8,128)(2,1)S(1)}, bf16[8,32,128]{2,1,0:T(8,128)(2,1)S(1)}, u32[]{:S(2)}, u32[]{:S(2)}) %collective-permute-start.31) | collective-permute-done | bytes 65568 | tf_op jit(solution)/shard_map/ppermute | solution.py:313
  37.1 1.4 %collective-permute-done.29.refs_2_ = bf16[8,32,128]{2,1,0:T(8,128)(2,1)S(1)} collective-permute-done((bf16[8,32,128]{2,1,0:T(8,128)(2,1)S(1)}, bf16[8,32,128]{2,1,0:T(8,128)(2,1)S(1)}, u32[]{:S(2)}, u32[]{:S(2)}) %collective-permute-start.29) | collective-permute-done | bytes 65568 | tf_op jit(solution)/shard_map/ppermute | solution.py:313
  39.0 0.7 %shard_map.118 = (bf16[256,128]{1,0:T(8,128)(2,1)S(1)}, f32[256,128]{1,0:T(8,128)S(1)}, bf16[8,32,128]{2,1,0:T(8,128)(2,1)}) custom-call(bf16[8,32,128]{2,1,0:T(8,128)(2,1)S(1)} %get-tuple-element.123.normed_ref.refs_0_, bf16[128,512]{1,0:T(8,128)(2,1)S(1)} %get-tuple-element.124.w_ref.refs_4_.refs_7_, bf16[8,32,128]{2,1,0:T(8,128)(2,1)S(1)} %get-tuple-element.125.pair_ref), custom_call_target="tpu_custom_call" | custom-call | flops 134217728 | bytes 1048576 | tf_op jit(solution)/shard_map/pallas_call | solution.py:444
  40.0 1.7 %shard_map.120 = (bf16[8,32,128]{2,1,0:T(8,128)(2,1)}, bf16[8,256,256]{2,1,0:T(8,128)(2,1)S(1)}) custom-call(bf16[8,32,128]{2,1,0:T(8,128)(2,1)S(1)} %collective-permute-done.26.refs_0_, bf16[8,32,128]{2,1,0:T(8,128)(2,1)S(1)} %collective-permute-done.28.refs_1_, ...), custom_call_target="tpu_custom_call", output_to_operand_aliasing={{1}: (4, {})} | custom-call | flops 536870912 | bytes 1048576 | tf_op jit(solution)/shard_map/pallas_call | solution.py:458
  (24 shorter events, 2.0 us)
Async XLA Ops:
  0.6 2.3 %collective-permute-start.15 = (bf16[256,1024]{1,0:T(8,128)(2,1)}, bf16[256,1024]{1,0:T(8,128)(2,1)S(1)}, u32[]{:S(2)}, u32[]{:S(2)}) collective-permute-start(bf16[256,1024]{1,0:T(8,128)(2,1)} %left_ref.1), channel_id=1, source_target_pairs={{0,1},{1,0},{2,3},{3,2},{4,5},{5,4},{6,7},{7,6},{8,9},{9,8},{10,11... | collective-permute-start | bytes 1572872 | tf_op jit(solution)/shard_map/ppermute | solution.py:313
  3.4 5.4 %collective-permute-start = (bf16[256,128]{1,0:T(8,128)(2,1)S(1)}, bf16[256,128]{1,0:T(8,128)(2,1)S(1)}, u32[]{:S(2)}, u32[]{:S(2)}) collective-permute-start(bf16[256,128]{1,0:T(8,128)(2,1)S(1)} %get-tuple-element.54), channel_id=1, source_target_pairs={{0,2},{1,3},{2,0},{3,1},{4,6},{5,7},{6,4},{7,5},{8,10},{9,11},{10,... | collective-permute-start | bytes 196616 | tf_op jit(solution)/shard_map/cond/branch_1_fun/ppermute | solution.py:313
  8.9 6.7 %collective-permute-start.18 = (bf16[256,128]{1,0:T(8,128)(2,1)S(1)}, bf16[256,128]{1,0:T(8,128)(2,1)S(1)}, u32[]{:S(2)}, u32[]{:S(2)}) collective-permute-start(bf16[256,128]{1,0:T(8,128)(2,1)S(1)} %get-tuple-element.132.refs_0_), channel_id=1, source_target_pairs={{0,6},{1,7},{2,4},{3,5},{4,2},{5,3},{6,0},{7,1},{8,14},{9,15},{10,... | collective-permute-start | bytes 196616 | tf_op jit(solution)/shard_map/ppermute | solution.py:313
  12.8 5.4 %collective-permute-start.17 = (bf16[256,128]{1,0:T(8,128)(2,1)S(1)}, bf16[256,128]{1,0:T(8,128)(2,1)S(1)}, u32[]{:S(2)}, u32[]{:S(2)}) collective-permute-start(bf16[256,128]{1,0:T(8,128)(2,1)S(1)} %get-tuple-element.132.refs_0_), channel_id=1, source_target_pairs={{0,4},{1,5},{2,6},{3,7},{4,0},{5,1},{6,2},{7,3},{8,12},{9,13},{10,... | collective-permute-start | bytes 196616 | tf_op jit(solution)/shard_map/ppermute | solution.py:313
  12.8 5.4 %collective-permute-start.16 = (bf16[256,128]{1,0:T(8,128)(2,1)S(1)}, bf16[256,128]{1,0:T(8,128)(2,1)S(1)}, u32[]{:S(2)}, u32[]{:S(2)}) collective-permute-start(bf16[256,128]{1,0:T(8,128)(2,1)S(1)} %get-tuple-element.132.refs_0_), channel_id=1, source_target_pairs={{0,2},{1,3},{2,0},{3,1},{4,6},{5,7},{6,4},{7,5},{8,10},{9,11},{10,... | collective-permute-start | bytes 196616 | tf_op jit(solution)/shard_map/ppermute | solution.py:313
  13.5 6.7 %collective-permute-start.19 = (bf16[256,128]{1,0:T(8,128)(2,1)S(1)}, bf16[256,128]{1,0:T(8,128)(2,1)S(1)}, u32[]{:S(2)}, u32[]{:S(2)}) collective-permute-start(bf16[256,128]{1,0:T(8,128)(2,1)S(1)} %get-tuple-element.132.refs_0_), channel_id=1, source_target_pairs={{0,1},{1,0},{2,3},{3,2},{4,5},{5,4},{6,7},{7,6},{8,9},{9,8},{10,11... | collective-permute-start | bytes 196616 | tf_op jit(solution)/shard_map/ppermute | solution.py:313
  15.5 4.7 %collective-permute-start.22 = (bf16[256,128]{1,0:T(8,128)(2,1)S(1)}, bf16[256,128]{1,0:T(8,128)(2,1)S(1)}, u32[]{:S(2)}, u32[]{:S(2)}) collective-permute-start(bf16[256,128]{1,0:T(8,128)(2,1)S(1)} %collective-permute-done.18.refs_3_), channel_id=1, source_target_pairs={{0,1},{1,0},{2,3},{3,2},{4,5},{5,4},{6,7},{7,6},{8,9},{9,8},{10,11... | collective-permute-start | bytes 196616 | tf_op jit(solution)/shard_map/ppermute | solution.py:313
  18.2 2.0 %collective-permute-start.21 = (bf16[256,128]{1,0:T(8,128)(2,1)S(1)}, bf16[256,128]{1,0:T(8,128)(2,1)S(1)}, u32[]{:S(2)}, u32[]{:S(2)}) collective-permute-start(bf16[256,128]{1,0:T(8,128)(2,1)S(1)} %collective-permute-done.17.refs_2_), channel_id=1, source_target_pairs={{0,1},{1,0},{2,3},{3,2},{4,5},{5,4},{6,7},{7,6},{8,9},{9,8},{10,11... | collective-permute-start | bytes 196616 | tf_op jit(solution)/shard_map/ppermute | solution.py:313
  18.2 2.0 %collective-permute-start.20 = (bf16[256,128]{1,0:T(8,128)(2,1)S(1)}, bf16[256,128]{1,0:T(8,128)(2,1)S(1)}, u32[]{:S(2)}, u32[]{:S(2)}) collective-permute-start(bf16[256,128]{1,0:T(8,128)(2,1)S(1)} %collective-permute-done.16.refs_1_), channel_id=1, source_target_pairs={{0,1},{1,0},{2,3},{3,2},{4,5},{5,4},{6,7},{7,6},{8,9},{9,8},{10,11... | collective-permute-start | bytes 196616 | tf_op jit(solution)/shard_map/ppermute | solution.py:313
  22.2 4.3 %collective-permute-start.23 = (bf16[256,128]{1,0:T(8,128)(2,1)S(1)}, bf16[256,128]{1,0:T(8,128)(2,1)S(1)}, u32[]{:S(2)}, u32[]{:S(2)}) collective-permute-start(bf16[256,128]{1,0:T(8,128)(2,1)S(1)} %get-tuple-element.119), channel_id=1, source_target_pairs={{0,8},{8,0},{16,24},{24,16},{1,9},{9,1},{17,25},{25,17},{2,10},{10... | collective-permute-start | bytes 196616 | tf_op jit(solution)/shard_map/ppermute | solution.py:313
  23.7 4.3 %collective-permute-start.24 = (bf16[256,128]{1,0:T(8,128)(2,1)S(1)}, bf16[256,128]{1,0:T(8,128)(2,1)S(1)}, u32[]{:S(2)}, u32[]{:S(2)}) collective-permute-start(bf16[256,128]{1,0:T(8,128)(2,1)S(1)} %get-tuple-element.120), channel_id=1, source_target_pairs={{0,16},{8,24},{16,0},{24,8},{1,17},{9,25},{17,1},{25,9},{2,18},{10... | collective-permute-start | bytes 196616 | tf_op jit(solution)/shard_map/ppermute | solution.py:313
  25.2 5.2 %collective-permute-start.25 = (bf16[256,128]{1,0:T(8,128)(2,1)S(1)}, bf16[256,128]{1,0:T(8,128)(2,1)S(1)}, u32[]{:S(2)}, u32[]{:S(2)}) collective-permute-start(bf16[256,128]{1,0:T(8,128)(2,1)S(1)} %get-tuple-element.121), channel_id=1, source_target_pairs={{0,24},{8,16},{16,8},{24,0},{1,25},{9,17},{17,9},{25,1},{2,26},{10... | collective-permute-start | bytes 196616 | tf_op jit(solution)/shard_map/ppermute | solution.py:313
  30.7 6.4 %collective-permute-start.31 = (bf16[8,32,128]{2,1,0:T(8,128)(2,1)S(1)}, bf16[8,32,128]{2,1,0:T(8,128)(2,1)S(1)}, u32[]{:S(2)}, u32[]{:S(2)}) collective-permute-start(bf16[8,32,128]{2,1,0:T(8,128)(2,1)S(1)} %get-tuple-element.123.normed_ref.refs_0_), channel_id=1, source_target_pairs={{0,6},{1,7},{2,4},{3,5},{4,2},{5,3},{6,0},{7,1},{8,14},{9,15},{10,... | collective-permute-start | bytes 196616 | tf_op jit(solution)/shard_map/ppermute | solution.py:313
  33.0 5.5 %collective-permute-start.29 = (bf16[8,32,128]{2,1,0:T(8,128)(2,1)S(1)}, bf16[8,32,128]{2,1,0:T(8,128)(2,1)S(1)}, u32[]{:S(2)}, u32[]{:S(2)}) collective-permute-start(bf16[8,32,128]{2,1,0:T(8,128)(2,1)S(1)} %get-tuple-element.123.normed_ref.refs_0_), channel_id=1, source_target_pairs={{0,4},{1,5},{2,6},{3,7},{4,0},{5,1},{6,2},{7,3},{8,12},{9,13},{10,... | collective-permute-start | bytes 196616 | tf_op jit(solution)/shard_map/ppermute | solution.py:313
  33.0 5.5 %collective-permute-start.27 = (bf16[8,32,128]{2,1,0:T(8,128)(2,1)S(1)}, bf16[8,32,128]{2,1,0:T(8,128)(2,1)S(1)}, u32[]{:S(2)}, u32[]{:S(2)}) collective-permute-start(bf16[8,32,128]{2,1,0:T(8,128)(2,1)S(1)} %get-tuple-element.123.normed_ref.refs_0_), channel_id=1, source_target_pairs={{0,2},{1,3},{2,0},{3,1},{4,6},{5,7},{6,4},{7,5},{8,10},{9,11},{10,... | collective-permute-start | bytes 196616 | tf_op jit(solution)/shard_map/ppermute | solution.py:313
  35.1 4.8 %collective-permute-start.26 = (bf16[8,32,128]{2,1,0:T(8,128)(2,1)S(1)}, bf16[8,32,128]{2,1,0:T(8,128)(2,1)S(1)}, u32[]{:S(2)}, u32[]{:S(2)}) collective-permute-start(bf16[8,32,128]{2,1,0:T(8,128)(2,1)S(1)} %get-tuple-element.123.normed_ref.refs_0_), channel_id=1, source_target_pairs={{0,1},{1,0},{2,3},{3,2},{4,5},{5,4},{6,7},{7,6},{8,9},{9,8},{10,11... | collective-permute-start | bytes 196616 | tf_op jit(solution)/shard_map/ppermute | solution.py:313
  37.0 2.9 %collective-permute-start.32 = (bf16[8,32,128]{2,1,0:T(8,128)(2,1)S(1)}, bf16[8,32,128]{2,1,0:T(8,128)(2,1)S(1)}, u32[]{:S(2)}, u32[]{:S(2)}) collective-permute-start(bf16[8,32,128]{2,1,0:T(8,128)(2,1)S(1)} %collective-permute-done.31.refs_3_), channel_id=1, source_target_pairs={{0,1},{1,0},{2,3},{3,2},{4,5},{5,4},{6,7},{7,6},{8,9},{9,8},{10,11... | collective-permute-start | bytes 196616 | tf_op jit(solution)/shard_map/ppermute | solution.py:313
  38.5 1.5 %collective-permute-start.30 = (bf16[8,32,128]{2,1,0:T(8,128)(2,1)S(1)}, bf16[8,32,128]{2,1,0:T(8,128)(2,1)S(1)}, u32[]{:S(2)}, u32[]{:S(2)}) collective-permute-start(bf16[8,32,128]{2,1,0:T(8,128)(2,1)S(1)} %collective-permute-done.29.refs_2_), channel_id=1, source_target_pairs={{0,1},{1,0},{2,3},{3,2},{4,5},{5,4},{6,7},{7,6},{8,9},{9,8},{10,11... | collective-permute-start | bytes 196616 | tf_op jit(solution)/shard_map/ppermute | solution.py:313
  38.5 1.5 %collective-permute-start.28 = (bf16[8,32,128]{2,1,0:T(8,128)(2,1)S(1)}, bf16[8,32,128]{2,1,0:T(8,128)(2,1)S(1)}, u32[]{:S(2)}, u32[]{:S(2)}) collective-permute-start(bf16[8,32,128]{2,1,0:T(8,128)(2,1)S(1)} %collective-permute-done.27.refs_1_), channel_id=1, source_target_pairs={{0,1},{1,0},{2,3},{3,2},{4,5},{5,4},{6,7},{7,6},{8,9},{9,8},{10,11... | collective-permute-start | bytes 196616 | tf_op jit(solution)/shard_map/ppermute | solution.py:313

commit v8 on v7

--- a/solution.py
+++ b/solution.py
@@ -115,10 +115,10 @@
 
 
 def prep_kernel(*refs):
-    sources, outs, scratch = refs[:8], refs[8:14], refs[14:]
-    wbd_ref, bias_ref = outs[:2]
+    sources, outs, scratch = refs[:8], refs[8:15], refs[15:]
+    wbd_ref, bias_ref, swapped_ref = outs[:3]
     w_ref, tri_ref, chain_ref, off_ref, sem = scratch
-    targets = [w_ref, tri_ref, chain_ref, off_ref, *outs[2:]]
+    targets = [w_ref, tri_ref, chain_ref, off_ref, *outs[3:]]
     copies = [
         pltpu.make_async_copy(a, b, sem.at[n])
         for n, (a, b) in enumerate(zip(sources, targets))
@@ -130,9 +130,17 @@
         copy.wait()
     for c in range(PROJ_CHANNELS):
         block = w_ref[c * PROJ_CHANNELS : (c + 1) * PROJ_CHANNELS, :]
-        for j in range(PACK):
-            row = c * LANES + j * PROJ_CHANNELS
-            wbd_ref[row : row + PROJ_CHANNELS, j * CZ : (j + 1) * CZ] = block
+        for part in range(2):
+            for j in range(PACK // 2):
+                row = (c // 2) * LANES + (c % 2 ^ part) * (LANES // 2) + j * PROJ_CHANNELS
+                wbd_ref[part, row : row + PROJ_CHANNELS, j * CZ : (j + 1) * CZ] = block
+    right_ref = outs[3]
+    for n in range(right_ref.shape[1] // LANES):
+        cols = slice(n * LANES, (n + 1) * LANES)
+        block = right_ref[:, cols]
+        swapped_ref[:, cols] = jnp.concatenate(
+            [block[:, LANES // 2 :], block[:, : LANES // 2]], axis=1
+        )
     tokens, keys = tri_ref.shape[1:]
     first = lax.axis_index("res") * tokens
     chain = jnp.broadcast_to(chain_ref[...], (tokens, keys))
@@ -160,16 +168,18 @@
     chip_ref[:, pl.ds(recv_at, width)] = recv_ref[pl.ds(pl.multiple_of(core * half, half), half), :]
     m = lax.broadcasted_iota(jnp.int32, (size, SPAN), 0)
     lane = lax.broadcasted_iota(jnp.int32, (size, SPAN), 1)
-    delta = lane - (m % R_DEV) * PROJ_CHANNELS - m // R_DEV
+    half_count = PROJ_CHANNELS // 2
     split = WINDOW // size
     groups = chips // split
     for k in range(chips):
         at = jnp.bitwise_xor(z, k)
-        first = at % split * (size // R_DEV)
+        place = at % split * (size // R_DEV) + m // R_DEV
+        channel = place % half_count * 2 + place // half_count
+        delta = lane - (m % R_DEV) * PROJ_CHANNELS - channel
         start = table[groups + at // split] * PROJ_CHANNELS - z * (2 * width)
         base = jnp.clip(start, 0, 2 * width - SPAN) // LANES * LANES
         base = pl.multiple_of(base, LANES)
-        pick = (delta == start + first - base).astype(F32).astype(BF)
+        pick = (delta == start - base).astype(F32).astype(BF)
         outs[k][...] = lax.dot_general(
             pick,
             chip_ref[:, pl.ds(base, SPAN)],
@@ -180,38 +190,49 @@
 
 def outer_kernel(chips, table, *refs):
     mine, theirs = refs[:chips], refs[chips : 2 * chips]
-    b_ref, wbd_ref, *outs = refs[2 * chips : -3]
-    at_ref, lhs_ref, acc_ref = refs[-3:]
+    b_ref, swapped_ref, wbd_ref, *outs = refs[2 * chips : -4]
+    at_ref, low_ref, high_ref, acc_ref = refs[-4:]
     size, half = mine[0].shape
     groups = len(outs)
+    part_rows = WINDOW // 2
     z = lax.axis_index("res") // 2
     core = lax.axis_index("res") % 2
     mine_at = pl.multiple_of(core * half, LANES)
     theirs_at = pl.multiple_of((1 - core) * half, LANES)
+    split = WINDOW // size
     for k in range(chips):
         at = jnp.bitwise_xor(z, k)
-        split = WINDOW // size
-        row = pl.multiple_of(table[at // split] * WINDOW + at % split * size, size)
-        at_ref[pl.ds(row, size), pl.ds(mine_at, half)] = mine[k][...]
-        at_ref[pl.ds(row, size), pl.ds(theirs_at, half)] = theirs[k][...]
+        window = table[at // split]
+        for n in range(size // part_rows):
+            parity = at % split * (size // part_rows) + n
+            row = pl.multiple_of((parity * groups + window) * part_rows, part_rows)
+            rows = slice(n * part_rows, (n + 1) * part_rows)
+            at_ref[pl.ds(row, part_rows), pl.ds(mine_at, half)] = mine[k][rows, :]
+            at_ref[pl.ds(row, part_rows), pl.ds(theirs_at, half)] = theirs[k][rows, :]
     width = b_ref.shape[1]
     rows = groups * R_DEV
+    pairs = PROJ_CHANNELS // 2
+    below = lax.broadcasted_iota(jnp.int32, (rows, LANES), 1) < LANES // 2
     for n in range(width // (2 * LANES)):
-        part = jnp.dot(
-            at_ref[...],
-            b_ref[:, n * 2 * LANES : (n + 1) * 2 * LANES],
-            preferred_element_type=F32,
-        ).reshape(groups, PROJ_CHANNELS, R_DEV, 2 * LANES)
-        for c in range(PROJ_CHANNELS):
+        cols = slice(n * 2 * LANES, (n + 1) * 2 * LANES)
+        shape = (groups, pairs, R_DEV, 2 * LANES)
+        middle = groups * part_rows
+        even = jnp.dot(at_ref[:middle, :], b_ref[:, cols], preferred_element_type=F32)
+        odd = jnp.dot(at_ref[middle:, :], swapped_ref[:, cols], preferred_element_type=F32)
+        even, odd = even.reshape(shape), odd.reshape(shape)
+        for c in range(pairs):
             for q in range(2):
-                slab = part[:, c, :, q * LANES : (q + 1) * LANES].reshape(rows, LANES)
-                lhs_ref[
-                    (2 * n + q) * rows : (2 * n + q + 1) * rows,
-                    c * LANES : (c + 1) * LANES,
-                ] = slab.astype(BF)
-    acc = jnp.dot(lhs_ref[...], wbd_ref[...], preferred_element_type=F32)
+                lanes = slice(q * LANES, (q + 1) * LANES)
+                x = even[:, c, :, lanes].reshape(rows, LANES)
+                y = odd[:, c, :, lanes].reshape(rows, LANES)
+                to = slice((2 * n + q) * rows, (2 * n + q + 1) * rows)
+                low_ref[to, c * LANES : (c + 1) * LANES] = jnp.where(below, x, y).astype(BF)
+                high_ref[to, c * LANES : (c + 1) * LANES] = jnp.where(below, y, x).astype(BF)
     chunks = width // LANES
-    acc_ref[...] = acc.reshape(chunks, groups, R_DEV, PACK * CZ)
+    wide = PACK * CZ // 2
+    for n, ref in enumerate((low_ref, high_ref)):
+        acc = jnp.dot(ref[...], wbd_ref[n], preferred_element_type=F32)
+        acc_ref[:, :, :, n * wide : (n + 1) * wide] = acc.reshape(chunks, groups, R_DEV, wide)
     for k in range(groups):
         g = jnp.bitwise_xor(lax.axis_index("depth"), k)
         block = acc_ref[:, g]
@@ -350,11 +371,12 @@
     )(*in_hbm(alignment_left, window_starts))
     recv = swap(alignment_left, "res", 1)
 
-    wbd, bias, right, qkvg, wo, shift = call(
+    wbd, bias, swapped, right, qkvg, wo, shift = call(
         prep_kernel,
         [
-            pltpu.VMEM((PROJ_CHANNELS * LANES, PACK * CZ), BF),
+            pltpu.VMEM((2, PROJ_CHANNELS * LANES // 2, PACK * CZ // 2), BF),
             pltpu.VMEM((H * tokens, keys), F32),
+            pltpu.VMEM(alignment_right.shape, BF),
             pltpu.VMEM(alignment_right.shape, BF),
             pltpu.VMEM(query_key_value_gate_weight.shape, BF),
             pltpu.VMEM(output_weight.shape, BF),
@@ -420,15 +442,16 @@
     partial = call(
         functools.partial(outer_kernel, chips),
         [pltpu.VMEM((R_DEV * tokens, CZ), BF)] * groups,
-        [SMEM] + [VMEM] * (2 * chips + 2),
+        [SMEM] + [VMEM] * (2 * chips + 3),
         [
             pltpu.VMEM((groups * WINDOW, seqs), BF),
-            pltpu.VMEM((rows * width // LANES, PROJ_CHANNELS * LANES), BF),
+            pltpu.VMEM((rows * width // LANES, PROJ_CHANNELS * LANES // 2), BF),
+            pltpu.VMEM((rows * width // LANES, PROJ_CHANNELS * LANES // 2), BF),
             pltpu.VMEM((width // LANES, groups, R_DEV, PACK * CZ), F32),
         ],
         flops=1 << 31,
         limit=32,
-    )(table, *mine, *theirs, right, wbd)
+    )(table, *mine, *theirs, right, swapped, wbd)
     parts = [partial[0]] + [swap(partial[k], "depth", k) for k in range(1, groups)]
 
     pair, normed = call(

time: 41.8 us -> 41.4 us (level)
    pallas_call x1, Pallas kernels: 1.94 us -> 1.43 us  [body(): call(functools.partial(outer_kernel, chips), [pltpu.VMEM((R_DEV * tokens,...]
  transfers between devices with their start and end apart: 19 -> 19, of which waited for: 9 -> 9; matrix products, arithmetic and copies ran while one was open for 0% -> 0% of each run, Pallas kernels for 8% -> 9%
where the time goes in v8:
time: 41.4 us; the launch traced here: 41.3 us
  starting transfers between devices  17.2 us (42%)
  waiting for transfers between devices  15.8 us (38%)
  Pallas kernels  7.41 us (18%)
  between operations  0.77 us (2%)
    ppermute x19, starting transfers between devices, swap(): return lax.ppermute(x, axis, [(i, i ^ mask) for i in range(n)])  17.2 us
    ppermute x19, waiting for transfers between devices, swap(): return lax.ppermute(x, axis, [(i, i ^ mask) for i in range(n)])  15.8 us
    pallas_call x1, Pallas kernels, body(): call(functools.partial(attend_kernel, chips), [jax.ShapeDtypeStruct((R_DE...  1.66 us
    pallas_call x1, Pallas kernels, body(): call(prep_kernel, [pltpu.VMEM((2, PROJ_CHANNELS * LANES // 2, PACK * CZ /...  1.63 us
    pallas_call x1, Pallas kernels, body(): call(functools.partial(outer_kernel, chips), [pltpu.VMEM((R_DEV * tokens,...  1.43 us
    pallas_call x1, Pallas kernels, body(): call(functools.partial(front_kernel, adaptive, 2 * tokens), [pltpu.VMEM((...  1.08 us
  transfers between devices with their start and end apart: 19, of which 9 were waited for; matrix products, arithmetic and copies ran while one was open for 0% of the time, Pallas kernels for 9%

profile of v8, /device:TPU:0, one launch (start us, length us, event | category | flops | bytes accessed | tf_op | source)
XLA Modules:
  0.0 41.3 jit_solution(13553888297358695335)
XLA Ops:
  0.6 0.6 %collective-permute-start.15 = (bf16[256,1024]{1,0:T(8,128)(2,1)}, bf16[256,1024]{1,0:T(8,128)(2,1)S(1)}, u32[]{:S(2)}, u32[]{:S(2)}) collective-permute-start(bf16[256,1024]{1,0:T(8,128)(2,1)} %left_ref.1), channel_id=1, source_target_pairs={{0,1},{1,0},{2,3},{3,2},{4,5},{5,4},{6,7},{7,6},{8,9},{9,8},{10,11... | collective-permute-start | bytes 1572872 | tf_op jit(solution)/shard_map/ppermute | solution.py:334
  1.2 1.1 %shard_map.113 = (bf16[128,1024]{1,0:T(8,128)(2,1)S(1)}, s32[8]{0:T(128)S(4)}, s32[1]{0:T(128)S(4)}) custom-call(bf16[256,1024]{1,0:T(8,128)(2,1)} %left_ref.1, s32[4]{0:T(128)} %starts_ref.1), custom_call_target="tpu_custom_call" | custom-call | bytes 1048576 | tf_op jit(solution)/shard_map/pallas_call | solution.py:362
  2.3 0.7 %collective-permute-done.15.recv_ref = bf16[256,1024]{1,0:T(8,128)(2,1)S(1)} collective-permute-done((bf16[256,1024]{1,0:T(8,128)(2,1)}, bf16[256,1024]{1,0:T(8,128)(2,1)S(1)}, u32[]{:S(2)}, u32[]{:S(2)}) %collective-permute-start.15) | collective-permute-done | bytes 524320 | tf_op jit(solution)/shard_map/ppermute | solution.py:334
  3.4 5.5 %conditional.1 = (bf16[256,128]{1,0:T(8,128)(2,1)S(1)}) conditional(s32[]{:T(128)} %bitcast, bf16[256,128]{1,0:T(8,128)(2,1)S(1)} %get-tuple-element.113, (bf16[256,128]{1,0:T(8,128)(2,1)S(1)}, bf16[256,128]{1,0:T(8,128)(2,1)S(1)}) %tuple.38, (bf16[256,128]{1,0:T(8,128)(2,1)S(1)}, ...), branch_computations={%region_0.0_spmd, %region_1.0_spmd, %region_2.0_spmd, %region_3.0_... | conditional | flops 98304 | bytes 1114240 | solution.py:436
  3.4 3.0 %collective-permute-start = (bf16[256,128]{1,0:T(8,128)(2,1)S(1)}, bf16[256,128]{1,0:T(8,128)(2,1)S(1)}, u32[]{:S(2)}, u32[]{:S(2)}) collective-permute-start(bf16[256,128]{1,0:T(8,128)(2,1)S(1)} %get-tuple-element.54), channel_id=1, source_target_pairs={{0,2},{1,3},{2,0},{3,1},{4,6},{5,7},{6,4},{7,5},{8,10},{9,11},{10,... | collective-permute-start | bytes 196616 | tf_op jit(solution)/shard_map/cond/branch_1_fun/ppermute | solution.py:334
  6.4 2.4 %collective-permute-done = bf16[256,128]{1,0:T(8,128)(2,1)S(1)} collective-permute-done((bf16[256,128]{1,0:T(8,128)(2,1)S(1)}, bf16[256,128]{1,0:T(8,128)(2,1)S(1)}, u32[]{:S(2)}, u32[]{:S(2)}) %collective-permute-start) | collective-permute-done | bytes 65568 | tf_op jit(solution)/shard_map/cond/branch_1_fun/ppermute | solution.py:334
  8.9 3.9 %collective-permute-start.18 = (bf16[256,128]{1,0:T(8,128)(2,1)S(1)}, bf16[256,128]{1,0:T(8,128)(2,1)S(1)}, u32[]{:S(2)}, u32[]{:S(2)}) collective-permute-start(bf16[256,128]{1,0:T(8,128)(2,1)S(1)} %get-tuple-element.134.refs_0_), channel_id=1, source_target_pairs={{0,6},{1,7},{2,4},{3,5},{4,2},{5,3},{6,0},{7,1},{8,14},{9,15},{10,... | collective-permute-start | bytes 196616 | tf_op jit(solution)/shard_map/ppermute | solution.py:334
  12.8 0.6 %collective-permute-start.16 = (bf16[256,128]{1,0:T(8,128)(2,1)S(1)}, bf16[256,128]{1,0:T(8,128)(2,1)S(1)}, u32[]{:S(2)}, u32[]{:S(2)}) collective-permute-start(bf16[256,128]{1,0:T(8,128)(2,1)S(1)} %get-tuple-element.134.refs_0_), channel_id=1, source_target_pairs={{0,2},{1,3},{2,0},{3,1},{4,6},{5,7},{6,4},{7,5},{8,10},{9,11},{10,... | collective-permute-start | bytes 196616 | tf_op jit(solution)/shard_map/ppermute | solution.py:334
  13.5 2.1 %collective-permute-done.18.refs_3_ = bf16[256,128]{1,0:T(8,128)(2,1)S(1)} collective-permute-done((bf16[256,128]{1,0:T(8,128)(2,1)S(1)}, bf16[256,128]{1,0:T(8,128)(2,1)S(1)}, u32[]{:S(2)}, u32[]{:S(2)}) %collective-permute-start.18) | collective-permute-done | bytes 65568 | tf_op jit(solution)/shard_map/ppermute | solution.py:334
  15.5 2.6 %collective-permute-done.17.refs_2_ = bf16[256,128]{1,0:T(8,128)(2,1)S(1)} collective-permute-done((bf16[256,128]{1,0:T(8,128)(2,1)S(1)}, bf16[256,128]{1,0:T(8,128)(2,1)S(1)}, u32[]{:S(2)}, u32[]{:S(2)}) %collective-permute-start.17) | collective-permute-done | bytes 65568 | tf_op jit(solution)/shard_map/ppermute | solution.py:334
  18.2 0.5 %collective-permute-start.20 = (bf16[256,128]{1,0:T(8,128)(2,1)S(1)}, bf16[256,128]{1,0:T(8,128)(2,1)S(1)}, u32[]{:S(2)}, u32[]{:S(2)}) collective-permute-start(bf16[256,128]{1,0:T(8,128)(2,1)S(1)} %collective-permute-done.16.refs_1_), channel_id=1, source_target_pairs={{0,1},{1,0},{2,3},{3,2},{4,5},{5,4},{6,7},{7,6},{8,9},{9,8},{10,11... | collective-permute-start | bytes 196616 | tf_op jit(solution)/shard_map/ppermute | solution.py:334
  18.7 1.6 %shard_map.115 = (bf16[2,2048,256]{2,1,0:T(8,128)(2,1)S(1)}, f32[128,256]{1,0:T(8,128)S(1)}, bf16[256,1024]{1,0:T(8,128)(2,1)S(1)}, bf16[256,1024]{1,0:T(8,128)(...) custom-call(bf16[1024,128]{1,0:T(8,128)(2,1)} %refs_0_.1, ...), custom_call_target="tpu_custom_call" | custom-call | flops 268435456 | bytes 1048576 | tf_op jit(solution)/shard_map/pallas_call | solution.py:374
  20.4 1.4 %shard_map.116 = (bf16[256,128]{1,0:T(8,128)(2,1)S(1)}, bf16[256,128]{1,0:T(8,128)(2,1)S(1)}, bf16[256,128]{1,0:T(8,128)(2,1)S(1)}, bf16[256,128]{1,0:T(8,128)(2,1)S(1)}) custom-call(s32[8]{0:T(128)S(4)} %get-tuple-element.110.table, bf16[256,128]{1,0:T(8,128)(2,1)S(1)} %get-tuple-element.134.refs_0_, bf16[256,128]{1,0:T(8,128)(2,1)S(1)} %collective-permute-done.16.refs_1_, ...), custom_call_target="tpu_custom_call" | custom-call | flops 2147483648 | bytes 1048576 | tf_op jit(solution)/shard_map/pallas_call | solution.py:442
  21.8 1.6 %collective-permute-start.23 = (bf16[256,128]{1,0:T(8,128)(2,1)S(1)}, bf16[256,128]{1,0:T(8,128)(2,1)S(1)}, u32[]{:S(2)}, u32[]{:S(2)}) collective-permute-start(bf16[256,128]{1,0:T(8,128)(2,1)S(1)} %get-tuple-element.121), channel_id=1, source_target_pairs={{0,8},{8,0},{16,24},{24,16},{1,9},{9,1},{17,25},{25,17},{2,10},{10... | collective-permute-start | bytes 196616 | tf_op jit(solution)/shard_map/ppermute | solution.py:334
  23.4 1.5 %collective-permute-start.24 = (bf16[256,128]{1,0:T(8,128)(2,1)S(1)}, bf16[256,128]{1,0:T(8,128)(2,1)S(1)}, u32[]{:S(2)}, u32[]{:S(2)}) collective-permute-start(bf16[256,128]{1,0:T(8,128)(2,1)S(1)} %get-tuple-element.122), channel_id=1, source_target_pairs={{0,16},{8,24},{16,0},{24,8},{1,17},{9,25},{17,1},{25,9},{2,18},{10... | collective-permute-start | bytes 196616 | tf_op jit(solution)/shard_map/ppermute | solution.py:334
  25.4 0.8 %collective-permute-done.23.refs_1_ = bf16[256,128]{1,0:T(8,128)(2,1)S(1)} collective-permute-done((bf16[256,128]{1,0:T(8,128)(2,1)S(1)}, bf16[256,128]{1,0:T(8,128)(2,1)S(1)}, u32[]{:S(2)}, u32[]{:S(2)}) %collective-permute-start.23) | collective-permute-done | bytes 65568 | tf_op jit(solution)/shard_map/ppermute | solution.py:334
  26.2 1.5 %collective-permute-done.24.refs_2_ = bf16[256,128]{1,0:T(8,128)(2,1)S(1)} collective-permute-done((bf16[256,128]{1,0:T(8,128)(2,1)S(1)}, bf16[256,128]{1,0:T(8,128)(2,1)S(1)}, u32[]{:S(2)}, u32[]{:S(2)}) %collective-permute-start.24) | collective-permute-done | bytes 65568 | tf_op jit(solution)/shard_map/ppermute | solution.py:334
  27.6 2.4 %collective-permute-done.25.refs_3_ = bf16[256,128]{1,0:T(8,128)(2,1)S(1)} collective-permute-done((bf16[256,128]{1,0:T(8,128)(2,1)S(1)}, bf16[256,128]{1,0:T(8,128)(2,1)S(1)}, u32[]{:S(2)}, u32[]{:S(2)}) %collective-permute-start.25) | collective-permute-done | bytes 65568 | tf_op jit(solution)/shard_map/ppermute | solution.py:334
  30.3 2.3 %collective-permute-start.31 = (bf16[8,32,128]{2,1,0:T(8,128)(2,1)S(1)}, bf16[8,32,128]{2,1,0:T(8,128)(2,1)S(1)}, u32[]{:S(2)}, u32[]{:S(2)}) collective-permute-start(bf16[8,32,128]{2,1,0:T(8,128)(2,1)S(1)} %get-tuple-element.125.normed_ref.refs_0_), channel_id=1, source_target_pairs={{0,6},{1,7},{2,4},{3,5},{4,2},{5,3},{6,0},{7,1},{8,14},{9,15},{10,... | collective-permute-start | bytes 196616 | tf_op jit(solution)/shard_map/ppermute | solution.py:334
  32.6 2.2 %collective-permute-start.27 = (bf16[8,32,128]{2,1,0:T(8,128)(2,1)S(1)}, bf16[8,32,128]{2,1,0:T(8,128)(2,1)S(1)}, u32[]{:S(2)}, u32[]{:S(2)}) collective-permute-start(bf16[8,32,128]{2,1,0:T(8,128)(2,1)S(1)} %get-tuple-element.125.normed_ref.refs_0_), channel_id=1, source_target_pairs={{0,2},{1,3},{2,0},{3,1},{4,6},{5,7},{6,4},{7,5},{8,10},{9,11},{10,... | collective-permute-start | bytes 196616 | tf_op jit(solution)/shard_map/ppermute | solution.py:334
  34.8 1.9 %collective-permute-done.31.refs_3_ = bf16[8,32,128]{2,1,0:T(8,128)(2,1)S(1)} collective-permute-done((bf16[8,32,128]{2,1,0:T(8,128)(2,1)S(1)}, bf16[8,32,128]{2,1,0:T(8,128)(2,1)S(1)}, u32[]{:S(2)}, u32[]{:S(2)}) %collective-permute-start.31) | collective-permute-done | bytes 65568 | tf_op jit(solution)/shard_map/ppermute | solution.py:334
  36.7 1.4 %collective-permute-done.29.refs_2_ = bf16[8,32,128]{2,1,0:T(8,128)(2,1)S(1)} collective-permute-done((bf16[8,32,128]{2,1,0:T(8,128)(2,1)S(1)}, bf16[8,32,128]{2,1,0:T(8,128)(2,1)S(1)}, u32[]{:S(2)}, u32[]{:S(2)}) %collective-permute-start.29) | collective-permute-done | bytes 65568 | tf_op jit(solution)/shard_map/ppermute | solution.py:334
  38.6 0.7 %shard_map.118 = (bf16[256,128]{1,0:T(8,128)(2,1)S(1)}, f32[256,128]{1,0:T(8,128)S(1)}, bf16[8,32,128]{2,1,0:T(8,128)(2,1)}) custom-call(bf16[8,32,128]{2,1,0:T(8,128)(2,1)S(1)} %get-tuple-element.125.normed_ref.refs_0_, bf16[128,512]{1,0:T(8,128)(2,1)S(1)} %get-tuple-element.126.w_ref.refs_4_.refs_7_, bf16[8,32,128]{2,1,0:T(8,128)(2,1)S(1)} %get-tuple-element.127.pair_ref), custom_call_target="tpu_custom_call" | custom-call | flops 134217728 | bytes 1048576 | tf_op jit(solution)/shard_map/pallas_call | solution.py:467
  39.6 1.7 %shard_map.120 = (bf16[8,32,128]{2,1,0:T(8,128)(2,1)}, bf16[8,256,256]{2,1,0:T(8,128)(2,1)S(1)}) custom-call(bf16[8,32,128]{2,1,0:T(8,128)(2,1)S(1)} %collective-permute-done.26.refs_0_, bf16[8,32,128]{2,1,0:T(8,128)(2,1)S(1)} %collective-permute-done.28.refs_1_, ...), custom_call_target="tpu_custom_call", output_to_operand_aliasing={{1}: (4, {})} | custom-call | flops 536870912 | bytes 1048576 | tf_op jit(solution)/shard_map/pallas_call | solution.py:481
  (24 shorter events, 2.0 us)
Async XLA Ops:
  0.6 2.3 %collective-permute-start.15 = (bf16[256,1024]{1,0:T(8,128)(2,1)}, bf16[256,1024]{1,0:T(8,128)(2,1)S(1)}, u32[]{:S(2)}, u32[]{:S(2)}) collective-permute-start(bf16[256,1024]{1,0:T(8,128)(2,1)} %left_ref.1), channel_id=1, source_target_pairs={{0,1},{1,0},{2,3},{3,2},{4,5},{5,4},{6,7},{7,6},{8,9},{9,8},{10,11... | collective-permute-start | bytes 1572872 | tf_op jit(solution)/shard_map/ppermute | solution.py:334
  3.4 5.4 %collective-permute-start = (bf16[256,128]{1,0:T(8,128)(2,1)S(1)}, bf16[256,128]{1,0:T(8,128)(2,1)S(1)}, u32[]{:S(2)}, u32[]{:S(2)}) collective-permute-start(bf16[256,128]{1,0:T(8,128)(2,1)S(1)} %get-tuple-element.54), channel_id=1, source_target_pairs={{0,2},{1,3},{2,0},{3,1},{4,6},{5,7},{6,4},{7,5},{8,10},{9,11},{10,... | collective-permute-start | bytes 196616 | tf_op jit(solution)/shard_map/cond/branch_1_fun/ppermute | solution.py:334
  8.9 6.7 %collective-permute-start.18 = (bf16[256,128]{1,0:T(8,128)(2,1)S(1)}, bf16[256,128]{1,0:T(8,128)(2,1)S(1)}, u32[]{:S(2)}, u32[]{:S(2)}) collective-permute-start(bf16[256,128]{1,0:T(8,128)(2,1)S(1)} %get-tuple-element.134.refs_0_), channel_id=1, source_target_pairs={{0,6},{1,7},{2,4},{3,5},{4,2},{5,3},{6,0},{7,1},{8,14},{9,15},{10,... | collective-permute-start | bytes 196616 | tf_op jit(solution)/shard_map/ppermute | solution.py:334
  12.8 5.4 %collective-permute-start.17 = (bf16[256,128]{1,0:T(8,128)(2,1)S(1)}, bf16[256,128]{1,0:T(8,128)(2,1)S(1)}, u32[]{:S(2)}, u32[]{:S(2)}) collective-permute-start(bf16[256,128]{1,0:T(8,128)(2,1)S(1)} %get-tuple-element.134.refs_0_), channel_id=1, source_target_pairs={{0,4},{1,5},{2,6},{3,7},{4,0},{5,1},{6,2},{7,3},{8,12},{9,13},{10,... | collective-permute-start | bytes 196616 | tf_op jit(solution)/shard_map/ppermute | solution.py:334
  12.8 5.4 %collective-permute-start.16 = (bf16[256,128]{1,0:T(8,128)(2,1)S(1)}, bf16[256,128]{1,0:T(8,128)(2,1)S(1)}, u32[]{:S(2)}, u32[]{:S(2)}) collective-permute-start(bf16[256,128]{1,0:T(8,128)(2,1)S(1)} %get-tuple-element.134.refs_0_), channel_id=1, source_target_pairs={{0,2},{1,3},{2,0},{3,1},{4,6},{5,7},{6,4},{7,5},{8,10},{9,11},{10,... | collective-permute-start | bytes 196616 | tf_op jit(solution)/shard_map/ppermute | solution.py:334
  13.5 6.9 %collective-permute-start.19 = (bf16[256,128]{1,0:T(8,128)(2,1)S(1)}, bf16[256,128]{1,0:T(8,128)(2,1)S(1)}, u32[]{:S(2)}, u32[]{:S(2)}) collective-permute-start(bf16[256,128]{1,0:T(8,128)(2,1)S(1)} %get-tuple-element.134.refs_0_), channel_id=1, source_target_pairs={{0,1},{1,0},{2,3},{3,2},{4,5},{5,4},{6,7},{7,6},{8,9},{9,8},{10,11... | collective-permute-start | bytes 196616 | tf_op jit(solution)/shard_map/ppermute | solution.py:334
  15.5 4.8 %collective-permute-start.22 = (bf16[256,128]{1,0:T(8,128)(2,1)S(1)}, bf16[256,128]{1,0:T(8,128)(2,1)S(1)}, u32[]{:S(2)}, u32[]{:S(2)}) collective-permute-start(bf16[256,128]{1,0:T(8,128)(2,1)S(1)} %collective-permute-done.18.refs_3_), channel_id=1, source_target_pairs={{0,1},{1,0},{2,3},{3,2},{4,5},{5,4},{6,7},{7,6},{8,9},{9,8},{10,11... | collective-permute-start | bytes 196616 | tf_op jit(solution)/shard_map/ppermute | solution.py:334
  18.2 2.2 %collective-permute-start.21 = (bf16[256,128]{1,0:T(8,128)(2,1)S(1)}, bf16[256,128]{1,0:T(8,128)(2,1)S(1)}, u32[]{:S(2)}, u32[]{:S(2)}) collective-permute-start(bf16[256,128]{1,0:T(8,128)(2,1)S(1)} %collective-permute-done.17.refs_2_), channel_id=1, source_target_pairs={{0,1},{1,0},{2,3},{3,2},{4,5},{5,4},{6,7},{7,6},{8,9},{9,8},{10,11... | collective-permute-start | bytes 196616 | tf_op jit(solution)/shard_map/ppermute | solution.py:334
  18.2 2.2 %collective-permute-start.20 = (bf16[256,128]{1,0:T(8,128)(2,1)S(1)}, bf16[256,128]{1,0:T(8,128)(2,1)S(1)}, u32[]{:S(2)}, u32[]{:S(2)}) collective-permute-start(bf16[256,128]{1,0:T(8,128)(2,1)S(1)} %collective-permute-done.16.refs_1_), channel_id=1, source_target_pairs={{0,1},{1,0},{2,3},{3,2},{4,5},{5,4},{6,7},{7,6},{8,9},{9,8},{10,11... | collective-permute-start | bytes 196616 | tf_op jit(solution)/shard_map/ppermute | solution.py:334
  21.8 4.3 %collective-permute-start.23 = (bf16[256,128]{1,0:T(8,128)(2,1)S(1)}, bf16[256,128]{1,0:T(8,128)(2,1)S(1)}, u32[]{:S(2)}, u32[]{:S(2)}) collective-permute-start(bf16[256,128]{1,0:T(8,128)(2,1)S(1)} %get-tuple-element.121), channel_id=1, source_target_pairs={{0,8},{8,0},{16,24},{24,16},{1,9},{9,1},{17,25},{25,17},{2,10},{10... | collective-permute-start | bytes 196616 | tf_op jit(solution)/shard_map/ppermute | solution.py:334
  23.4 4.3 %collective-permute-start.24 = (bf16[256,128]{1,0:T(8,128)(2,1)S(1)}, bf16[256,128]{1,0:T(8,128)(2,1)S(1)}, u32[]{:S(2)}, u32[]{:S(2)}) collective-permute-start(bf16[256,128]{1,0:T(8,128)(2,1)S(1)} %get-tuple-element.122), channel_id=1, source_target_pairs={{0,16},{8,24},{16,0},{24,8},{1,17},{9,25},{17,1},{25,9},{2,18},{10... | collective-permute-start | bytes 196616 | tf_op jit(solution)/shard_map/ppermute | solution.py:334
  24.9 5.2 %collective-permute-start.25 = (bf16[256,128]{1,0:T(8,128)(2,1)S(1)}, bf16[256,128]{1,0:T(8,128)(2,1)S(1)}, u32[]{:S(2)}, u32[]{:S(2)}) collective-permute-start(bf16[256,128]{1,0:T(8,128)(2,1)S(1)} %get-tuple-element.123), channel_id=1, source_target_pairs={{0,24},{8,16},{16,8},{24,0},{1,25},{9,17},{17,9},{25,1},{2,26},{10... | collective-permute-start | bytes 196616 | tf_op jit(solution)/shard_map/ppermute | solution.py:334
  30.3 6.4 %collective-permute-start.31 = (bf16[8,32,128]{2,1,0:T(8,128)(2,1)S(1)}, bf16[8,32,128]{2,1,0:T(8,128)(2,1)S(1)}, u32[]{:S(2)}, u32[]{:S(2)}) collective-permute-start(bf16[8,32,128]{2,1,0:T(8,128)(2,1)S(1)} %get-tuple-element.125.normed_ref.refs_0_), channel_id=1, source_target_pairs={{0,6},{1,7},{2,4},{3,5},{4,2},{5,3},{6,0},{7,1},{8,14},{9,15},{10,... | collective-permute-start | bytes 196616 | tf_op jit(solution)/shard_map/ppermute | solution.py:334
  32.6 5.5 %collective-permute-start.29 = (bf16[8,32,128]{2,1,0:T(8,128)(2,1)S(1)}, bf16[8,32,128]{2,1,0:T(8,128)(2,1)S(1)}, u32[]{:S(2)}, u32[]{:S(2)}) collective-permute-start(bf16[8,32,128]{2,1,0:T(8,128)(2,1)S(1)} %get-tuple-element.125.normed_ref.refs_0_), channel_id=1, source_target_pairs={{0,4},{1,5},{2,6},{3,7},{4,0},{5,1},{6,2},{7,3},{8,12},{9,13},{10,... | collective-permute-start | bytes 196616 | tf_op jit(solution)/shard_map/ppermute | solution.py:334
  32.6 5.5 %collective-permute-start.27 = (bf16[8,32,128]{2,1,0:T(8,128)(2,1)S(1)}, bf16[8,32,128]{2,1,0:T(8,128)(2,1)S(1)}, u32[]{:S(2)}, u32[]{:S(2)}) collective-permute-start(bf16[8,32,128]{2,1,0:T(8,128)(2,1)S(1)} %get-tuple-element.125.normed_ref.refs_0_), channel_id=1, source_target_pairs={{0,2},{1,3},{2,0},{3,1},{4,6},{5,7},{6,4},{7,5},{8,10},{9,11},{10,... | collective-permute-start | bytes 196616 | tf_op jit(solution)/shard_map/ppermute | solution.py:334
  34.8 4.8 %collective-permute-start.26 = (bf16[8,32,128]{2,1,0:T(8,128)(2,1)S(1)}, bf16[8,32,128]{2,1,0:T(8,128)(2,1)S(1)}, u32[]{:S(2)}, u32[]{:S(2)}) collective-permute-start(bf16[8,32,128]{2,1,0:T(8,128)(2,1)S(1)} %get-tuple-element.125.normed_ref.refs_0_), channel_id=1, source_target_pairs={{0,1},{1,0},{2,3},{3,2},{4,5},{5,4},{6,7},{7,6},{8,9},{9,8},{10,11... | collective-permute-start | bytes 196616 | tf_op jit(solution)/shard_map/ppermute | solution.py:334
  36.7 2.9 %collective-permute-start.32 = (bf16[8,32,128]{2,1,0:T(8,128)(2,1)S(1)}, bf16[8,32,128]{2,1,0:T(8,128)(2,1)S(1)}, u32[]{:S(2)}, u32[]{:S(2)}) collective-permute-start(bf16[8,32,128]{2,1,0:T(8,128)(2,1)S(1)} %collective-permute-done.31.refs_3_), channel_id=1, source_target_pairs={{0,1},{1,0},{2,3},{3,2},{4,5},{5,4},{6,7},{7,6},{8,9},{9,8},{10,11... | collective-permute-start | bytes 196616 | tf_op jit(solution)/shard_map/ppermute | solution.py:334
  38.1 1.5 %collective-permute-start.30 = (bf16[8,32,128]{2,1,0:T(8,128)(2,1)S(1)}, bf16[8,32,128]{2,1,0:T(8,128)(2,1)S(1)}, u32[]{:S(2)}, u32[]{:S(2)}) collective-permute-start(bf16[8,32,128]{2,1,0:T(8,128)(2,1)S(1)} %collective-permute-done.29.refs_2_), channel_id=1, source_target_pairs={{0,1},{1,0},{2,3},{3,2},{4,5},{5,4},{6,7},{7,6},{8,9},{9,8},{10,11... | collective-permute-start | bytes 196616 | tf_op jit(solution)/shard_map/ppermute | solution.py:334
  38.1 1.5 %collective-permute-start.28 = (bf16[8,32,128]{2,1,0:T(8,128)(2,1)S(1)}, bf16[8,32,128]{2,1,0:T(8,128)(2,1)S(1)}, u32[]{:S(2)}, u32[]{:S(2)}) collective-permute-start(bf16[8,32,128]{2,1,0:T(8,128)(2,1)S(1)} %collective-permute-done.27.refs_1_), channel_id=1, source_target_pairs={{0,1},{1,0},{2,3},{3,2},{4,5},{5,4},{6,7},{7,6},{8,9},{9,8},{10,11... | collective-permute-start | bytes 196616 | tf_op jit(solution)/shard_map/ppermute | solution.py:334

commit v9 on v8

--- a/solution.py
+++ b/solution.py
@@ -269,14 +269,16 @@
 
 
 def near_kernel(chips, *refs):
-    near, w_ref, kv_ref = refs[:chips], refs[chips], refs[chips + 1]
-    fill(near, w_ref, kv_ref, lax.axis_index("res") % 2)
-
-
-def fill(pieces, w_ref, kv_ref, core):
+    near, partner, w_ref, kv_ref = refs[:chips], *refs[chips:]
+    core = lax.axis_index("res") % 2
+    fill(near, w_ref, kv_ref, core, 0)
+    fill([partner], w_ref, kv_ref, 1 - core, 0)
+
+
+def fill(pieces, w_ref, kv_ref, core, first):
     tokens = pieces[0].shape[1]
     z = lax.axis_index("res") // 2
-    for k, piece in enumerate(pieces):
+    for k, piece in enumerate(pieces, first):
         at = (jnp.bitwise_xor(z, k) * 2 + core) * tokens
         kv = jnp.dot(
             piece[...].reshape(R_DEV * tokens, CZ),
@@ -289,11 +291,11 @@
 
 
 def attend_kernel(chips, *refs):
-    far = refs[:chips]
-    _, q_ref, gate_ref, w_ref, wo_ref, bias_ref, out_ref, kv_ref = refs[chips:-2]
+    far = refs[: chips - 1]
+    _, q_ref, gate_ref, w_ref, wo_ref, bias_ref, out_ref, kv_ref = refs[chips - 1 : -2]
     scores_ref, gated_ref = refs[-2:]
     tokens = far[0].shape[1]
-    fill(far, w_ref, kv_ref, 1 - lax.axis_index("res") % 2)
+    fill(far, w_ref, kv_ref, 1 - lax.axis_index("res") % 2, 1)
     scale = DH ** (-0.5)
     lane_head = lax.broadcasted_iota(jnp.int32, (tokens, CZ), 1) // DH
     for u in range(R_DEV):
@@ -476,20 +478,20 @@
     )(normed, qkvg, pair)
     kv = pltpu.VMEM((R_DEV, keys, 2 * CZ), BF)
     (half_kv,) = call(
-        functools.partial(near_kernel, chips), [kv], [VMEM] * (chips + 1), flops=1 << 28
-    )(*near, qkvg)
+        functools.partial(near_kernel, chips), [kv], [VMEM] * (chips + 2), flops=1 << 28
+    )(*near, far[0], qkvg)
     update, _ = call(
         functools.partial(attend_kernel, chips),
         [jax.ShapeDtypeStruct((R_DEV, tokens, CZ), BF), kv],
-        [VMEM] * (chips + 6),
+        [VMEM] * (chips + 5),
         [
             pltpu.VMEM((R_DEV, H * tokens, keys), F32),
             pltpu.VMEM((R_DEV * tokens, CZ), BF),
         ],
         flops=1 << 29,
         limit=24,
-        aliases={chips: 1},
-    )(*far, half_kv, queries, gate, qkvg, wo, bias)
+        aliases={chips - 1: 1},
+    )(*far[1:], half_kv, queries, gate, qkvg, wo, bias)
     return (pair_strip, update)
 
 

time: 41.4 us -> 41.4 us (level)
  no operation moved by 1% of the time
where the time goes in v9:
time: 41.4 us; the launch traced here: 41.3 us
  starting transfers between devices  17.2 us (42%)
  waiting for transfers between devices  15.8 us (38%)
  Pallas kernels  7.4 us (18%)
  between operations  0.76 us (2%)
    ppermute x19, starting transfers between devices, swap(): return lax.ppermute(x, axis, [(i, i ^ mask) for i in range(n)])  17.2 us
    ppermute x19, waiting for transfers between devices, swap(): return lax.ppermute(x, axis, [(i, i ^ mask) for i in range(n)])  15.8 us
    pallas_call x1, Pallas kernels, body(): call(prep_kernel, [pltpu.VMEM((2, PROJ_CHANNELS * LANES // 2, PACK * CZ /...  1.63 us
    pallas_call x1, Pallas kernels, body(): call(functools.partial(attend_kernel, chips), [jax.ShapeDtypeStruct((R_DE...  1.61 us
    pallas_call x1, Pallas kernels, body(): call(functools.partial(outer_kernel, chips), [pltpu.VMEM((R_DEV * tokens,...  1.43 us
    pallas_call x1, Pallas kernels, body(): call(functools.partial(front_kernel, adaptive, 2 * tokens), [pltpu.VMEM((...  1.08 us
  transfers between devices with their start and end apart: 19, of which 9 were waited for; matrix products, arithmetic and copies ran while one was open for 0% of the time, Pallas kernels for 9%

profile of v9, /device:TPU:0, one launch (start us, length us, event | category | flops | bytes accessed | tf_op | source)
XLA Modules:
  0.0 41.3 jit_solution(10629705709238335569)
XLA Ops:
  0.6 0.6 %collective-permute-start.15 = (bf16[256,1024]{1,0:T(8,128)(2,1)}, bf16[256,1024]{1,0:T(8,128)(2,1)S(1)}, u32[]{:S(2)}, u32[]{:S(2)}) collective-permute-start(bf16[256,1024]{1,0:T(8,128)(2,1)} %left_ref.1), channel_id=1, source_target_pairs={{0,1},{1,0},{2,3},{3,2},{4,5},{5,4},{6,7},{7,6},{8,9},{9,8},{10,11... | collective-permute-start | bytes 1572872 | tf_op jit(solution)/shard_map/ppermute | solution.py:336
  1.2 1.1 %shard_map.113 = (bf16[128,1024]{1,0:T(8,128)(2,1)S(1)}, s32[8]{0:T(128)S(4)}, s32[1]{0:T(128)S(4)}) custom-call(bf16[256,1024]{1,0:T(8,128)(2,1)} %left_ref.1, s32[4]{0:T(128)} %starts_ref.1), custom_call_target="tpu_custom_call" | custom-call | bytes 1048576 | tf_op jit(solution)/shard_map/pallas_call | solution.py:364
  2.3 0.7 %collective-permute-done.15.recv_ref = bf16[256,1024]{1,0:T(8,128)(2,1)S(1)} collective-permute-done((bf16[256,1024]{1,0:T(8,128)(2,1)}, bf16[256,1024]{1,0:T(8,128)(2,1)S(1)}, u32[]{:S(2)}, u32[]{:S(2)}) %collective-permute-start.15) | collective-permute-done | bytes 524320 | tf_op jit(solution)/shard_map/ppermute | solution.py:336
  3.4 5.5 %conditional.1 = (bf16[256,128]{1,0:T(8,128)(2,1)S(1)}) conditional(s32[]{:T(128)} %bitcast, bf16[256,128]{1,0:T(8,128)(2,1)S(1)} %get-tuple-element.113, (bf16[256,128]{1,0:T(8,128)(2,1)S(1)}, bf16[256,128]{1,0:T(8,128)(2,1)S(1)}) %tuple.38, (bf16[256,128]{1,0:T(8,128)(2,1)S(1)}, ...), branch_computations={%region_0.0_spmd, %region_1.0_spmd, %region_2.0_spmd, %region_3.0_... | conditional | flops 98304 | bytes 1114240 | solution.py:438
  3.4 3.0 %collective-permute-start = (bf16[256,128]{1,0:T(8,128)(2,1)S(1)}, bf16[256,128]{1,0:T(8,128)(2,1)S(1)}, u32[]{:S(2)}, u32[]{:S(2)}) collective-permute-start(bf16[256,128]{1,0:T(8,128)(2,1)S(1)} %get-tuple-element.54), channel_id=1, source_target_pairs={{0,2},{1,3},{2,0},{3,1},{4,6},{5,7},{6,4},{7,5},{8,10},{9,11},{10,... | collective-permute-start | bytes 196616 | tf_op jit(solution)/shard_map/cond/branch_1_fun/ppermute | solution.py:336
  6.4 2.4 %collective-permute-done = bf16[256,128]{1,0:T(8,128)(2,1)S(1)} collective-permute-done((bf16[256,128]{1,0:T(8,128)(2,1)S(1)}, bf16[256,128]{1,0:T(8,128)(2,1)S(1)}, u32[]{:S(2)}, u32[]{:S(2)}) %collective-permute-start) | collective-permute-done | bytes 65568 | tf_op jit(solution)/shard_map/cond/branch_1_fun/ppermute | solution.py:336
  8.9 3.9 %collective-permute-start.18 = (bf16[256,128]{1,0:T(8,128)(2,1)S(1)}, bf16[256,128]{1,0:T(8,128)(2,1)S(1)}, u32[]{:S(2)}, u32[]{:S(2)}) collective-permute-start(bf16[256,128]{1,0:T(8,128)(2,1)S(1)} %get-tuple-element.134.refs_0_), channel_id=1, source_target_pairs={{0,6},{1,7},{2,4},{3,5},{4,2},{5,3},{6,0},{7,1},{8,14},{9,15},{10,... | collective-permute-start | bytes 196616 | tf_op jit(solution)/shard_map/ppermute | solution.py:336
  12.8 0.6 %collective-permute-start.16 = (bf16[256,128]{1,0:T(8,128)(2,1)S(1)}, bf16[256,128]{1,0:T(8,128)(2,1)S(1)}, u32[]{:S(2)}, u32[]{:S(2)}) collective-permute-start(bf16[256,128]{1,0:T(8,128)(2,1)S(1)} %get-tuple-element.134.refs_0_), channel_id=1, source_target_pairs={{0,2},{1,3},{2,0},{3,1},{4,6},{5,7},{6,4},{7,5},{8,10},{9,11},{10,... | collective-permute-start | bytes 196616 | tf_op jit(solution)/shard_map/ppermute | solution.py:336
  13.5 2.1 %collective-permute-done.18.refs_3_ = bf16[256,128]{1,0:T(8,128)(2,1)S(1)} collective-permute-done((bf16[256,128]{1,0:T(8,128)(2,1)S(1)}, bf16[256,128]{1,0:T(8,128)(2,1)S(1)}, u32[]{:S(2)}, u32[]{:S(2)}) %collective-permute-start.18) | collective-permute-done | bytes 65568 | tf_op jit(solution)/shard_map/ppermute | solution.py:336
  15.5 2.6 %collective-permute-done.17.refs_2_ = bf16[256,128]{1,0:T(8,128)(2,1)S(1)} collective-permute-done((bf16[256,128]{1,0:T(8,128)(2,1)S(1)}, bf16[256,128]{1,0:T(8,128)(2,1)S(1)}, u32[]{:S(2)}, u32[]{:S(2)}) %collective-permute-start.17) | collective-permute-done | bytes 65568 | tf_op jit(solution)/shard_map/ppermute | solution.py:336
  18.2 0.5 %collective-permute-start.20 = (bf16[256,128]{1,0:T(8,128)(2,1)S(1)}, bf16[256,128]{1,0:T(8,128)(2,1)S(1)}, u32[]{:S(2)}, u32[]{:S(2)}) collective-permute-start(bf16[256,128]{1,0:T(8,128)(2,1)S(1)} %collective-permute-done.16.refs_1_), channel_id=1, source_target_pairs={{0,1},{1,0},{2,3},{3,2},{4,5},{5,4},{6,7},{7,6},{8,9},{9,8},{10,11... | collective-permute-start | bytes 196616 | tf_op jit(solution)/shard_map/ppermute | solution.py:336
  18.7 1.6 %shard_map.115 = (bf16[2,2048,256]{2,1,0:T(8,128)(2,1)S(1)}, f32[128,256]{1,0:T(8,128)S(1)}, bf16[256,1024]{1,0:T(8,128)(2,1)S(1)}, bf16[256,1024]{1,0:T(8,128)(...) custom-call(bf16[1024,128]{1,0:T(8,128)(2,1)} %refs_0_.1, ...), custom_call_target="tpu_custom_call" | custom-call | flops 268435456 | bytes 1048576 | tf_op jit(solution)/shard_map/pallas_call | solution.py:376
  20.4 1.4 %shard_map.116 = (bf16[256,128]{1,0:T(8,128)(2,1)S(1)}, bf16[256,128]{1,0:T(8,128)(2,1)S(1)}, bf16[256,128]{1,0:T(8,128)(2,1)S(1)}, bf16[256,128]{1,0:T(8,128)(2,1)S(1)}) custom-call(s32[8]{0:T(128)S(4)} %get-tuple-element.110.table, bf16[256,128]{1,0:T(8,128)(2,1)S(1)} %get-tuple-element.134.refs_0_, bf16[256,128]{1,0:T(8,128)(2,1)S(1)} %collective-permute-done.16.refs_1_, ...), custom_call_target="tpu_custom_call" | custom-call | flops 2147483648 | bytes 1048576 | tf_op jit(solution)/shard_map/pallas_call | solution.py:444
  21.8 1.6 %collective-permute-start.23 = (bf16[256,128]{1,0:T(8,128)(2,1)S(1)}, bf16[256,128]{1,0:T(8,128)(2,1)S(1)}, u32[]{:S(2)}, u32[]{:S(2)}) collective-permute-start(bf16[256,128]{1,0:T(8,128)(2,1)S(1)} %get-tuple-element.121), channel_id=1, source_target_pairs={{0,8},{8,0},{16,24},{24,16},{1,9},{9,1},{17,25},{25,17},{2,10},{10... | collective-permute-start | bytes 196616 | tf_op jit(solution)/shard_map/ppermute | solution.py:336
  23.4 1.5 %collective-permute-start.24 = (bf16[256,128]{1,0:T(8,128)(2,1)S(1)}, bf16[256,128]{1,0:T(8,128)(2,1)S(1)}, u32[]{:S(2)}, u32[]{:S(2)}) collective-permute-start(bf16[256,128]{1,0:T(8,128)(2,1)S(1)} %get-tuple-element.122), channel_id=1, source_target_pairs={{0,16},{8,24},{16,0},{24,8},{1,17},{9,25},{17,1},{25,9},{2,18},{10... | collective-permute-start | bytes 196616 | tf_op jit(solution)/shard_map/ppermute | solution.py:336
  25.4 0.8 %collective-permute-done.23.refs_1_ = bf16[256,128]{1,0:T(8,128)(2,1)S(1)} collective-permute-done((bf16[256,128]{1,0:T(8,128)(2,1)S(1)}, bf16[256,128]{1,0:T(8,128)(2,1)S(1)}, u32[]{:S(2)}, u32[]{:S(2)}) %collective-permute-start.23) | collective-permute-done | bytes 65568 | tf_op jit(solution)/shard_map/ppermute | solution.py:336
  26.2 1.5 %collective-permute-done.24.refs_2_ = bf16[256,128]{1,0:T(8,128)(2,1)S(1)} collective-permute-done((bf16[256,128]{1,0:T(8,128)(2,1)S(1)}, bf16[256,128]{1,0:T(8,128)(2,1)S(1)}, u32[]{:S(2)}, u32[]{:S(2)}) %collective-permute-start.24) | collective-permute-done | bytes 65568 | tf_op jit(solution)/shard_map/ppermute | solution.py:336
  27.6 2.4 %collective-permute-done.25.refs_3_ = bf16[256,128]{1,0:T(8,128)(2,1)S(1)} collective-permute-done((bf16[256,128]{1,0:T(8,128)(2,1)S(1)}, bf16[256,128]{1,0:T(8,128)(2,1)S(1)}, u32[]{:S(2)}, u32[]{:S(2)}) %collective-permute-start.25) | collective-permute-done | bytes 65568 | tf_op jit(solution)/shard_map/ppermute | solution.py:336
  30.3 2.3 %collective-permute-start.30 = (bf16[8,32,128]{2,1,0:T(8,128)(2,1)S(1)}, bf16[8,32,128]{2,1,0:T(8,128)(2,1)S(1)}, u32[]{:S(2)}, u32[]{:S(2)}) collective-permute-start(bf16[8,32,128]{2,1,0:T(8,128)(2,1)S(1)} %get-tuple-element.125.normed_ref.refs_0_), channel_id=1, source_target_pairs={{0,6},{1,7},{2,4},{3,5},{4,2},{5,3},{6,0},{7,1},{8,14},{9,15},{10,... | collective-permute-start | bytes 196616 | tf_op jit(solution)/shard_map/ppermute | solution.py:336
  32.6 2.2 %collective-permute-start.26 = (bf16[8,32,128]{2,1,0:T(8,128)(2,1)S(1)}, bf16[8,32,128]{2,1,0:T(8,128)(2,1)S(1)}, u32[]{:S(2)}, u32[]{:S(2)}) collective-permute-start(bf16[8,32,128]{2,1,0:T(8,128)(2,1)S(1)} %get-tuple-element.125.normed_ref.refs_0_), channel_id=1, source_target_pairs={{0,2},{1,3},{2,0},{3,1},{4,6},{5,7},{6,4},{7,5},{8,10},{9,11},{10,... | collective-permute-start | bytes 196616 | tf_op jit(solution)/shard_map/ppermute | solution.py:336
  34.8 1.9 %collective-permute-done.30.refs_3_ = bf16[8,32,128]{2,1,0:T(8,128)(2,1)S(1)} collective-permute-done((bf16[8,32,128]{2,1,0:T(8,128)(2,1)S(1)}, bf16[8,32,128]{2,1,0:T(8,128)(2,1)S(1)}, u32[]{:S(2)}, u32[]{:S(2)}) %collective-permute-start.30) | collective-permute-done | bytes 65568 | tf_op jit(solution)/shard_map/ppermute | solution.py:336
  36.7 1.4 %collective-permute-done.28.refs_2_ = bf16[8,32,128]{2,1,0:T(8,128)(2,1)S(1)} collective-permute-done((bf16[8,32,128]{2,1,0:T(8,128)(2,1)S(1)}, bf16[8,32,128]{2,1,0:T(8,128)(2,1)S(1)}, u32[]{:S(2)}, u32[]{:S(2)}) %collective-permute-start.28) | collective-permute-done | bytes 65568 | tf_op jit(solution)/shard_map/ppermute | solution.py:336
  38.6 0.7 %shard_map.118 = (bf16[256,128]{1,0:T(8,128)(2,1)S(1)}, f32[256,128]{1,0:T(8,128)S(1)}, bf16[8,32,128]{2,1,0:T(8,128)(2,1)}) custom-call(bf16[8,32,128]{2,1,0:T(8,128)(2,1)S(1)} %get-tuple-element.125.normed_ref.refs_0_, bf16[128,512]{1,0:T(8,128)(2,1)S(1)} %get-tuple-element.126.w_ref.refs_5_.refs_6_, bf16[8,32,128]{2,1,0:T(8,128)(2,1)S(1)} %get-tuple-element.127.pair_ref), custom_call_target="tpu_custom_call" | custom-call | flops 134217728 | bytes 1048576 | tf_op jit(solution)/shard_map/pallas_call | solution.py:469
  39.7 1.6 %shard_map.120 = (bf16[8,32,128]{2,1,0:T(8,128)(2,1)}, bf16[8,256,256]{2,1,0:T(8,128)(2,1)S(1)}) custom-call(bf16[8,32,128]{2,1,0:T(8,128)(2,1)S(1)} %collective-permute-done.27.refs_0_, bf16[8,32,128]{2,1,0:T(8,128)(2,1)S(1)} %collective-permute-done.29.refs_1_, ...), custom_call_target="tpu_custom_call", output_to_operand_aliasing={{1}: (3, {})} | custom-call | flops 536870912 | bytes 1048576 | tf_op jit(solution)/shard_map/pallas_call | solution.py:483
  (24 shorter events, 2.1 us)
Async XLA Ops:
  0.6 2.3 %collective-permute-start.15 = (bf16[256,1024]{1,0:T(8,128)(2,1)}, bf16[256,1024]{1,0:T(8,128)(2,1)S(1)}, u32[]{:S(2)}, u32[]{:S(2)}) collective-permute-start(bf16[256,1024]{1,0:T(8,128)(2,1)} %left_ref.1), channel_id=1, source_target_pairs={{0,1},{1,0},{2,3},{3,2},{4,5},{5,4},{6,7},{7,6},{8,9},{9,8},{10,11... | collective-permute-start | bytes 1572872 | tf_op jit(solution)/shard_map/ppermute | solution.py:336
  3.4 5.4 %collective-permute-start = (bf16[256,128]{1,0:T(8,128)(2,1)S(1)}, bf16[256,128]{1,0:T(8,128)(2,1)S(1)}, u32[]{:S(2)}, u32[]{:S(2)}) collective-permute-start(bf16[256,128]{1,0:T(8,128)(2,1)S(1)} %get-tuple-element.54), channel_id=1, source_target_pairs={{0,2},{1,3},{2,0},{3,1},{4,6},{5,7},{6,4},{7,5},{8,10},{9,11},{10,... | collective-permute-start | bytes 196616 | tf_op jit(solution)/shard_map/cond/branch_1_fun/ppermute | solution.py:336
  8.9 6.7 %collective-permute-start.18 = (bf16[256,128]{1,0:T(8,128)(2,1)S(1)}, bf16[256,128]{1,0:T(8,128)(2,1)S(1)}, u32[]{:S(2)}, u32[]{:S(2)}) collective-permute-start(bf16[256,128]{1,0:T(8,128)(2,1)S(1)} %get-tuple-element.134.refs_0_), channel_id=1, source_target_pairs={{0,6},{1,7},{2,4},{3,5},{4,2},{5,3},{6,0},{7,1},{8,14},{9,15},{10,... | collective-permute-start | bytes 196616 | tf_op jit(solution)/shard_map/ppermute | solution.py:336
  12.8 5.4 %collective-permute-start.17 = (bf16[256,128]{1,0:T(8,128)(2,1)S(1)}, bf16[256,128]{1,0:T(8,128)(2,1)S(1)}, u32[]{:S(2)}, u32[]{:S(2)}) collective-permute-start(bf16[256,128]{1,0:T(8,128)(2,1)S(1)} %get-tuple-element.134.refs_0_), channel_id=1, source_target_pairs={{0,4},{1,5},{2,6},{3,7},{4,0},{5,1},{6,2},{7,3},{8,12},{9,13},{10,... | collective-permute-start | bytes 196616 | tf_op jit(solution)/shard_map/ppermute | solution.py:336
  12.8 5.4 %collective-permute-start.16 = (bf16[256,128]{1,0:T(8,128)(2,1)S(1)}, bf16[256,128]{1,0:T(8,128)(2,1)S(1)}, u32[]{:S(2)}, u32[]{:S(2)}) collective-permute-start(bf16[256,128]{1,0:T(8,128)(2,1)S(1)} %get-tuple-element.134.refs_0_), channel_id=1, source_target_pairs={{0,2},{1,3},{2,0},{3,1},{4,6},{5,7},{6,4},{7,5},{8,10},{9,11},{10,... | collective-permute-start | bytes 196616 | tf_op jit(solution)/shard_map/ppermute | solution.py:336
  13.5 6.9 %collective-permute-start.19 = (bf16[256,128]{1,0:T(8,128)(2,1)S(1)}, bf16[256,128]{1,0:T(8,128)(2,1)S(1)}, u32[]{:S(2)}, u32[]{:S(2)}) collective-permute-start(bf16[256,128]{1,0:T(8,128)(2,1)S(1)} %get-tuple-element.134.refs_0_), channel_id=1, source_target_pairs={{0,1},{1,0},{2,3},{3,2},{4,5},{5,4},{6,7},{7,6},{8,9},{9,8},{10,11... | collective-permute-start | bytes 196616 | tf_op jit(solution)/shard_map/ppermute | solution.py:336
  15.5 4.8 %collective-permute-start.22 = (bf16[256,128]{1,0:T(8,128)(2,1)S(1)}, bf16[256,128]{1,0:T(8,128)(2,1)S(1)}, u32[]{:S(2)}, u32[]{:S(2)}) collective-permute-start(bf16[256,128]{1,0:T(8,128)(2,1)S(1)} %collective-permute-done.18.refs_3_), channel_id=1, source_target_pairs={{0,1},{1,0},{2,3},{3,2},{4,5},{5,4},{6,7},{7,6},{8,9},{9,8},{10,11... | collective-permute-start | bytes 196616 | tf_op jit(solution)/shard_map/ppermute | solution.py:336
  18.2 2.2 %collective-permute-start.21 = (bf16[256,128]{1,0:T(8,128)(2,1)S(1)}, bf16[256,128]{1,0:T(8,128)(2,1)S(1)}, u32[]{:S(2)}, u32[]{:S(2)}) collective-permute-start(bf16[256,128]{1,0:T(8,128)(2,1)S(1)} %collective-permute-done.17.refs_2_), channel_id=1, source_target_pairs={{0,1},{1,0},{2,3},{3,2},{4,5},{5,4},{6,7},{7,6},{8,9},{9,8},{10,11... | collective-permute-start | bytes 196616 | tf_op jit(solution)/shard_map/ppermute | solution.py:336
  18.2 2.2 %collective-permute-start.20 = (bf16[256,128]{1,0:T(8,128)(2,1)S(1)}, bf16[256,128]{1,0:T(8,128)(2,1)S(1)}, u32[]{:S(2)}, u32[]{:S(2)}) collective-permute-start(bf16[256,128]{1,0:T(8,128)(2,1)S(1)} %collective-permute-done.16.refs_1_), channel_id=1, source_target_pairs={{0,1},{1,0},{2,3},{3,2},{4,5},{5,4},{6,7},{7,6},{8,9},{9,8},{10,11... | collective-permute-start | bytes 196616 | tf_op jit(solution)/shard_map/ppermute | solution.py:336
  21.8 4.3 %collective-permute-start.23 = (bf16[256,128]{1,0:T(8,128)(2,1)S(1)}, bf16[256,128]{1,0:T(8,128)(2,1)S(1)}, u32[]{:S(2)}, u32[]{:S(2)}) collective-permute-start(bf16[256,128]{1,0:T(8,128)(2,1)S(1)} %get-tuple-element.121), channel_id=1, source_target_pairs={{0,8},{8,0},{16,24},{24,16},{1,9},{9,1},{17,25},{25,17},{2,10},{10... | collective-permute-start | bytes 196616 | tf_op jit(solution)/shard_map/ppermute | solution.py:336
  23.4 4.3 %collective-permute-start.24 = (bf16[256,128]{1,0:T(8,128)(2,1)S(1)}, bf16[256,128]{1,0:T(8,128)(2,1)S(1)}, u32[]{:S(2)}, u32[]{:S(2)}) collective-permute-start(bf16[256,128]{1,0:T(8,128)(2,1)S(1)} %get-tuple-element.122), channel_id=1, source_target_pairs={{0,16},{8,24},{16,0},{24,8},{1,17},{9,25},{17,1},{25,9},{2,18},{10... | collective-permute-start | bytes 196616 | tf_op jit(solution)/shard_map/ppermute | solution.py:336
  24.9 5.2 %collective-permute-start.25 = (bf16[256,128]{1,0:T(8,128)(2,1)S(1)}, bf16[256,128]{1,0:T(8,128)(2,1)S(1)}, u32[]{:S(2)}, u32[]{:S(2)}) collective-permute-start(bf16[256,128]{1,0:T(8,128)(2,1)S(1)} %get-tuple-element.123), channel_id=1, source_target_pairs={{0,24},{8,16},{16,8},{24,0},{1,25},{9,17},{17,9},{25,1},{2,26},{10... | collective-permute-start | bytes 196616 | tf_op jit(solution)/shard_map/ppermute | solution.py:336
  30.3 6.4 %collective-permute-start.30 = (bf16[8,32,128]{2,1,0:T(8,128)(2,1)S(1)}, bf16[8,32,128]{2,1,0:T(8,128)(2,1)S(1)}, u32[]{:S(2)}, u32[]{:S(2)}) collective-permute-start(bf16[8,32,128]{2,1,0:T(8,128)(2,1)S(1)} %get-tuple-element.125.normed_ref.refs_0_), channel_id=1, source_target_pairs={{0,6},{1,7},{2,4},{3,5},{4,2},{5,3},{6,0},{7,1},{8,14},{9,15},{10,... | collective-permute-start | bytes 196616 | tf_op jit(solution)/shard_map/ppermute | solution.py:336
  32.6 5.5 %collective-permute-start.28 = (bf16[8,32,128]{2,1,0:T(8,128)(2,1)S(1)}, bf16[8,32,128]{2,1,0:T(8,128)(2,1)S(1)}, u32[]{:S(2)}, u32[]{:S(2)}) collective-permute-start(bf16[8,32,128]{2,1,0:T(8,128)(2,1)S(1)} %get-tuple-element.125.normed_ref.refs_0_), channel_id=1, source_target_pairs={{0,4},{1,5},{2,6},{3,7},{4,0},{5,1},{6,2},{7,3},{8,12},{9,13},{10,... | collective-permute-start | bytes 196616 | tf_op jit(solution)/shard_map/ppermute | solution.py:336
  32.6 5.5 %collective-permute-start.26 = (bf16[8,32,128]{2,1,0:T(8,128)(2,1)S(1)}, bf16[8,32,128]{2,1,0:T(8,128)(2,1)S(1)}, u32[]{:S(2)}, u32[]{:S(2)}) collective-permute-start(bf16[8,32,128]{2,1,0:T(8,128)(2,1)S(1)} %get-tuple-element.125.normed_ref.refs_0_), channel_id=1, source_target_pairs={{0,2},{1,3},{2,0},{3,1},{4,6},{5,7},{6,4},{7,5},{8,10},{9,11},{10,... | collective-permute-start | bytes 196616 | tf_op jit(solution)/shard_map/ppermute | solution.py:336
  34.8 4.5 %collective-permute-start.32 = (bf16[8,32,128]{2,1,0:T(8,128)(2,1)S(1)}, bf16[8,32,128]{2,1,0:T(8,128)(2,1)S(1)}, u32[]{:S(2)}, u32[]{:S(2)}) collective-permute-start(bf16[8,32,128]{2,1,0:T(8,128)(2,1)S(1)} %get-tuple-element.125.normed_ref.refs_0_), channel_id=1, source_target_pairs={{0,1},{1,0},{2,3},{3,2},{4,5},{5,4},{6,7},{7,6},{8,9},{9,8},{10,11... | collective-permute-start | bytes 196616 | tf_op jit(solution)/shard_map/ppermute | solution.py:336
  36.7 2.9 %collective-permute-start.31 = (bf16[8,32,128]{2,1,0:T(8,128)(2,1)S(1)}, bf16[8,32,128]{2,1,0:T(8,128)(2,1)S(1)}, u32[]{:S(2)}, u32[]{:S(2)}) collective-permute-start(bf16[8,32,128]{2,1,0:T(8,128)(2,1)S(1)} %collective-permute-done.30.refs_3_), channel_id=1, source_target_pairs={{0,1},{1,0},{2,3},{3,2},{4,5},{5,4},{6,7},{7,6},{8,9},{9,8},{10,11... | collective-permute-start | bytes 196616 | tf_op jit(solution)/shard_map/ppermute | solution.py:336
  38.1 1.5 %collective-permute-start.29 = (bf16[8,32,128]{2,1,0:T(8,128)(2,1)S(1)}, bf16[8,32,128]{2,1,0:T(8,128)(2,1)S(1)}, u32[]{:S(2)}, u32[]{:S(2)}) collective-permute-start(bf16[8,32,128]{2,1,0:T(8,128)(2,1)S(1)} %collective-permute-done.28.refs_2_), channel_id=1, source_target_pairs={{0,1},{1,0},{2,3},{3,2},{4,5},{5,4},{6,7},{7,6},{8,9},{9,8},{10,11... | collective-permute-start | bytes 196616 | tf_op jit(solution)/shard_map/ppermute | solution.py:336
  38.1 1.5 %collective-permute-start.27 = (bf16[8,32,128]{2,1,0:T(8,128)(2,1)S(1)}, bf16[8,32,128]{2,1,0:T(8,128)(2,1)S(1)}, u32[]{:S(2)}, u32[]{:S(2)}) collective-permute-start(bf16[8,32,128]{2,1,0:T(8,128)(2,1)S(1)} %collective-permute-done.26.refs_1_), channel_id=1, source_target_pairs={{0,1},{1,0},{2,3},{3,2},{4,5},{5,4},{6,7},{7,6},{8,9},{9,8},{10,11... | collective-permute-start | bytes 196616 | tf_op jit(solution)/shard_map/ppermute | solution.py:336
